TPU v7x, 32 devices: a whole 2x2x4 slice. The times are simulated.
32 devices in a mesh: pairs: 2 (over x), blk: 16 (over z, y, core).
Axes of the slice: x: 2, y: 2, z: 4, core: 2. Of those that a mesh axis runs over, the one named last changes fastest.
Arguments:
- src_emb: bfloat16 [32768, 1024], P(('pairs', 'blk')), parts along dimension 0, may hold values from -4 to 4
- src_scale: float32 [32768], P(('pairs', 'blk')), parts along dimension 0, may hold values from 0.3 to 3
- src_count: int32 [32], P(('pairs', 'blk')), parts along dimension 0, may hold values from 512 to 1024, as said below
- tgt_emb: bfloat16 [512, 1024], P(('pairs', 'blk')), parts along dimension 0, may hold values from -4 to 4
- tgt_scale: float32 [512], P(('pairs', 'blk')), parts along dimension 0, may hold values from 0.3 to 3
- tgt_count: int32 [32], P(('pairs', 'blk')), parts along dimension 0, may hold values from 8 to 16, as said below
Outputs:
- best_source: float32 [32768], P(('pairs', 'blk')), parts along dimension 0
- best_target: float32 [512], P(('pairs', 'blk')), parts along dimension 0
There are 2 independent parts, one for each index of `pairs`. A program takes and returns all parts, laid end to end along the dimension named above; each array names one. Nothing has to cross between parts.
Inputs may be any that keep to these rules, and one draw needn't show every extreme that they name: `src_count`: counts the live rows of each block of 1024 source rows, which are its first rows; at least one block is full. `tgt_count`: counts the live rows of each block of 16 target rows, which are its first rows; at least one block is full.
All inputs are finite; a program needn't handle non-finite values.
Results may differ from a plain program's by a relative error of at most 0.0003.
Values may be sent and summed in bfloat16 or wider, within the bound.
No kernel may reach another device: no remote copies, remote signals or barrier semaphores. Data moves between devices by JAX's collectives and lax.ppermute only.
A program may use at most 64 MiB of HBM per device.

v0:
```python
import jax
import jax.numpy as jnp
from jax import lax
from jax.sharding import PartitionSpec as P

NEG_BIG = -1e30


def body(src_emb, src_scale, src_count, tgt_emb, tgt_scale, tgt_count):
    ranks = lax.axis_size("blk")
    tgt_dev = tgt_emb.shape[0]
    src_dev = src_emb.shape[0]
    src_live = jnp.arange(src_dev, dtype=jnp.int32) < src_count[0]
    own_live = (jnp.arange(tgt_dev, dtype=jnp.int32) < tgt_count[0]).astype(jnp.float32)
    all_scales, all_live = (
        lax.all_gather(tgt_scale, "blk", axis=0, tiled=True),
        lax.all_gather(own_live, "blk", axis=0, tiled=True),
    )

    def score_tile(rows_in):
        product = lax.dot_general(
            rows_in, src_emb, (((1,), (1,)), ((), ())), preferred_element_type=jnp.float32
        )
        alive = all_live > 0.5
        return (product * all_scales[:, None] * src_scale[None, :], alive[:, None])

    row_max = jnp.full((src_dev,), NEG_BIG, jnp.float32)
    scores, alive = score_tile(lax.all_gather(tgt_emb, "blk", axis=0, tiled=True))
    highest = jnp.maximum(row_max, jnp.max(jnp.where(alive, scores, NEG_BIG), axis=0))
    fresh = jnp.sum(jnp.where(alive, jnp.exp(scores - highest[None, :]), 0.0), axis=0)
    row_sum = fresh
    part_max = jnp.max(jnp.where(src_live[None, :], scores, NEG_BIG), axis=1)
    part_sum = jnp.sum(
        jnp.where(src_live[None, :], jnp.exp(scores - part_max[:, None]), 0.0), axis=1
    )
    col_max = part_max
    col_sum = part_sum
    first = (highest, row_sum, col_max, col_sum)
    row_max, row_sum, col_max, col_sum = first
    row_den = row_max + jnp.log(row_sum)
    parts_max, parts_sum = (
        lax.all_to_all(
            col_max.reshape(ranks, tgt_dev), "blk", split_axis=0, concat_axis=0, tiled=True
        ),
        lax.all_to_all(
            col_sum.reshape(ranks, tgt_dev), "blk", split_axis=0, concat_axis=0, tiled=True
        ),
    )
    highest = jnp.max(parts_max, axis=0)
    total = jnp.sum(parts_sum * jnp.exp(parts_max - highest[None, :]), axis=0)
    own_alive = own_live > 0.5
    own_den = jnp.where(own_alive, highest + jnp.log(jnp.where(own_alive, total, 1.0)), 0.0)
    col_den = lax.all_gather(own_den, "blk", axis=0, tiled=True)
    row_best = jnp.full((src_dev,), NEG_BIG, jnp.float32)
    scores, alive = score_tile(lax.all_gather(tgt_emb, "blk", axis=0, tiled=True))
    margin = scores - 0.5 * (row_den[None, :] + col_den[:, None])
    row_best = jnp.maximum(row_best, jnp.max(jnp.where(alive, margin, NEG_BIG), axis=0))
    part_best = jnp.max(jnp.where(src_live[None, :], margin, NEG_BIG), axis=1)
    col_best = part_best
    row_best, col_best = (row_best, col_best)
    best_source = jnp.where(src_live, row_best, 0.0)
    parts_best = lax.all_to_all(
        col_best.reshape(ranks, tgt_dev), "blk", split_axis=0, concat_axis=0, tiled=True
    )
    own_best = jnp.max(parts_best, axis=0)
    best_target = jnp.where(own_live > 0.5, own_best, 0.0)
    return (best_source, best_target)


def solution(mesh):
    return jax.shard_map(
        body,
        mesh=mesh,
        in_specs=(
            P(("pairs", "blk"), None),
            P(("pairs", "blk")),
            P(("pairs", "blk")),
            P(("pairs", "blk"), None),
            P(("pairs", "blk")),
            P(("pairs", "blk")),
        ),
        out_specs=(P(("pairs", "blk")), P(("pairs", "blk"))),
        check_vma=False,
    )
```

profile of v0, /device:TPU:0, one launch (start us, length us, event | category | flops | bytes accessed | tf_op | source)
XLA Modules:
  0.0 122.3 jit_solution(3399174599737110030)
XLA Ops:
  0.6 0.0 copy-start
  1.4 1.2 %dynamic-slice = u32[1]{0:T(128)} dynamic-slice(u32[32]{0:T(128)} %constant.19, u32[]{:T(128)S(6)} %add.28), dynamic_slice_sizes={1} | dynamic-slice | bytes 12
  3.3 0.1 fusion.1
  3.5 0.8 dynamic-update-slice.1
  4.3 34.9 %all-reduce.3 = (f32[256]{0:T(256)S(1)}, f32[256]{0:T(256)S(1)}) all-reduce(f32[256]{0:T(256)S(1)} %dynamic-update-slice.1, f32[256]{0:T(256)S(1)} %fusion.1), channel_id=1, replica_groups=mesh['pairs'=2,'blk'=16] {'blk'}, use_global_device_ids=true, to_apply=%add.1 | all-reduce | flops 512 | bytes 4096
  39.9 18.9 %all_gather.14 = bf16[256,1024]{1,0:T(8,128)(2,1)S(1)} all-gather(bf16[16,1024]{1,0:T(8,128)(2,1)} %param.9), channel_id=1, replica_groups=mesh['pairs'=2,'blk'=16] {'blk'}, dimensions={0}, use_global_device_ids=true | all-gather | bytes 557056 | tf_op jit(solution)/shard_map/all_gather | solution.py:55
  58.8 0.0 copy-done
  58.8 1.6 %select_reduce_fusion.5 = (f32[1024]{0:T(1024)S(1)}, f32[256]{0:T(256)S(1)}, f32[256,1024]{1,0:T(8,128)S(1)}) fusion(pred[256]{0:T(512)(128)(4,1)S(1)} %broadcast_compare_fusion, pred[1024]{0:T(1024)(128)(4,1)S(1)} %iota_compare_fusion, f32[1024]{0:T(1024)} %param.7, f32[256]{0:T(256)S(1)} %get-tuple-element.8, bf16[256,1024]{1,0:T(8,128)(2,1)S(1)} %all_gather.14, ...), kind=kOutput, calls=%fused_computation.8 | convolution fusion | flops 538442496 | bytes 3681536 | tf_op jit(solution)/shard_map/dot_general | solution.py:21
  60.5 0.7 all_to_all.22
  61.2 3.8 %all-to-all-start = ((f32[16,1,16]{2,1,0:T(1,128)}), f32[16,1,16]{2,1,0:T(1,128)S(1)}, u32[]{:S(2)}, u32[]{:S(2)}) async-start(f32[16,1,16]{2,1,0:T(1,128)} %all_to_all.22), calls=%async_computation | async-start | bytes 16384 | tf_op jit(solution)/shard_map/all_to_all | solution.py:42
  64.9 0.5 select_reduce_fusion.4
  65.4 0.7 all_to_all.24
  66.1 5.3 %all-to-all-done = f32[16,1,16]{2,1,0:T(1,128)S(1)} async-done(((f32[16,1,16]{2,1,0:T(1,128)}), f32[16,1,16]{2,1,0:T(1,128)S(1)}, u32[]{:S(2)}, u32[]{:S(2)}) %all-to-all-start) | async-done | bytes 1056 | tf_op jit(solution)/shard_map/all_to_all | solution.py:42
  71.4 3.4 %all-to-all-start.1 = ((f32[16,1,16]{2,1,0:T(1,128)}), f32[16,1,16]{2,1,0:T(1,128)S(1)}, u32[]{:S(2)}, u32[]{:S(2)}) async-start(f32[16,1,16]{2,1,0:T(1,128)} %all_to_all.24), calls=%async_computation.1 | async-start | bytes 16384 | tf_op jit(solution)/shard_map/all_to_all | solution.py:45
  74.8 6.3 %all-to-all-done.1 = f32[16,1,16]{2,1,0:T(1,128)S(1)} async-done(((f32[16,1,16]{2,1,0:T(1,128)}), f32[16,1,16]{2,1,0:T(1,128)S(1)}, u32[]{:S(2)}, u32[]{:S(2)}) %all-to-all-start.1) | async-done | bytes 1056 | tf_op jit(solution)/shard_map/all_to_all | solution.py:45
  81.2 0.1 select_dynamic-update-slice_fusion
  81.3 29.5 %all-reduce.2 = f32[256]{0:T(256)S(1)} all-reduce(f32[256]{0:T(256)S(1)} %select_dynamic-update-slice_fusion), channel_id=1, replica_groups=mesh['pairs'=2,'blk'=16] {'blk'}, use_global_device_ids=true, to_apply=%add.2 | all-reduce | flops 256 | bytes 2048
  110.8 0.4 select_reduce_fusion
  111.2 0.7 all_to_all.28
  111.9 3.5 %all-to-all-start.2 = ((f32[16,1,16]{2,1,0:T(1,128)}), f32[16,1,16]{2,1,0:T(1,128)S(1)}, u32[]{:S(2)}, u32[]{:S(2)}) async-start(f32[16,1,16]{2,1,0:T(1,128)} %all_to_all.28), calls=%async_computation.2 | async-start | bytes 16384 | tf_op jit(solution)/shard_map/all_to_all | solution.py:62
  115.4 0.6 maximum_select_fusion
  116.0 5.8 %all-to-all-done.2 = f32[16,1,16]{2,1,0:T(1,128)S(1)} async-done(((f32[16,1,16]{2,1,0:T(1,128)}), f32[16,1,16]{2,1,0:T(1,128)S(1)}, u32[]{:S(2)}, u32[]{:S(2)}) %all-to-all-start.2) | async-done | bytes 1056 | tf_op jit(solution)/shard_map/all_to_all | solution.py:62
  121.8 0.5 compare_select_fusion
  (10 shorter events, 0.1 us)
Async XLA Ops:
  0.6 58.2 %copy-start = (bf16[1024,1024]{1,0:T(8,128)(2,1)S(1)}, bf16[1024,1024]{1,0:T(8,128)(2,1)}, u32[]{:S(2)}) copy-start(bf16[1024,1024]{1,0:T(8,128)(2,1)} %param.6) | copy-start | bytes 6291460
  61.2 10.2 %all-to-all-start = ((f32[16,1,16]{2,1,0:T(1,128)}), f32[16,1,16]{2,1,0:T(1,128)S(1)}, u32[]{:S(2)}, u32[]{:S(2)}) async-start(f32[16,1,16]{2,1,0:T(1,128)} %all_to_all.22), calls=%async_computation | async-start | bytes 16384 | tf_op jit(solution)/shard_map/all_to_all | solution.py:42
  71.4 9.8 %all-to-all-start.1 = ((f32[16,1,16]{2,1,0:T(1,128)}), f32[16,1,16]{2,1,0:T(1,128)S(1)}, u32[]{:S(2)}, u32[]{:S(2)}) async-start(f32[16,1,16]{2,1,0:T(1,128)} %all_to_all.24), calls=%async_computation.1 | async-start | bytes 16384 | tf_op jit(solution)/shard_map/all_to_all | solution.py:45
  111.9 9.9 %all-to-all-start.2 = ((f32[16,1,16]{2,1,0:T(1,128)}), f32[16,1,16]{2,1,0:T(1,128)S(1)}, u32[]{:S(2)}, u32[]{:S(2)}) async-start(f32[16,1,16]{2,1,0:T(1,128)} %all_to_all.28), calls=%async_computation.2 | async-start | bytes 16384 | tf_op jit(solution)/shard_map/all_to_all | solution.py:62
where the time goes:
time: 123 us; the launch traced here: 122 us
  blocking collectives  83.4 us (68%)
  waiting for transfers between devices  17.4 us (14%)
  starting transfers between devices  10.7 us (9%)
  local copies, waits for them, and re-layouts  4.15 us (3%)
  between operations  2.82 us (2%)
  other arithmetic  2.32 us (2%)
  matrix products  1.63 us (1%)
    unnamed x2, blocking collectives  64.4 us
    all_gather x1, blocking collectives, body(): lax.all_gather(tgt_emb, 'blk', axis=0, tiled=True)  18.9 us
    all_to_all x1, waiting for transfers between devices, body(): lax.all_to_all(col_sum.reshape(ranks, tgt_dev), 'blk', split_axis=0, conc...  6.34 us
    all_to_all x1, waiting for transfers between devices, body(): lax.all_to_all(col_best.reshape(ranks, tgt_dev), 'blk', split_axis=0, con...  5.8 us
    all_to_all x1, waiting for transfers between devices, body(): lax.all_to_all(col_max.reshape(ranks, tgt_dev), 'blk', split_axis=0, conc...  5.28 us
    all_to_all x1, starting transfers between devices, body(): lax.all_to_all(col_max.reshape(ranks, tgt_dev), 'blk', split_axis=0, conc...  3.75 us
    all_to_all x1, starting transfers between devices, body(): lax.all_to_all(col_best.reshape(ranks, tgt_dev), 'blk', split_axis=0, con...  3.49 us
    all_to_all x1, starting transfers between devices, body(): lax.all_to_all(col_sum.reshape(ranks, tgt_dev), 'blk', split_axis=0, conc...  3.41 us
  transfers between devices with their start and end apart: 3, of which 3 were waited for; matrix products, arithmetic and copies ran while one was open for 1% of the time, Pallas kernels for 0%

commit v1 on v0

v1 whole, which is shorter than its diff:
```python
import functools

import jax
import jax.numpy as jnp
from jax import lax
from jax.experimental import pallas as pl
from jax.experimental.pallas import tpu as pltpu
from jax.sharding import PartitionSpec as P

NEG_BIG = -1e30
LANES = 128
VMEM = pl.BlockSpec(memory_space=pltpu.VMEM)
SMEM = pl.BlockSpec(memory_space=pltpu.SMEM)


def exchange_masks(ranks):
    bits = ranks.bit_length() - 1
    return [(1 << k) | 1 for k in range(bits - 1, 0, -1)] + [1]


def slot_of(masks, offset):
    bits = len(masks)
    slot = 0
    parity = offset & 1
    for step in range(bits - 1):
        bit = (offset >> (bits - 1 - step)) & 1
        parity = parity ^ bit
        slot = slot + bit * (1 << step)
    return slot + parity * (1 << (bits - 1))


def packed_targets(tgt_emb, tgt_scale, tgt_count):
    rows = tgt_emb.shape[0]
    live = jnp.arange(rows, dtype=jnp.int32) < tgt_count[0]
    scale = jnp.where(live, tgt_scale, 0.0)
    high = lax.reduce_precision(scale, 8, 7)
    middle = lax.reduce_precision(scale - high, 8, 7)
    low = (scale - high) - middle
    lane = jnp.arange(LANES, dtype=jnp.int32)[None, :]
    terms = jnp.where(
        lane == 0, high[:, None], jnp.where(lane == 1, middle[:, None], jnp.where(lane == 2, low[:, None], 0.0))
    )
    return jnp.concatenate([tgt_emb, terms.astype(jnp.bfloat16)], axis=1)


def diagonal():
    shape = (LANES, LANES)
    return lax.broadcasted_iota(jnp.int32, shape, 0) == lax.broadcasted_iota(jnp.int32, shape, 1)


def column_to_row(column, eye):
    return jnp.sum(jnp.where(eye, column, 0.0), axis=0, keepdims=True)


def row_to_column(row, eye):
    return jnp.sum(jnp.where(eye, row, 0.0), axis=1, keepdims=True)


def score_kernel(
    masks, tgt_dev, count_ref, near_ref, far_ref, src_ref, src_scale_ref,
    scores_ref, row_den_ref, stats_ref, tgt_sc,
):
    ranks = 1 << len(masks)
    me = lax.axis_index("blk")
    total, width = tgt_sc.shape
    depth = src_ref.shape[1]
    sources = src_ref.shape[0]
    half = near_ref.shape[0]
    for owner in range(ranks):
        slot = slot_of(masks, me ^ owner)
        rows = pl.ds(owner * tgt_dev, tgt_dev)
        inner = slot & (ranks // 2 - 1)
        at = pl.ds(pl.multiple_of(inner * tgt_dev, tgt_dev), tgt_dev)

        @pl.when(slot < ranks // 2)
        def _():
            tgt_sc[rows, :] = near_ref[at, :]

        @pl.when(slot >= ranks // 2)
        def _():
            tgt_sc[rows, :] = far_ref[at, :]

    src_live = lax.broadcasted_iota(jnp.int32, (1, sources), 1) < count_ref[0]
    src_scale = src_scale_ref[...]
    eye = diagonal()
    blocks = total // LANES
    row_max = jnp.full((1, sources), NEG_BIG, jnp.float32)
    for block in range(blocks):
        rows = pl.ds(block * LANES, LANES)
        product = lax.dot_general(
            tgt_sc[rows, :depth], src_ref[...], (((1,), (1,)), ((), ())), preferred_element_type=jnp.float32
        )
        scale = jnp.sum(tgt_sc[rows, depth:].astype(jnp.float32), axis=1, keepdims=True)
        scores = jnp.where(scale > 0.0, product * scale * src_scale, NEG_BIG)
        scores_ref[rows, :] = scores
        row_max = jnp.maximum(row_max, jnp.max(scores, axis=0, keepdims=True))
        masked = jnp.where(src_live, scores, NEG_BIG)
        highest = jnp.max(masked, axis=1, keepdims=True)
        part = jnp.sum(jnp.exp(masked - highest), axis=1, keepdims=True)
        stats_ref[0, pl.ds(block, 1), :] = column_to_row(highest + jnp.log(part), eye)
    row_sum = jnp.zeros((1, sources), jnp.float32)
    for block in range(blocks):
        rows = pl.ds(block * LANES, LANES)
        row_sum = row_sum + jnp.sum(jnp.exp(scores_ref[rows, :] - row_max), axis=0, keepdims=True)
    row_den = row_max + jnp.log(row_sum)
    row_den_ref[...] = row_den
    half_den = 0.5 * row_den
    for block in range(blocks):
        rows = pl.ds(block * LANES, LANES)
        partial = jnp.where(src_live, scores_ref[rows, :] - half_den, NEG_BIG)
        stats_ref[0, pl.ds(blocks + block, 1), :] = column_to_row(jnp.max(partial, axis=1, keepdims=True), eye)
    pad = stats_ref.shape[1] - 2 * blocks
    if pad:
        stats_ref[0, pl.ds(2 * blocks, pad), :] = jnp.zeros((pad, LANES), jnp.float32)
    for peer in range(1, ranks):
        stats_ref[peer] = stats_ref[0]


def finish_kernel(
    tgt_dev, count_ref, tgt_count_ref, stats_ref, scores_ref, row_den_ref, best_source_ref, best_target_ref
):
    me = lax.axis_index("blk")
    total, sources = scores_ref.shape
    blocks = total // LANES
    eye = diagonal()
    logs = stats_ref[:, :blocks, :]
    highest = jnp.max(logs, axis=0)
    col_den = highest + jnp.log(jnp.sum(jnp.exp(logs - highest[None]), axis=0))
    best = jnp.max(stats_ref[:, blocks : 2 * blocks, :], axis=0) - 0.5 * col_den
    row_best = jnp.full((1, sources), NEG_BIG, jnp.float32)
    for block in range(blocks):
        half_den = row_to_column(0.5 * col_den[block : block + 1, :], eye)
        rows = pl.ds(block * LANES, LANES)
        scores = scores_ref[rows, :]
        margin = jnp.where(scores > 0.5 * NEG_BIG, scores - half_den, NEG_BIG)
        row_best = jnp.maximum(row_best, jnp.max(margin, axis=0, keepdims=True))
    src_live = lax.broadcasted_iota(jnp.int32, (1, sources), 1) < count_ref[0]
    best_source_ref[...] = jnp.where(src_live, row_best - 0.5 * row_den_ref[...], 0.0)
    lane = lax.broadcasted_iota(jnp.int32, (tgt_dev, LANES), 1)
    wanted = lax.broadcasted_iota(jnp.int32, (tgt_dev, LANES), 0) + me * tgt_dev
    own = jnp.zeros((tgt_dev, 1), jnp.float32)
    for block in range(blocks):
        hit = lane + block * LANES == wanted
        own = own + jnp.sum(jnp.where(hit, best[block : block + 1, :], 0.0), axis=1, keepdims=True)
    line = (tgt_dev, tgt_dev)
    same = lax.broadcasted_iota(jnp.int32, line, 0) == lax.broadcasted_iota(jnp.int32, line, 1)
    own = jnp.sum(jnp.where(same, own, 0.0), axis=0, keepdims=True)
    own_live = lax.broadcasted_iota(jnp.int32, (1, tgt_dev), 1) < tgt_count_ref[0]
    best_target_ref[...] = jnp.where(own_live, own, 0.0)


def body(src_emb, src_scale, src_count, tgt_emb, tgt_scale, tgt_count):
    ranks = lax.axis_size("blk")
    src_dev, depth = src_emb.shape
    tgt_dev = tgt_emb.shape[0]
    total = ranks * tgt_dev
    masks = exchange_masks(ranks)
    held = packed_targets(tgt_emb, tgt_scale, tgt_count)
    for mask in masks[:-1]:
        came = lax.ppermute(held, "blk", [(i, i ^ mask) for i in range(ranks)])
        held = jnp.concatenate([held, came], axis=0)
    far = lax.ppermute(held, "blk", [(i, i ^ masks[-1]) for i in range(ranks)])
    stat_rows = -(-2 * total // (8 * LANES)) * 8
    scores, row_den, stats = pl.pallas_call(
        functools.partial(score_kernel, masks, tgt_dev),
        out_shape=(
            jax.ShapeDtypeStruct((total, src_dev), jnp.float32),
            jax.ShapeDtypeStruct((1, src_dev), jnp.float32),
            jax.ShapeDtypeStruct((ranks, stat_rows, LANES), jnp.float32),
        ),
        in_specs=[SMEM, VMEM, VMEM, VMEM, VMEM],
        out_specs=(VMEM, VMEM, VMEM),
        scratch_shapes=[pltpu.VMEM((total, depth + LANES), jnp.bfloat16)],
        name="scores",
    )(src_count, held, far, src_emb, src_scale.reshape(1, src_dev))
    stats = lax.all_to_all(stats, "blk", split_axis=0, concat_axis=0, tiled=True)
    best_source, best_target = pl.pallas_call(
        functools.partial(finish_kernel, tgt_dev),
        out_shape=(
            jax.ShapeDtypeStruct((1, src_dev), jnp.float32),
            jax.ShapeDtypeStruct((1, tgt_dev), jnp.float32),
        ),
        in_specs=[SMEM, SMEM, VMEM, VMEM, VMEM],
        out_specs=(VMEM, VMEM),
        name="finish",
    )(src_count, tgt_count, stats, scores, row_den)
    return best_source.reshape(src_dev), best_target.reshape(tgt_dev)


def solution(mesh):
    return jax.shard_map(
        body,
        mesh=mesh,
        in_specs=(
            P(("pairs", "blk"), None),
            P(("pairs", "blk")),
            P(("pairs", "blk")),
            P(("pairs", "blk"), None),
            P(("pairs", "blk")),
            P(("pairs", "blk")),
        ),
        out_specs=(P(("pairs", "blk")), P(("pairs", "blk"))),
        check_vma=False,
    )
```

time: 123 us -> 44.7 us (0.36)
  blocking collectives: 83.4 us -> 14.5 us
  waiting for transfers between devices: 17.4 us -> 8.83 us
  Pallas kernels: 0 us -> 6.68 us
  local copies, waits for them, and re-layouts: 4.15 us -> 0.71 us
  starting transfers between devices: 10.7 us -> 7.6 us
  matrix products: 1.63 us -> 0 us
  other arithmetic: 2.32 us -> 3.84 us
    unnamed x2 -> x0, blocking collectives: 64.4 us -> none
    all_gather x1 -> x0, blocking collectives: 18.9 us -> none  [body(): lax.all_gather(tgt_emb, 'blk', axis=0, tiled=True)]
    all_to_all x3 -> x0, waiting for transfers between devices: 17.4 us -> none  [the longest x1 6.34 us: body(): lax.all_to_all(col_sum.reshape(ranks, tgt_dev), 'blk', split_axis=0, conc...]
    all_to_all x0 -> x1, blocking collectives: none -> 14.5 us  [body(): lax.all_to_all(stats, 'blk', split_axis=0, concat_axis=0, tiled=True)]
    all_to_all x3 -> x0, starting transfers between devices: 10.7 us -> none  [the longest x1 3.75 us: body(): lax.all_to_all(col_max.reshape(ranks, tgt_dev), 'blk', split_axis=0, conc...]
    ppermute x0 -> x4, waiting for transfers between devices: none -> 8.83 us  [the longest x3 8.18 us: body(): came = lax.ppermute(held, 'blk', [(i, i ^ mask) for i in range(ranks)])]
    ppermute x0 -> x4, starting transfers between devices: none -> 7.6 us  [the longest x3 7.25 us: body(): came = lax.ppermute(held, 'blk', [(i, i ^ mask) for i in range(ranks)])]
    pallas_call x0 -> x2, Pallas kernels: none -> 6.68 us  [the longest x1 4.58 us: body(): pl.pallas_call(functools.partial(score_kernel, masks, tgt_dev), out_shape...]
  transfers between devices with their start and end apart: 3 -> 4, of which waited for: 3 -> 4; matrix products, arithmetic and copies ran while one was open for 1% -> 0% of each run, Pallas kernels for 0% -> 0%
where the time goes in v1:
time: 44.7 us; the launch traced here: 44.2 us
  blocking collectives  14.5 us (32%)
  waiting for transfers between devices  8.83 us (20%)
  starting transfers between devices  7.6 us (17%)
  Pallas kernels  6.68 us (15%)
  other arithmetic  3.84 us (9%)
  between operations  1.96 us (4%)
  local copies, waits for them, and re-layouts  0.71 us (2%)
    all_to_all x1, blocking collectives, body(): lax.all_to_all(stats, 'blk', split_axis=0, concat_axis=0, tiled=True)  14.5 us
    ppermute x3, waiting for transfers between devices, body(): came = lax.ppermute(held, 'blk', [(i, i ^ mask) for i in range(ranks)])  8.18 us
    ppermute x3, starting transfers between devices, body(): came = lax.ppermute(held, 'blk', [(i, i ^ mask) for i in range(ranks)])  7.25 us
    pallas_call x1, Pallas kernels, body(): pl.pallas_call(functools.partial(score_kernel, masks, tgt_dev), out_shape...  4.58 us
    concatenate x3, other arithmetic, body(): held = jnp.concatenate([held, came], axis=0)  2.32 us
    pallas_call x1, Pallas kernels, body(): pl.pallas_call(functools.partial(finish_kernel, tgt_dev), out_shape=(jax....  2.1 us
  transfers between devices with their start and end apart: 4, of which 4 were waited for; matrix products, arithmetic and copies ran while one was open for 0% of the time, Pallas kernels for 0%

profile of v1, /device:TPU:0, one launch (start us, length us, event | category | flops | bytes accessed | tf_op | source)
XLA Modules:
  0.0 44.2 jit_solution(407704533010958860)
XLA Ops:
  1.3 0.7 %fusion = (bf16[16]{0:T(256)(128)(2,1)S(1)}, bf16[16]{0:T(256)(128)(2,1)S(1)}, bf16[16]{0:T(256)(128)(2,1)S(1)}) fusion(f32[16]{0:T(128)} %param.10, s32[]{:T(128)} %bitcast.4), kind=kLoop, calls=%fused_computation.11 | loop fusion | flops 144 | bytes 164 | tf_op jit(solution)/shard_map/reduce_precision | solution.py:36
  2.0 0.1 select_convert_fusion
  2.0 0.8 %pad_maximum_fusion.3 = bf16[16,1152]{1,0:T(8,128)(2,1)S(1)} fusion(bf16[16,128]{1,0:T(8,128)(2,1)S(1)} %select_convert_fusion, bf16[16,1024]{1,0:T(8,128)(2,1)} %param.9), kind=kLoop, calls=%fused_computation.3 | loop fusion | flops 73728 | bytes 73728 | tf_op jit(solution)/shard_map/concatenate | solution.py:43
  2.8 3.5 %collective-permute-start = (bf16[16,1152]{1,0:T(8,128)(2,1)S(1)}, bf16[16,1152]{1,0:T(8,128)(2,1)S(1)}, u32[]{:S(2)}, u32[]{:S(2)}) collective-permute-start(bf16[16,1152]{1,0:T(8,128)(2,1)S(1)} %pad_maximum_fusion.3), channel_id=1, source_target_pairs={{0,9},{1,8},{2,11},{3,10},{4,13},{5,12},{6,15},{7,14},{8,1},{9,0},... | collective-permute-start | bytes 110600 | tf_op jit(solution)/shard_map/ppermute | solution.py:160
  6.3 1.9 %collective-permute-done = bf16[16,1152]{1,0:T(8,128)(2,1)S(1)} collective-permute-done((bf16[16,1152]{1,0:T(8,128)(2,1)S(1)}, bf16[16,1152]{1,0:T(8,128)(2,1)S(1)}, u32[]{:S(2)}, u32[]{:S(2)}) %collective-permute-start) | collective-permute-done | bytes 36896 | tf_op jit(solution)/shard_map/ppermute | solution.py:160
  8.2 0.8 %pad_maximum_fusion.2 = bf16[32,1152]{1,0:T(8,128)(2,1)S(1)} fusion(bf16[16,1152]{1,0:T(8,128)(2,1)S(1)} %collective-permute-done, bf16[16,128]{1,0:T(8,128)(2,1)S(1)} %select_convert_fusion, bf16[16,1024]{1,0:T(8,128)(2,1)} %param.9), kind=kLoop, calls=%fused_computation.2 | loop fusion | flops 221184 | bytes 147456 | tf_op jit(solution)/shard_map/concatenate | solution.py:161
  8.9 1.8 %collective-permute-start.1 = (bf16[32,1152]{1,0:T(8,128)(2,1)S(1)}, bf16[32,1152]{1,0:T(8,128)(2,1)S(1)}, u32[]{:S(2)}, u32[]{:S(2)}) collective-permute-start(bf16[32,1152]{1,0:T(8,128)(2,1)S(1)} %pad_maximum_fusion.2), channel_id=1, source_target_pairs={{0,5},{1,4},{2,7},{3,6},{4,1},{5,0},{6,3},{7,2},{8,13},{9,12},{10,... | collective-permute-start | bytes 221192 | tf_op jit(solution)/shard_map/ppermute | solution.py:160
  10.8 2.4 %collective-permute-done.1 = bf16[32,1152]{1,0:T(8,128)(2,1)S(1)} collective-permute-done((bf16[32,1152]{1,0:T(8,128)(2,1)S(1)}, bf16[32,1152]{1,0:T(8,128)(2,1)S(1)}, u32[]{:S(2)}, u32[]{:S(2)}) %collective-permute-start.1) | collective-permute-done | bytes 73760 | tf_op jit(solution)/shard_map/ppermute | solution.py:160
  13.1 0.8 %pad_maximum_fusion.1 = bf16[64,1152]{1,0:T(8,128)(2,1)S(1)} fusion(bf16[32,1152]{1,0:T(8,128)(2,1)S(1)} %collective-permute-done.1, bf16[16,1152]{1,0:T(8,128)(2,1)S(1)} %collective-permute-done, bf16[16,128]{1,0:T(8,128)(2,1)S(1)} %select_convert_fusion, bf16[16,1024]{1,0:T(8,128)(2,1)} %param.9), kind=kLoop, calls=%fused_computation.1 | loop fusion | flops 589824 | bytes 294912 | tf_op jit(solution)/shard_map/concatenate | solution.py:161
  13.9 1.9 %collective-permute-start.2 = (bf16[64,1152]{1,0:T(8,128)(2,1)S(1)}, bf16[64,1152]{1,0:T(8,128)(2,1)S(1)}, u32[]{:S(2)}, u32[]{:S(2)}) collective-permute-start(bf16[64,1152]{1,0:T(8,128)(2,1)S(1)} %pad_maximum_fusion.1), channel_id=1, source_target_pairs={{0,3},{1,2},{2,1},{3,0},{4,7},{5,6},{6,5},{7,4},{8,11},{9,10},{10,... | collective-permute-start | bytes 442376 | tf_op jit(solution)/shard_map/ppermute | solution.py:160
  15.8 3.9 %collective-permute-done.2 = bf16[64,1152]{1,0:T(8,128)(2,1)S(1)} collective-permute-done((bf16[64,1152]{1,0:T(8,128)(2,1)S(1)}, bf16[64,1152]{1,0:T(8,128)(2,1)S(1)}, u32[]{:S(2)}, u32[]{:S(2)}) %collective-permute-start.2) | collective-permute-done | bytes 147488 | tf_op jit(solution)/shard_map/ppermute | solution.py:160
  19.8 0.8 %pad_maximum_fusion.near_ref = bf16[128,1152]{1,0:T(8,128)(2,1)S(1)} fusion(bf16[64,1152]{1,0:T(8,128)(2,1)S(1)} %collective-permute-done.2, bf16[32,1152]{1,0:T(8,128)(2,1)S(1)} %collective-permute-done.1, bf16[16,1152]{1,0:T(8,128)(2,1)S(1)} %collective-permute-done, bf16[16,128]{1,0:T(8,128)(2,1)S(1)} %select_convert_fusion, bf16[16,1024]{1,0:T(8,128)(2,1)} %param.9), kind=kLoop, calls=%fused_computation | loop fusion | flops 1474560 | bytes 589824 | tf_op jit(solution)/shard_map/concatenate | solution.py:161
  20.6 0.0 copy-start
  20.6 0.3 collective-permute-start.3
  21.6 0.6 %collective-permute-done.3.far_ref = bf16[128,1152]{1,0:T(8,128)(2,1)S(1)} collective-permute-done((bf16[128,1152]{1,0:T(8,128)(2,1)S(1)}, bf16[128,1152]{1,0:T(8,128)(2,1)S(1)}, u32[]{:S(2)}, u32[]{:S(2)}) %collective-permute-start.3) | collective-permute-done | bytes 294944 | tf_op jit(solution)/shard_map/ppermute | solution.py:162
  22.2 0.0 copy-start.1
  22.2 0.0 copy-done
  22.2 0.7 %copy-done.1 = bf16[128,1152]{1,0:T(8,128)(2,1)} copy-done((bf16[128,1152]{1,0:T(8,128)(2,1)}, bf16[128,1152]{1,0:T(8,128)(2,1)S(1)}, u32[]{:S(2)}) %copy-start.1) | copy-done | bytes 294936
  22.9 4.6 %scores.1 = (f32[256,1024]{1,0:T(8,128)}, f32[1,1024]{1,0:T(1,128)}, f32[16,8,128]{2,1,0:T(8,128)}) custom-call(s32[1]{0:T(128)S(6)} %copy.8.count_ref, bf16[128,1152]{1,0:T(8,128)(2,1)} %copy-done, bf16[128,1152]{1,0:T(8,128)(2,1)} %copy-done.1, bf16[1024,1024]{1,0:T(8,128)(2,1)} %src_ref.1, f32[1,1024]{1,0:T(1,128)} %bitcast.5), custom_call_target="tpu_custom_call" | custom-call | tf_op jit(solution)/shard_map/scores/pallas_call | solution.py:164
  27.5 14.5 %all_to_all.5.stats_ref = f32[16,8,128]{2,1,0:T(8,128)} all-to-all(f32[16,8,128]{2,1,0:T(8,128)} %get-tuple-element.7), channel_id=1, replica_groups=mesh['pairs'=2,'blk'=16] {'blk'}, dimensions={0} | all-to-all | bytes 131072 | tf_op jit(solution)/shard_map/all_to_all | solution.py:176
  42.1 2.1 %finish.1 = (f32[1,1024]{1,0:T(1,128)}, f32[1,16]{1,0:T(1,128)}) custom-call(s32[1]{0:T(128)S(6)} %copy.8.count_ref, s32[1]{0:T(128)} %copy.9.tgt_count_ref, f32[16,8,128]{2,1,0:T(8,128)} %all_to_all.5.stats_ref, f32[256,1024]{1,0:T(8,128)} %get-tuple-element.8.scores_ref, f32[1,1024]{1,0:T(1,128)} %get-tuple-element.9.row_den_ref), custom_call_target="tpu_custom_call" | custom-call | tf_op jit(solution)/shard_map/finish/pallas_call | solution.py:177
  (2 shorter events, 0.0 us)
Async XLA Ops:
  2.8 5.4 %collective-permute-start = (bf16[16,1152]{1,0:T(8,128)(2,1)S(1)}, bf16[16,1152]{1,0:T(8,128)(2,1)S(1)}, u32[]{:S(2)}, u32[]{:S(2)}) collective-permute-start(bf16[16,1152]{1,0:T(8,128)(2,1)S(1)} %pad_maximum_fusion.3), channel_id=1, source_target_pairs={{0,9},{1,8},{2,11},{3,10},{4,13},{5,12},{6,15},{7,14},{8,1},{9,0},... | collective-permute-start | bytes 110600 | tf_op jit(solution)/shard_map/ppermute | solution.py:160
  8.9 4.2 %collective-permute-start.1 = (bf16[32,1152]{1,0:T(8,128)(2,1)S(1)}, bf16[32,1152]{1,0:T(8,128)(2,1)S(1)}, u32[]{:S(2)}, u32[]{:S(2)}) collective-permute-start(bf16[32,1152]{1,0:T(8,128)(2,1)S(1)} %pad_maximum_fusion.2), channel_id=1, source_target_pairs={{0,5},{1,4},{2,7},{3,6},{4,1},{5,0},{6,3},{7,2},{8,13},{9,12},{10,... | collective-permute-start | bytes 221192 | tf_op jit(solution)/shard_map/ppermute | solution.py:160
  13.9 5.9 %collective-permute-start.2 = (bf16[64,1152]{1,0:T(8,128)(2,1)S(1)}, bf16[64,1152]{1,0:T(8,128)(2,1)S(1)}, u32[]{:S(2)}, u32[]{:S(2)}) collective-permute-start(bf16[64,1152]{1,0:T(8,128)(2,1)S(1)} %pad_maximum_fusion.1), channel_id=1, source_target_pairs={{0,3},{1,2},{2,1},{3,0},{4,7},{5,6},{6,5},{7,4},{8,11},{9,10},{10,... | collective-permute-start | bytes 442376 | tf_op jit(solution)/shard_map/ppermute | solution.py:160
  20.6 1.7 %copy-start = (bf16[128,1152]{1,0:T(8,128)(2,1)}, bf16[128,1152]{1,0:T(8,128)(2,1)S(1)}, u32[]{:S(2)}) copy-start(bf16[128,1152]{1,0:T(8,128)(2,1)S(1)} %pad_maximum_fusion.near_ref) | copy-start | bytes 884740
  20.6 1.6 %collective-permute-start.3 = (bf16[128,1152]{1,0:T(8,128)(2,1)S(1)}, bf16[128,1152]{1,0:T(8,128)(2,1)S(1)}, u32[]{:S(2)}, u32[]{:S(2)}) collective-permute-start(bf16[128,1152]{1,0:T(8,128)(2,1)S(1)} %pad_maximum_fusion.near_ref), channel_id=1, source_target_pairs={{0,1},{1,0},{2,3},{3,2},{4,5},{5,4},{6,7},{7,6},{8,9},{9,8},{10,11... | collective-permute-start | bytes 884744 | tf_op jit(solution)/shard_map/ppermute | solution.py:162
  22.2 0.7 %copy-start.1 = (bf16[128,1152]{1,0:T(8,128)(2,1)}, bf16[128,1152]{1,0:T(8,128)(2,1)S(1)}, u32[]{:S(2)}) copy-start(bf16[128,1152]{1,0:T(8,128)(2,1)S(1)} %collective-permute-done.3.far_ref) | copy-start | bytes 884740

commit v2 on v0

v2 whole, which is shorter than its diff:
```python
import functools

import jax
import jax.numpy as jnp
from jax import lax
from jax.experimental import pallas as pl
from jax.experimental.pallas import tpu as pltpu
from jax.sharding import PartitionSpec as P


NEG_BIG = -1e30
LANES = 128
VMEM = pl.BlockSpec(memory_space=pltpu.VMEM)
SMEM = pl.BlockSpec(memory_space=pltpu.SMEM)
HBM = pl.BlockSpec(memory_space=pltpu.HBM)


def exchange_phases(ranks):
    bits = list(range(ranks.bit_length() - 2, 0, -1))
    phases = []
    if len(bits) % 2:
        phases.append([(1 << bits.pop(0)) | 1])
    for high, low in zip(bits[::2], bits[1::2]):
        phases.append([(1 << high) | (1 << low) | 1, (1 << high) | 1, (1 << low) | 1])
    return phases


def exchange(block, ranks, mask):
    return lax.ppermute(block, "blk", [(i, i ^ mask) for i in range(ranks)])


def on_chip(array):
    return pltpu.with_memory_space_constraint(array, pltpu.VMEM)


def in_hbm(array):
    return pltpu.with_memory_space_constraint(array, pltpu.HBM)


def diagonal(size):
    shape = (size, size)
    return lax.broadcasted_iota(jnp.int32, shape, 0) == lax.broadcasted_iota(jnp.int32, shape, 1)


def column_to_row(column, eye):
    return jnp.sum(jnp.where(eye, column, 0.0), axis=0, keepdims=True)


def row_to_column(row, eye):
    return jnp.sum(jnp.where(eye, row, 0.0), axis=1, keepdims=True)


def pack_kernel(count_ref, tgt_hbm, scale_hbm, packed_ref, live_ref, scale_ref, sems):
    rows, depth = tgt_hbm.shape
    copies = [
        pltpu.make_async_copy(scale_hbm, scale_ref, sems.at[0]),
        pltpu.make_async_copy(tgt_hbm, packed_ref.at[:, pl.ds(0, depth)], sems.at[1]),
    ]
    for copy in copies:
        copy.start()
    copies[0].wait()
    live = lax.broadcasted_iota(jnp.int32, (1, rows), 1) < count_ref[0]
    live_ref[...] = jnp.where(live, 1.0, 0.0)
    scale = row_to_column(jnp.where(live, scale_ref[...], 0.0), diagonal(rows))
    high = scale.astype(jnp.bfloat16).astype(jnp.float32)
    rest = scale - high
    middle = rest.astype(jnp.bfloat16).astype(jnp.float32)
    low = rest - middle
    lane = lax.broadcasted_iota(jnp.int32, (rows, LANES), 1)
    terms = jnp.where(lane == 0, high, jnp.where(lane == 1, middle, jnp.where(lane == 2, low, 0.0)))
    packed_ref[:, depth:] = terms.astype(jnp.bfloat16)
    copies[1].wait()


def load_kernel(src_hbm, scale_hbm, src_ref, scale_ref, sems):
    copies = [
        pltpu.make_async_copy(src_hbm, src_ref, sems.at[0]),
        pltpu.make_async_copy(scale_hbm, scale_ref, sems.at[1]),
    ]
    for copy in copies:
        copy.start()
    for copy in copies:
        copy.wait()


def half_scores(offsets, blocks_ref, tgt_sc, src_ref, src_scale_ref, src_live, scores_ref, tgt_dev):
    me = lax.axis_index("blk")
    depth = src_ref.shape[1]
    half = tgt_sc.shape[0]
    for slot, offset in enumerate(offsets):
        at = pl.multiple_of(((me ^ offset) >> 1) * tgt_dev, tgt_dev)
        tgt_sc[pl.ds(at, tgt_dev), :] = blocks_ref[pl.ds(slot * tgt_dev, tgt_dev), :]
    eye = diagonal(LANES)
    logs = []
    row_max = jnp.full(src_scale_ref.shape, NEG_BIG, jnp.float32)
    for start in range(0, half, LANES):
        rows = pl.ds(start, LANES)
        product = lax.dot_general(
            tgt_sc[rows, :depth], src_ref[...], (((1,), (1,)), ((), ())), preferred_element_type=jnp.float32
        )
        scale = jnp.sum(tgt_sc[rows, depth:].astype(jnp.float32), axis=1, keepdims=True)
        scores = jnp.where(scale > 0.0, product * scale * src_scale_ref[...], NEG_BIG)
        scores_ref[rows, :] = scores
        row_max = jnp.maximum(row_max, jnp.max(scores, axis=0, keepdims=True))
        masked = jnp.where(src_live, scores, NEG_BIG)
        highest = jnp.max(masked, axis=1, keepdims=True)
        part = jnp.sum(jnp.exp(masked - highest), axis=1, keepdims=True)
        logs.append(column_to_row(highest + jnp.log(part), eye))
    return row_max, logs


def exp_sums(scores_ref, row_max):
    row_sum = jnp.zeros_like(row_max)
    for start in range(0, scores_ref.shape[0], LANES):
        row_sum = row_sum + jnp.sum(jnp.exp(scores_ref[pl.ds(start, LANES), :] - row_max), axis=0, keepdims=True)
    return row_sum


def live_lanes(count_ref, size):
    return lax.broadcasted_iota(jnp.int32, (1, size), 1) < count_ref[0]


def near_kernel(
    offsets, tgt_dev, count_ref, near_ref, src_ref, src_scale_ref, scores_ref, row_max_ref, row_sum_ref, logs_ref, tgt_sc
):
    src_live = live_lanes(count_ref, src_ref.shape[0])
    row_max, logs = half_scores(offsets, near_ref, tgt_sc, src_ref, src_scale_ref, src_live, scores_ref, tgt_dev)
    row_max_ref[...] = row_max
    row_sum_ref[...] = exp_sums(scores_ref, row_max)
    for row, values in enumerate(logs):
        logs_ref[pl.ds(row, 1), :] = values


def near_holds_core_0(phases, tgt_dev, row):
    me = lax.axis_index("blk")
    lane = lax.broadcasted_iota(jnp.int32, (1, LANES), 1) + row * LANES
    away = (lane // tgt_dev) ^ (me >> 1)
    core = jnp.full((1, LANES), me & 1, jnp.int32)
    for masks in phases:
        bits = functools.reduce(lambda a, b: a | b, masks) >> 1
        core = core ^ jnp.where((away & bits) != 0, 1, 0)
    return core == 0


def far_kernel(
    phases, offsets, tgt_dev,
    count_ref, far_ref, src_ref, src_scale_ref, near_scores_ref, near_max_ref, near_sum_ref, near_logs_ref,
    scores_ref, row_den_ref, stats_ref, tgt_sc,
):
    src_live = live_lanes(count_ref, src_ref.shape[0])
    offsets = [offset ^ 1 for offset in offsets]
    far_max, logs = half_scores(offsets, far_ref, tgt_sc, src_ref, src_scale_ref, src_live, scores_ref, tgt_dev)
    row_max = jnp.maximum(near_max_ref[...], far_max)
    row_sum = near_sum_ref[...] * jnp.exp(near_max_ref[...] - row_max) + exp_sums(scores_ref, row_max)
    row_den = row_max + jnp.log(row_sum)
    row_den_ref[...] = row_den
    half_den = 0.5 * row_den
    count = len(logs)
    eye = diagonal(LANES)

    def best(ref, row):
        margin = jnp.where(src_live, ref[pl.ds(row * LANES, LANES), :] - half_den, NEG_BIG)
        return column_to_row(jnp.max(margin, axis=1, keepdims=True), eye)

    for row in range(count):
        near_first = near_holds_core_0(phases, tgt_dev, row)
        pairs = ((near_logs_ref[pl.ds(row, 1), :], logs[row]), (best(near_scores_ref, row), best(scores_ref, row)))
        for kind, (near, far) in enumerate(pairs):
            stats_ref[0, pl.ds((2 * kind) * count + row, 1), :] = jnp.where(near_first, near, far)
            stats_ref[0, pl.ds((2 * kind + 1) * count + row, 1), :] = jnp.where(near_first, far, near)
    for peer in range(1, stats_ref.shape[0]):
        stats_ref[peer] = stats_ref[0]


def finish_kernel(
    phases, tgt_dev, count_ref, own_live_ref, stats_ref, near_ref, far_ref, half_den_ref,
    best_source_ref, best_target_ref,
):
    me = lax.axis_index("blk")
    sources = near_ref.shape[1]
    count = near_ref.shape[0] // LANES
    eye = diagonal(LANES)
    logs = stats_ref[:, : 2 * count, :]
    highest = jnp.max(logs, axis=0)
    half_col = 0.5 * (highest + jnp.log(jnp.sum(jnp.exp(logs - highest[None]), axis=0)))
    best = jnp.max(stats_ref[:, 2 * count :, :], axis=0) - half_col
    row_best = jnp.full((1, sources), NEG_BIG, jnp.float32)
    for row in range(count):
        near_first = near_holds_core_0(phases, tgt_dev, row)
        first, second = half_col[row : row + 1, :], half_col[count + row : count + row + 1, :]
        for ref, values in (
            (near_ref, jnp.where(near_first, first, second)),
            (far_ref, jnp.where(near_first, second, first)),
        ):
            scores = ref[pl.ds(row * LANES, LANES), :]
            margin = jnp.where(scores > 0.5 * NEG_BIG, scores - row_to_column(values, eye), NEG_BIG)
            row_best = jnp.maximum(row_best, jnp.max(margin, axis=0, keepdims=True))
    best_source_ref[...] = jnp.where(live_lanes(count_ref, sources), row_best - half_den_ref[...], 0.0)
    lane = lax.broadcasted_iota(jnp.int32, (tgt_dev, LANES), 1)
    wanted = lax.broadcasted_iota(jnp.int32, (tgt_dev, LANES), 0) + (me >> 1) * tgt_dev
    own = jnp.zeros((tgt_dev, 1), jnp.float32)
    for row in range(count):
        values = jnp.where((me & 1) == 0, best[row : row + 1, :], best[count + row : count + row + 1, :])
        own = own + jnp.sum(jnp.where(lane + row * LANES == wanted, values, 0.0), axis=1, keepdims=True)
    best_target_ref[...] = jnp.where(own_live_ref[...] > 0.5, column_to_row(own, diagonal(tgt_dev)), 0.0)


def mine(src_emb, src_scale, src_count, tgt_emb, tgt_scale, tgt_count):
    ranks = lax.axis_size("blk")
    params = pltpu.CompilerParams(vmem_limit_bytes=24 << 20)
    src_dev, depth = src_emb.shape
    tgt_dev = tgt_emb.shape[0]
    half = ranks // 2 * tgt_dev
    width = depth + LANES
    phases = exchange_phases(ranks)
    source_line = pltpu.VMEM((1, src_dev), jnp.float32)
    half_shape = pltpu.VMEM((half, src_dev), jnp.float32)
    near, own_live = pl.pallas_call(
        pack_kernel,
        out_shape=(pltpu.VMEM((tgt_dev, width), jnp.bfloat16), pltpu.VMEM((1, tgt_dev), jnp.float32)),
        in_specs=[SMEM, HBM, HBM],
        out_specs=(VMEM, VMEM),
        scratch_shapes=[
            pltpu.VMEM((1, tgt_dev), jnp.float32),
            pltpu.SemaphoreType.DMA((2,)),
        ],
        compiler_params=params,
        name="pack",
    )(tgt_count, in_hbm(tgt_emb), in_hbm(tgt_scale.reshape(1, tgt_dev)))
    load = pl.pallas_call(
        load_kernel,
        out_shape=(pltpu.VMEM((src_dev, depth), src_emb.dtype), source_line),
        in_specs=[HBM, HBM],
        out_specs=(VMEM, VMEM),
        scratch_shapes=[pltpu.SemaphoreType.DMA((2,))],
        compiler_params=params,
        cost_estimate=pl.CostEstimate(flops=0, bytes_accessed=2 * src_emb.size * 2, transcendentals=0),
        name="load",
    )
    sources, source_scales = load(in_hbm(src_emb), in_hbm(src_scale.reshape(1, src_dev)))
    offsets = [0]
    for masks in phases:
        came = [exchange(near, ranks, mask) for mask in masks]
        near = jnp.concatenate([near] + came, axis=0)
        offsets = offsets + [offset ^ mask for mask in masks for offset in offsets]
    far = exchange(near, ranks, 1)
    near_scores, near_max, near_sum, near_logs = pl.pallas_call(
        functools.partial(near_kernel, offsets, tgt_dev),
        out_shape=(half_shape, source_line, source_line, pltpu.VMEM((half // LANES, LANES), jnp.float32)),
        in_specs=[SMEM, VMEM, VMEM, VMEM],
        out_specs=(VMEM,) * 4,
        scratch_shapes=[pltpu.VMEM((half, width), jnp.bfloat16)],
        compiler_params=params,
        cost_estimate=pl.CostEstimate(
            flops=2 * half * src_dev * depth, bytes_accessed=4 * half * src_dev, transcendentals=2 * half * src_dev
        ),
        name="near",
    )(src_count, on_chip(near), on_chip(sources), on_chip(source_scales))
    far_scores, row_den, stats = pl.pallas_call(
        functools.partial(far_kernel, phases, offsets, tgt_dev),
        out_shape=(half_shape, source_line, jax.ShapeDtypeStruct((ranks, 4 * half // LANES, LANES), jnp.float32)),
        in_specs=[SMEM] + [VMEM] * 7,
        out_specs=(VMEM,) * 3,
        scratch_shapes=[pltpu.VMEM((half, width), jnp.bfloat16)],
        compiler_params=params,
        name="far",
    )(
        src_count, on_chip(far), on_chip(sources), on_chip(source_scales),
        on_chip(near_scores), on_chip(near_max), on_chip(near_sum), on_chip(near_logs),
    )
    stats = lax.all_to_all(stats, "blk", split_axis=0, concat_axis=0, tiled=True)
    best_source, best_target = pl.pallas_call(
        functools.partial(finish_kernel, phases, tgt_dev),
        out_shape=(
            jax.ShapeDtypeStruct((1, src_dev), jnp.float32),
            jax.ShapeDtypeStruct((1, tgt_dev), jnp.float32),
        ),
        in_specs=[SMEM] + [VMEM] * 5,
        out_specs=(VMEM, VMEM),
        compiler_params=params,
        name="finish",
    )(src_count, on_chip(own_live), on_chip(stats), on_chip(near_scores), on_chip(far_scores), 0.5 * row_den)
    return best_source.reshape(src_dev), best_target.reshape(tgt_dev)


def solution(mesh):
    return jax.shard_map(
        mine,
        mesh=mesh,
        in_specs=(
            P(("pairs", "blk"), None),
            P(("pairs", "blk")),
            P(("pairs", "blk")),
            P(("pairs", "blk"), None),
            P(("pairs", "blk")),
            P(("pairs", "blk")),
        ),
        out_specs=(P(("pairs", "blk")), P(("pairs", "blk"))),
        check_vma=False,
    )
```

time: 123 us -> 34.2 us (0.28)
  blocking collectives: 83.4 us -> 0 us
  Pallas kernels: 0 us -> 6.18 us
  waiting for transfers between devices: 17.4 us -> 12.6 us
  local copies, waits for them, and re-layouts: 4.15 us -> 0.06 us
  starting transfers between devices: 10.7 us -> 13.1 us
  other arithmetic: 2.32 us -> 0.01 us
  matrix products: 1.63 us -> 0 us
    unnamed x2 -> x0, blocking collectives: 64.4 us -> none
    all_gather x1 -> x0, blocking collectives: 18.9 us -> none  [body(): lax.all_gather(tgt_emb, 'blk', axis=0, tiled=True)]
    all_to_all x3 -> x1, waiting for transfers between devices: 17.4 us -> 6.62 us  [mine(): lax.all_to_all(stats, 'blk', split_axis=0, concat_axis=0, tiled=True)]
    ppermute x0 -> x5, starting transfers between devices: none -> 7.24 us  [exchange(): return lax.ppermute(block, 'blk', [(i, i ^ mask) for i in range(ranks)])]
    pallas_call x0 -> x5, Pallas kernels: none -> 6.18 us  [the longest x1 1.83 us: mine(): pl.pallas_call(functools.partial(far_kernel, phases, offsets, tgt_dev), o...]
    ppermute x0 -> x5, waiting for transfers between devices: none -> 5.99 us  [exchange(): return lax.ppermute(block, 'blk', [(i, i ^ mask) for i in range(ranks)])]
    all_to_all x3 -> x1, starting transfers between devices: 10.7 us -> 5.86 us  [mine(): lax.all_to_all(stats, 'blk', split_axis=0, concat_axis=0, tiled=True)]
    unnamed x7 -> x3, local copies, waits for them, and re-layouts: 2.1 us -> 0.03 us
  transfers between devices with their start and end apart: 3 -> 6, of which waited for: 3 -> 4; matrix products, arithmetic and copies ran while one was open for 1% -> 0% of each run, Pallas kernels for 0% -> 8%
where the time goes in v2:
time: 34.2 us; the launch traced here: 33.9 us
  starting transfers between devices  13.1 us (38%)
  waiting for transfers between devices  12.6 us (37%)
  Pallas kernels  6.18 us (18%)
  between operations  1.99 us (6%)
    ppermute x5, starting transfers between devices, exchange(): return lax.ppermute(block, 'blk', [(i, i ^ mask) for i in range(ranks)])  7.24 us
    all_to_all x1, waiting for transfers between devices, mine(): lax.all_to_all(stats, 'blk', split_axis=0, concat_axis=0, tiled=True)  6.62 us
    ppermute x5, waiting for transfers between devices, exchange(): return lax.ppermute(block, 'blk', [(i, i ^ mask) for i in range(ranks)])  5.99 us
    all_to_all x1, starting transfers between devices, mine(): lax.all_to_all(stats, 'blk', split_axis=0, concat_axis=0, tiled=True)  5.86 us
    pallas_call x1, Pallas kernels, mine(): pl.pallas_call(functools.partial(far_kernel, phases, offsets, tgt_dev), o...  1.83 us
    pallas_call x1, Pallas kernels, mine(): load(in_hbm(src_emb), in_hbm(src_scale.reshape(1, src_dev)))  1.61 us
    pallas_call x1, Pallas kernels, mine(): pl.pallas_call(functools.partial(near_kernel, offsets, tgt_dev), out_shap...  1.06 us
    pallas_call x1, Pallas kernels, mine(): pl.pallas_call(functools.partial(finish_kernel, phases, tgt_dev), out_sha...  0.87 us
  transfers between devices with their start and end apart: 6, of which 4 were waited for; matrix products, arithmetic and copies ran while one was open for 0% of the time, Pallas kernels for 8%

profile of v2, /device:TPU:0, one launch (start us, length us, event | category | flops | bytes accessed | tf_op | source)
XLA Modules:
  0.0 33.9 jit_solution(17755932105767092117)
XLA Ops:
  1.3 0.8 %pack.1 = (bf16[16,1152]{1,0:T(8,128)(2,1)S(1)}, f32[1,16]{1,0:T(1,128)S(1)}) custom-call(s32[1]{0:T(128)S(6)} %copy.14.count_ref, bf16[16,1024]{1,0:T(8,128)(2,1)} %tgt_hbm.1, f32[1,16]{1,0:T(1,128)} %bitcast.5), custom_call_target="tpu_custom_call" | custom-call | tf_op jit(solution)/shard_map/pack/pallas_call | solution.py:218
  2.1 3.6 %collective-permute-start = (bf16[16,1152]{1,0:T(8,128)(2,1)S(1)}, bf16[16,1152]{1,0:T(8,128)(2,1)S(1)}, u32[]{:S(2)}, u32[]{:S(2)}) collective-permute-start(bf16[16,1152]{1,0:T(8,128)(2,1)S(1)} %get-tuple-element.16), channel_id=1, source_target_pairs={{0,9},{1,8},{2,11},{3,10},{4,13},{5,12},{6,15},{7,14},{8,1},{9,0},... | collective-permute-start | bytes 110600 | tf_op jit(solution)/shard_map/ppermute | solution.py:29
  5.7 1.9 %collective-permute-done = bf16[16,1152]{1,0:T(8,128)(2,1)S(1)} collective-permute-done((bf16[16,1152]{1,0:T(8,128)(2,1)S(1)}, bf16[16,1152]{1,0:T(8,128)(2,1)S(1)}, u32[]{:S(2)}, u32[]{:S(2)}) %collective-permute-start) | collective-permute-done | bytes 36896 | tf_op jit(solution)/shard_map/ppermute | solution.py:29
  7.5 2.8 %collective-permute-start.1 = (bf16[32,1152]{1,0:T(8,128)(2,1)S(1)}, bf16[32,1152]{1,0:T(8,128)(2,1)S(1)}, u32[]{:S(2)}, u32[]{:S(2)}) collective-permute-start(bf16[32,1152]{1,0:T(8,128)(2,1)S(1)} %get-tuple-element.28), channel_id=1, source_target_pairs={{0,7},{1,6},{2,5},{3,4},{4,3},{5,2},{6,1},{7,0},{8,15},{9,14},{10,... | collective-permute-start | bytes 221192 | tf_op jit(solution)/shard_map/ppermute | solution.py:29
  10.4 0.5 %collective-permute-start.3 = (bf16[32,1152]{1,0:T(8,128)(2,1)S(1)}, bf16[32,1152]{1,0:T(8,128)(2,1)S(1)}, u32[]{:S(2)}, u32[]{:S(2)}) collective-permute-start(bf16[32,1152]{1,0:T(8,128)(2,1)S(1)} %get-tuple-element.28), channel_id=1, source_target_pairs={{0,3},{1,2},{2,1},{3,0},{4,7},{5,6},{6,5},{7,4},{8,11},{9,10},{10,... | collective-permute-start | bytes 221192 | tf_op jit(solution)/shard_map/ppermute | solution.py:29
  10.9 0.1 collective-permute-start.2
  11.0 2.1 %collective-permute-done.1 = bf16[32,1152]{1,0:T(8,128)(2,1)S(1)} collective-permute-done((bf16[32,1152]{1,0:T(8,128)(2,1)S(1)}, bf16[32,1152]{1,0:T(8,128)(2,1)S(1)}, u32[]{:S(2)}, u32[]{:S(2)}) %collective-permute-start.1) | collective-permute-done | bytes 73760 | tf_op jit(solution)/shard_map/ppermute | solution.py:29
  13.1 2.1 %collective-permute-done.2 = bf16[32,1152]{1,0:T(8,128)(2,1)S(1)} collective-permute-done((bf16[32,1152]{1,0:T(8,128)(2,1)S(1)}, bf16[32,1152]{1,0:T(8,128)(2,1)S(1)}, u32[]{:S(2)}, u32[]{:S(2)}) %collective-permute-start.2) | collective-permute-done | bytes 73760 | tf_op jit(solution)/shard_map/ppermute | solution.py:29
  15.2 0.0 collective-permute-done.3
  15.2 0.2 collective-permute-start.4
  16.0 1.6 %load.1 = (bf16[1024,1024]{1,0:T(8,128)(2,1)S(1)}, f32[1,1024]{1,0:T(1,128)S(1)}) custom-call(bf16[1024,1024]{1,0:T(8,128)(2,1)} %src_hbm.1, f32[1,1024]{1,0:T(1,128)} %bitcast.4), custom_call_target="tpu_custom_call" | custom-call | bytes 4194304 | tf_op jit(solution)/shard_map/load/pallas_call | solution.py:240
  17.7 1.1 %near.1 = (f32[128,1024]{1,0:T(8,128)S(1)}, f32[1,1024]{1,0:T(1,128)S(1)}, f32[1,1024]{1,0:T(1,128)S(1)}, f32[1,128]{1,0:T(1,128)S(1)}) custom-call(s32[1]{0:T(128)S(6)} %copy.13.count_ref, bf16[128,1152]{1,0:T(8,128)(2,1)S(1)} %constant_dynamic-update-slice_fusion.2.near_ref, bf16[1024,1024]{1,0:T(8,128)(2,1)S(1)} %get-tuple-element.17.src_ref, ...), custom_call_target="tpu_custom_call" | custom-call | flops 268435456 | bytes 524288 | tf_op jit(solution)/shard_map/near/pallas_call | solution.py:247
  18.7 0.0 collective-permute-done.4.far_ref
  18.7 1.8 %far.1 = (f32[128,1024]{1,0:T(8,128)S(1)}, f32[1,1024]{1,0:T(1,128)S(1)}, f32[16,4,128]{2,1,0:T(4,128)}) custom-call(s32[1]{0:T(128)S(6)} %copy.13.count_ref, bf16[128,1152]{1,0:T(8,128)(2,1)S(1)} %collective-permute-done.4.far_ref, bf16[1024,1024]{1,0:T(8,128)(2,1)S(1)} %get-tuple-element.17.src_ref, f32[1,1024]{1,0:T(1,128)S(1)} %get-tuple-element.18.src_scale_ref, ...), custom_call_target="tpu_custom_call" | custom-call | tf_op jit(solution)/shard_map/far/pallas_call | solution.py:259
  20.6 5.9 %all-to-all-start = ((f32[16,4,128]{2,1,0:T(4,128)}), f32[16,4,128]{2,1,0:T(4,128)S(1)}, u32[]{:S(2)}, u32[]{:S(2)}) async-start(f32[16,4,128]{2,1,0:T(4,128)} %get-tuple-element.23), calls=%async_computation | async-start | bytes 65536 | tf_op jit(solution)/shard_map/all_to_all | solution.py:271
  26.5 6.6 %all-to-all-done.stats_ref = f32[16,4,128]{2,1,0:T(4,128)S(1)} async-done(((f32[16,4,128]{2,1,0:T(4,128)}), f32[16,4,128]{2,1,0:T(4,128)S(1)}, u32[]{:S(2)}, u32[]{:S(2)}) %all-to-all-start) | async-done | bytes 32800 | tf_op jit(solution)/shard_map/all_to_all | solution.py:271
  33.1 0.9 %finish.1 = (f32[1,1024]{1,0:T(1,128)}, f32[1,16]{1,0:T(1,128)}) custom-call(s32[1]{0:T(128)S(6)} %copy.13.count_ref, f32[1,16]{1,0:T(1,128)S(1)} %get-tuple-element.15.own_live_ref, f32[16,4,128]{2,1,0:T(4,128)S(1)} %all-to-all-done.stats_ref, f32[128,1024]{1,0:T(8,128)S(1)} %get-tuple-element.19.near_scores_ref.near_ref, ...), custom_call_target="tpu_custom_call" | custom-call | tf_op jit(solution)/shard_map/finish/pallas_call | solution.py:272
  (6 shorter events, 0.1 us)
Async XLA Ops:
  2.1 5.4 %collective-permute-start = (bf16[16,1152]{1,0:T(8,128)(2,1)S(1)}, bf16[16,1152]{1,0:T(8,128)(2,1)S(1)}, u32[]{:S(2)}, u32[]{:S(2)}) collective-permute-start(bf16[16,1152]{1,0:T(8,128)(2,1)S(1)} %get-tuple-element.16), channel_id=1, source_target_pairs={{0,9},{1,8},{2,11},{3,10},{4,13},{5,12},{6,15},{7,14},{8,1},{9,0},... | collective-permute-start | bytes 110600 | tf_op jit(solution)/shard_map/ppermute | solution.py:29
  7.5 5.6 %collective-permute-start.1 = (bf16[32,1152]{1,0:T(8,128)(2,1)S(1)}, bf16[32,1152]{1,0:T(8,128)(2,1)S(1)}, u32[]{:S(2)}, u32[]{:S(2)}) collective-permute-start(bf16[32,1152]{1,0:T(8,128)(2,1)S(1)} %get-tuple-element.28), channel_id=1, source_target_pairs={{0,7},{1,6},{2,5},{3,4},{4,3},{5,2},{6,1},{7,0},{8,15},{9,14},{10,... | collective-permute-start | bytes 221192 | tf_op jit(solution)/shard_map/ppermute | solution.py:29
  10.4 4.8 %collective-permute-start.3 = (bf16[32,1152]{1,0:T(8,128)(2,1)S(1)}, bf16[32,1152]{1,0:T(8,128)(2,1)S(1)}, u32[]{:S(2)}, u32[]{:S(2)}) collective-permute-start(bf16[32,1152]{1,0:T(8,128)(2,1)S(1)} %get-tuple-element.28), channel_id=1, source_target_pairs={{0,3},{1,2},{2,1},{3,0},{4,7},{5,6},{6,5},{7,4},{8,11},{9,10},{10,... | collective-permute-start | bytes 221192 | tf_op jit(solution)/shard_map/ppermute | solution.py:29
  10.9 4.3 %collective-permute-start.2 = (bf16[32,1152]{1,0:T(8,128)(2,1)S(1)}, bf16[32,1152]{1,0:T(8,128)(2,1)S(1)}, u32[]{:S(2)}, u32[]{:S(2)}) collective-permute-start(bf16[32,1152]{1,0:T(8,128)(2,1)S(1)} %get-tuple-element.28), channel_id=1, source_target_pairs={{0,5},{1,4},{2,7},{3,6},{4,1},{5,0},{6,3},{7,2},{8,13},{9,12},{10,... | collective-permute-start | bytes 221192 | tf_op jit(solution)/shard_map/ppermute | solution.py:29
  15.2 3.5 %collective-permute-start.4 = (bf16[128,1152]{1,0:T(8,128)(2,1)S(1)}, bf16[128,1152]{1,0:T(8,128)(2,1)S(1)}, u32[]{:S(2)}, u32[]{:S(2)}) collective-permute-start(bf16[128,1152]{1,0:T(8,128)(2,1)S(1)} %constant_dynamic-update-slice_fusion.2.near_ref), channel_id=1, source_target_pairs={{0,1},{1,0},{2,3},{3,2},{4,5},{5,4},{6,7},{7,6},{8,9},{9,8},{10,11... | collective-permute-start | bytes 884744 | tf_op jit(solution)/shard_map/ppermute | solution.py:29
  20.6 12.5 %all-to-all-start = ((f32[16,4,128]{2,1,0:T(4,128)}), f32[16,4,128]{2,1,0:T(4,128)S(1)}, u32[]{:S(2)}, u32[]{:S(2)}) async-start(f32[16,4,128]{2,1,0:T(4,128)} %get-tuple-element.23), calls=%async_computation | async-start | bytes 65536 | tf_op jit(solution)/shard_map/all_to_all | solution.py:271

commit v3 on v2

--- a/solution.py
+++ b/solution.py
@@ -10,8 +10,8 @@
 
 NEG_BIG = -1e30
 LANES = 128
+SMEM = pl.BlockSpec(memory_space=pltpu.SMEM)
 VMEM = pl.BlockSpec(memory_space=pltpu.VMEM)
-SMEM = pl.BlockSpec(memory_space=pltpu.SMEM)
 HBM = pl.BlockSpec(memory_space=pltpu.HBM)
 
 
@@ -72,13 +72,15 @@
     copies[1].wait()
 
 
-def load_kernel(src_hbm, scale_hbm, src_ref, scale_ref, sems):
+def load_kernel(count_ref, src_hbm, scale_hbm, src_ref, scale_ref, live_ref, sems):
     copies = [
         pltpu.make_async_copy(src_hbm, src_ref, sems.at[0]),
         pltpu.make_async_copy(scale_hbm, scale_ref, sems.at[1]),
     ]
     for copy in copies:
         copy.start()
+    live = lax.broadcasted_iota(jnp.int32, live_ref.shape, 1) < count_ref[0]
+    live_ref[...] = jnp.where(live, 1.0, 0.0)
     for copy in copies:
         copy.wait()
 
@@ -116,14 +118,10 @@
     return row_sum
 
 
-def live_lanes(count_ref, size):
-    return lax.broadcasted_iota(jnp.int32, (1, size), 1) < count_ref[0]
-
-
 def near_kernel(
-    offsets, tgt_dev, count_ref, near_ref, src_ref, src_scale_ref, scores_ref, row_max_ref, row_sum_ref, logs_ref, tgt_sc
+    offsets, tgt_dev, src_live_ref, near_ref, src_ref, src_scale_ref, scores_ref, row_max_ref, row_sum_ref, logs_ref, tgt_sc
 ):
-    src_live = live_lanes(count_ref, src_ref.shape[0])
+    src_live = src_live_ref[...] > 0.5
     row_max, logs = half_scores(offsets, near_ref, tgt_sc, src_ref, src_scale_ref, src_live, scores_ref, tgt_dev)
     row_max_ref[...] = row_max
     row_sum_ref[...] = exp_sums(scores_ref, row_max)
@@ -144,10 +142,10 @@
 
 def far_kernel(
     phases, offsets, tgt_dev,
-    count_ref, far_ref, src_ref, src_scale_ref, near_scores_ref, near_max_ref, near_sum_ref, near_logs_ref,
+    src_live_ref, far_ref, src_ref, src_scale_ref, near_scores_ref, near_max_ref, near_sum_ref, near_logs_ref,
     scores_ref, row_den_ref, stats_ref, tgt_sc,
 ):
-    src_live = live_lanes(count_ref, src_ref.shape[0])
+    src_live = src_live_ref[...] > 0.5
     offsets = [offset ^ 1 for offset in offsets]
     far_max, logs = half_scores(offsets, far_ref, tgt_sc, src_ref, src_scale_ref, src_live, scores_ref, tgt_dev)
     row_max = jnp.maximum(near_max_ref[...], far_max)
@@ -166,24 +164,27 @@
         near_first = near_holds_core_0(phases, tgt_dev, row)
         pairs = ((near_logs_ref[pl.ds(row, 1), :], logs[row]), (best(near_scores_ref, row), best(scores_ref, row)))
         for kind, (near, far) in enumerate(pairs):
-            stats_ref[0, pl.ds((2 * kind) * count + row, 1), :] = jnp.where(near_first, near, far)
-            stats_ref[0, pl.ds((2 * kind + 1) * count + row, 1), :] = jnp.where(near_first, far, near)
-    for peer in range(1, stats_ref.shape[0]):
-        stats_ref[peer] = stats_ref[0]
+            stats_ref[pl.ds((2 * kind) * count + row, 1), :] = jnp.where(near_first, near, far)
+            stats_ref[pl.ds((2 * kind + 1) * count + row, 1), :] = jnp.where(near_first, far, near)
+
+
+def merged(parts):
+    highest = functools.reduce(jnp.maximum, parts)
+    logs = highest + jnp.log(sum(jnp.exp(part - highest) for part in parts))
+    row = lax.broadcasted_iota(jnp.int32, highest.shape, 0)
+    return jnp.where(row < highest.shape[0] // 2, logs, highest)
 
 
 def finish_kernel(
-    phases, tgt_dev, count_ref, own_live_ref, stats_ref, near_ref, far_ref, half_den_ref,
+    phases, tgt_dev, src_live_ref, own_live_ref, stats_ref, near_ref, far_ref, row_den_ref,
     best_source_ref, best_target_ref,
 ):
     me = lax.axis_index("blk")
     sources = near_ref.shape[1]
     count = near_ref.shape[0] // LANES
     eye = diagonal(LANES)
-    logs = stats_ref[:, : 2 * count, :]
-    highest = jnp.max(logs, axis=0)
-    half_col = 0.5 * (highest + jnp.log(jnp.sum(jnp.exp(logs - highest[None]), axis=0)))
-    best = jnp.max(stats_ref[:, 2 * count :, :], axis=0) - half_col
+    half_col = 0.5 * stats_ref[: 2 * count, :]
+    best = stats_ref[2 * count :, :] - half_col
     row_best = jnp.full((1, sources), NEG_BIG, jnp.float32)
     for row in range(count):
         near_first = near_holds_core_0(phases, tgt_dev, row)
@@ -195,7 +196,7 @@
             scores = ref[pl.ds(row * LANES, LANES), :]
             margin = jnp.where(scores > 0.5 * NEG_BIG, scores - row_to_column(values, eye), NEG_BIG)
             row_best = jnp.maximum(row_best, jnp.max(margin, axis=0, keepdims=True))
-    best_source_ref[...] = jnp.where(live_lanes(count_ref, sources), row_best - half_den_ref[...], 0.0)
+    best_source_ref[...] = jnp.where(src_live_ref[...] > 0.5, row_best - 0.5 * row_den_ref[...], 0.0)
     lane = lax.broadcasted_iota(jnp.int32, (tgt_dev, LANES), 1)
     wanted = lax.broadcasted_iota(jnp.int32, (tgt_dev, LANES), 0) + (me >> 1) * tgt_dev
     own = jnp.zeros((tgt_dev, 1), jnp.float32)
@@ -229,15 +230,17 @@
     )(tgt_count, in_hbm(tgt_emb), in_hbm(tgt_scale.reshape(1, tgt_dev)))
     load = pl.pallas_call(
         load_kernel,
-        out_shape=(pltpu.VMEM((src_dev, depth), src_emb.dtype), source_line),
-        in_specs=[HBM, HBM],
-        out_specs=(VMEM, VMEM),
+        out_shape=(pltpu.VMEM((src_dev, depth), src_emb.dtype), source_line, source_line),
+        in_specs=[SMEM, HBM, HBM],
+        out_specs=(VMEM,) * 3,
         scratch_shapes=[pltpu.SemaphoreType.DMA((2,))],
         compiler_params=params,
         cost_estimate=pl.CostEstimate(flops=0, bytes_accessed=2 * src_emb.size * 2, transcendentals=0),
         name="load",
     )
-    sources, source_scales = load(in_hbm(src_emb), in_hbm(src_scale.reshape(1, src_dev)))
+    sources, source_scales, sources_live = load(
+        src_count, in_hbm(src_emb), in_hbm(src_scale.reshape(1, src_dev))
+    )
     offsets = [0]
     for masks in phases:
         came = [exchange(near, ranks, mask) for mask in masks]
@@ -247,7 +250,7 @@
     near_scores, near_max, near_sum, near_logs = pl.pallas_call(
         functools.partial(near_kernel, offsets, tgt_dev),
         out_shape=(half_shape, source_line, source_line, pltpu.VMEM((half // LANES, LANES), jnp.float32)),
-        in_specs=[SMEM, VMEM, VMEM, VMEM],
+        in_specs=[VMEM] * 4,
         out_specs=(VMEM,) * 4,
         scratch_shapes=[pltpu.VMEM((half, width), jnp.bfloat16)],
         compiler_params=params,
@@ -255,31 +258,34 @@
             flops=2 * half * src_dev * depth, bytes_accessed=4 * half * src_dev, transcendentals=2 * half * src_dev
         ),
         name="near",
-    )(src_count, on_chip(near), on_chip(sources), on_chip(source_scales))
+    )(on_chip(sources_live), on_chip(near), on_chip(sources), on_chip(source_scales))
     far_scores, row_den, stats = pl.pallas_call(
         functools.partial(far_kernel, phases, offsets, tgt_dev),
-        out_shape=(half_shape, source_line, jax.ShapeDtypeStruct((ranks, 4 * half // LANES, LANES), jnp.float32)),
-        in_specs=[SMEM] + [VMEM] * 7,
+        out_shape=(half_shape, source_line, pltpu.VMEM((4 * half // LANES, LANES), jnp.float32)),
+        in_specs=[VMEM] * 8,
         out_specs=(VMEM,) * 3,
         scratch_shapes=[pltpu.VMEM((half, width), jnp.bfloat16)],
         compiler_params=params,
         name="far",
     )(
-        src_count, on_chip(far), on_chip(sources), on_chip(source_scales),
+        on_chip(sources_live), on_chip(far), on_chip(sources), on_chip(source_scales),
         on_chip(near_scores), on_chip(near_max), on_chip(near_sum), on_chip(near_logs),
     )
-    stats = lax.all_to_all(stats, "blk", split_axis=0, concat_axis=0, tiled=True)
+    stats = merged([stats, exchange(stats, ranks, 1)])
+    for masks in phases:
+        came = [exchange(stats, ranks, mask) for mask in masks]
+        stats = merged([stats] + came)
     best_source, best_target = pl.pallas_call(
         functools.partial(finish_kernel, phases, tgt_dev),
         out_shape=(
             jax.ShapeDtypeStruct((1, src_dev), jnp.float32),
             jax.ShapeDtypeStruct((1, tgt_dev), jnp.float32),
         ),
-        in_specs=[SMEM] + [VMEM] * 5,
+        in_specs=[VMEM] * 6,
         out_specs=(VMEM, VMEM),
         compiler_params=params,
         name="finish",
-    )(src_count, on_chip(own_live), on_chip(stats), on_chip(near_scores), on_chip(far_scores), 0.5 * row_den)
+    )(on_chip(sources_live), on_chip(own_live), on_chip(stats), on_chip(near_scores), on_chip(far_scores), on_chip(row_den))
     return best_source.reshape(src_dev), best_target.reshape(tgt_dev)
 
 

time: 34.2 us -> 34 us (level)
  starting transfers between devices: 13.1 us -> 14.1 us
  waiting for transfers between devices: 12.6 us -> 11.9 us
  Pallas kernels: 6.18 us -> 5.57 us
    ppermute x5 -> x10, starting transfers between devices: 7.24 us -> 14.1 us  [exchange(): return lax.ppermute(block, 'blk', [(i, i ^ mask) for i in range(ranks)])]
    all_to_all x1 -> x0, waiting for transfers between devices: 6.62 us -> none  [mine(): lax.all_to_all(stats, 'blk', split_axis=0, concat_axis=0, tiled=True)]
    ppermute x5 -> x10, waiting for transfers between devices: 5.99 us -> 11.9 us  [exchange(): return lax.ppermute(block, 'blk', [(i, i ^ mask) for i in range(ranks)])]
    all_to_all x1 -> x0, starting transfers between devices: 5.86 us -> none  [mine(): lax.all_to_all(stats, 'blk', split_axis=0, concat_axis=0, tiled=True)]
    pallas_call x1, Pallas kernels: 1.83 us -> 1.23 us  [mine(): pl.pallas_call(functools.partial(far_kernel, phases, offsets, tgt_dev), o...]
  transfers between devices with their start and end apart: 6 -> 10, of which waited for: 4 -> 8; matrix products, arithmetic and copies ran while one was open for 0% -> 0% of each run, Pallas kernels for 8% -> 8%
where the time goes in v3:
time: 34 us; the launch traced here: 33.8 us
  starting transfers between devices  14.1 us (41%)
  waiting for transfers between devices  11.9 us (35%)
  Pallas kernels  5.57 us (16%)
  between operations  1.98 us (6%)
    ppermute x10, starting transfers between devices, exchange(): return lax.ppermute(block, 'blk', [(i, i ^ mask) for i in range(ranks)])  14.1 us
    ppermute x10, waiting for transfers between devices, exchange(): return lax.ppermute(block, 'blk', [(i, i ^ mask) for i in range(ranks)])  11.9 us
    pallas_call x1, Pallas kernels, mine(): load(src_count, in_hbm(src_emb), in_hbm(src_scale.reshape(1, src_dev)))  1.61 us
    pallas_call x1, Pallas kernels, mine(): pl.pallas_call(functools.partial(far_kernel, phases, offsets, tgt_dev), o...  1.23 us
    pallas_call x1, Pallas kernels, mine(): pl.pallas_call(functools.partial(near_kernel, offsets, tgt_dev), out_shap...  1.08 us
    pallas_call x1, Pallas kernels, mine(): pl.pallas_call(functools.partial(finish_kernel, phases, tgt_dev), out_sha...  0.85 us
    pallas_call x1, Pallas kernels, mine(): pl.pallas_call(pack_kernel, out_shape=(pltpu.VMEM((tgt_dev, width), jnp.b...  0.79 us
  transfers between devices with their start and end apart: 10, of which 8 were waited for; matrix products, arithmetic and copies ran while one was open for 0% of the time, Pallas kernels for 8%

profile of v3, /device:TPU:0, one launch (start us, length us, event | category | flops | bytes accessed | tf_op | source)
XLA Modules:
  0.0 33.8 jit_solution(6608578974236369517)
XLA Ops:
  1.3 0.8 %pack.1 = (bf16[16,1152]{1,0:T(8,128)(2,1)S(1)}, f32[1,16]{1,0:T(1,128)S(1)}) custom-call(s32[1]{0:T(128)S(6)} %copy.14.count_ref, bf16[16,1024]{1,0:T(8,128)(2,1)} %tgt_hbm.1, f32[1,16]{1,0:T(1,128)} %bitcast.5), custom_call_target="tpu_custom_call" | custom-call | tf_op jit(solution)/shard_map/pack/pallas_call | solution.py:219
  2.1 3.6 %collective-permute-start = (bf16[16,1152]{1,0:T(8,128)(2,1)S(1)}, bf16[16,1152]{1,0:T(8,128)(2,1)S(1)}, u32[]{:S(2)}, u32[]{:S(2)}) collective-permute-start(bf16[16,1152]{1,0:T(8,128)(2,1)S(1)} %get-tuple-element.18), channel_id=1, source_target_pairs={{0,9},{1,8},{2,11},{3,10},{4,13},{5,12},{6,15},{7,14},{8,1},{9,0},... | collective-permute-start | bytes 110600 | tf_op jit(solution)/shard_map/ppermute | solution.py:29
  5.7 1.9 %collective-permute-done = bf16[16,1152]{1,0:T(8,128)(2,1)S(1)} collective-permute-done((bf16[16,1152]{1,0:T(8,128)(2,1)S(1)}, bf16[16,1152]{1,0:T(8,128)(2,1)S(1)}, u32[]{:S(2)}, u32[]{:S(2)}) %collective-permute-start) | collective-permute-done | bytes 36896 | tf_op jit(solution)/shard_map/ppermute | solution.py:29
  7.5 2.8 %collective-permute-start.1 = (bf16[32,1152]{1,0:T(8,128)(2,1)S(1)}, bf16[32,1152]{1,0:T(8,128)(2,1)S(1)}, u32[]{:S(2)}, u32[]{:S(2)}) collective-permute-start(bf16[32,1152]{1,0:T(8,128)(2,1)S(1)} %get-tuple-element.30), channel_id=1, source_target_pairs={{0,7},{1,6},{2,5},{3,4},{4,3},{5,2},{6,1},{7,0},{8,15},{9,14},{10,... | collective-permute-start | bytes 221192 | tf_op jit(solution)/shard_map/ppermute | solution.py:29
  10.4 0.4 %collective-permute-start.2 = (bf16[32,1152]{1,0:T(8,128)(2,1)S(1)}, bf16[32,1152]{1,0:T(8,128)(2,1)S(1)}, u32[]{:S(2)}, u32[]{:S(2)}) collective-permute-start(bf16[32,1152]{1,0:T(8,128)(2,1)S(1)} %get-tuple-element.30), channel_id=1, source_target_pairs={{0,5},{1,4},{2,7},{3,6},{4,1},{5,0},{6,3},{7,2},{8,13},{9,12},{10,... | collective-permute-start | bytes 221192 | tf_op jit(solution)/shard_map/ppermute | solution.py:29
  10.8 0.2 collective-permute-start.3
  11.0 2.0 %collective-permute-done.1 = bf16[32,1152]{1,0:T(8,128)(2,1)S(1)} collective-permute-done((bf16[32,1152]{1,0:T(8,128)(2,1)S(1)}, bf16[32,1152]{1,0:T(8,128)(2,1)S(1)}, u32[]{:S(2)}, u32[]{:S(2)}) %collective-permute-start.1) | collective-permute-done | bytes 73760 | tf_op jit(solution)/shard_map/ppermute | solution.py:29
  13.1 1.9 %collective-permute-done.2 = bf16[32,1152]{1,0:T(8,128)(2,1)S(1)} collective-permute-done((bf16[32,1152]{1,0:T(8,128)(2,1)S(1)}, bf16[32,1152]{1,0:T(8,128)(2,1)S(1)}, u32[]{:S(2)}, u32[]{:S(2)}) %collective-permute-start.2) | collective-permute-done | bytes 73760 | tf_op jit(solution)/shard_map/ppermute | solution.py:29
  14.9 0.2 collective-permute-done.3
  15.1 0.2 collective-permute-start.4
  16.0 1.6 %load.1 = (bf16[1024,1024]{1,0:T(8,128)(2,1)S(1)}, f32[1,1024]{1,0:T(1,128)S(1)}, f32[1,1024]{1,0:T(1,128)S(1)}) custom-call(s32[1]{0:T(128)S(6)} %copy.13.count_ref, bf16[1024,1024]{1,0:T(8,128)(2,1)} %src_hbm.1, f32[1,1024]{1,0:T(1,128)} %bitcast.4), custom_call_target="tpu_custom_call" | custom-call | bytes 4194304 | tf_op jit(solution)/shard_map/load/pallas_call | solution.py:241
  17.6 1.1 %near.1 = (f32[128,1024]{1,0:T(8,128)S(1)}, f32[1,1024]{1,0:T(1,128)S(1)}, f32[1,1024]{1,0:T(1,128)S(1)}, f32[1,128]{1,0:T(1,128)S(1)}) custom-call(f32[1,1024]{1,0:T(1,128)S(1)} %get-tuple-element.16.src_live_ref, bf16[128,1152]{1,0:T(8,128)(2,1)S(1)} %constant_dynamic-update-slice_fusion.2.near_ref, bf16[1024,1024]{1,0:T(8,128)(2,1)S(1)} %get-tuple-element.19.src_ref, ...), custom_call_target="tpu_custom_call" | custom-call | flops 268435456 | bytes 524288 | tf_op jit(solution)/shard_map/near/pallas_call | solution.py:250
  18.7 1.2 %far.1 = (f32[128,1024]{1,0:T(8,128)S(1)}, f32[1,1024]{1,0:T(1,128)S(1)}, f32[4,128]{1,0:T(4,128)S(1)}) custom-call(f32[1,1024]{1,0:T(1,128)S(1)} %get-tuple-element.16.src_live_ref, bf16[128,1152]{1,0:T(8,128)(2,1)S(1)} %collective-permute-done.4.far_ref, bf16[1024,1024]{1,0:T(8,128)(2,1)S(1)} %get-tuple-element.19.src_ref, ...), custom_call_target="tpu_custom_call" | custom-call | tf_op jit(solution)/shard_map/far/pallas_call | solution.py:262
  19.9 0.4 %collective-permute-start.5 = (f32[4,128]{1,0:T(4,128)S(1)}, f32[4,128]{1,0:T(4,128)S(1)}, u32[]{:S(2)}, u32[]{:S(2)}) collective-permute-start(f32[4,128]{1,0:T(4,128)S(1)} %get-tuple-element.25), channel_id=1, source_target_pairs={{0,1},{1,0},{2,3},{3,2},{4,5},{5,4},{6,7},{7,6},{8,9},{9,8},{10,11... | collective-permute-start | bytes 6152 | tf_op jit(solution)/shard_map/ppermute | solution.py:29
  20.4 0.8 %collective-permute-done.5 = f32[4,128]{1,0:T(4,128)S(1)} collective-permute-done((f32[4,128]{1,0:T(4,128)S(1)}, f32[4,128]{1,0:T(4,128)S(1)}, u32[]{:S(2)}, u32[]{:S(2)}) %collective-permute-start.5) | collective-permute-done | bytes 2080 | tf_op jit(solution)/shard_map/ppermute | solution.py:29
  21.2 0.1 add_select_fusion.2
  21.3 2.8 %collective-permute-start.6 = (f32[4,128]{1,0:T(4,128)S(1)}, f32[4,128]{1,0:T(4,128)S(1)}, u32[]{:S(2)}, u32[]{:S(2)}) collective-permute-start(f32[4,128]{1,0:T(4,128)S(1)} %add_select_fusion.2), channel_id=1, source_target_pairs={{0,9},{1,8},{2,11},{3,10},{4,13},{5,12},{6,15},{7,14},{8,1},{9,0},... | collective-permute-start | bytes 6152 | tf_op jit(solution)/shard_map/ppermute | solution.py:29
  24.1 1.3 %collective-permute-done.6 = f32[4,128]{1,0:T(4,128)S(1)} collective-permute-done((f32[4,128]{1,0:T(4,128)S(1)}, f32[4,128]{1,0:T(4,128)S(1)}, u32[]{:S(2)}, u32[]{:S(2)}) %collective-permute-start.6) | collective-permute-done | bytes 2080 | tf_op jit(solution)/shard_map/ppermute | solution.py:29
  25.5 1.3 %collective-permute-start.9 = (f32[4,128]{1,0:T(4,128)S(1)}, f32[4,128]{1,0:T(4,128)S(1)}, u32[]{:S(2)}, u32[]{:S(2)}) collective-permute-start(f32[4,128]{1,0:T(4,128)S(1)} %add_select_fusion.1), channel_id=1, source_target_pairs={{0,3},{1,2},{2,1},{3,0},{4,7},{5,6},{6,5},{7,4},{8,11},{9,10},{10,... | collective-permute-start | bytes 6152 | tf_op jit(solution)/shard_map/ppermute | solution.py:29
  26.7 2.2 %collective-permute-start.8 = (f32[4,128]{1,0:T(4,128)S(1)}, f32[4,128]{1,0:T(4,128)S(1)}, u32[]{:S(2)}, u32[]{:S(2)}) collective-permute-start(f32[4,128]{1,0:T(4,128)S(1)} %add_select_fusion.1), channel_id=1, source_target_pairs={{0,5},{1,4},{2,7},{3,6},{4,1},{5,0},{6,3},{7,2},{8,13},{9,12},{10,... | collective-permute-start | bytes 6152 | tf_op jit(solution)/shard_map/ppermute | solution.py:29
  29.0 1.3 %collective-permute-done.8 = f32[4,128]{1,0:T(4,128)S(1)} collective-permute-done((f32[4,128]{1,0:T(4,128)S(1)}, f32[4,128]{1,0:T(4,128)S(1)}, u32[]{:S(2)}, u32[]{:S(2)}) %collective-permute-start.8) | collective-permute-done | bytes 2080 | tf_op jit(solution)/shard_map/ppermute | solution.py:29
  30.3 2.6 %collective-permute-done.7 = f32[4,128]{1,0:T(4,128)S(1)} collective-permute-done((f32[4,128]{1,0:T(4,128)S(1)}, f32[4,128]{1,0:T(4,128)S(1)}, u32[]{:S(2)}, u32[]{:S(2)}) %collective-permute-start.7) | collective-permute-done | bytes 2080 | tf_op jit(solution)/shard_map/ppermute | solution.py:29
  32.9 0.1 add_select_fusion.stats_ref
  33.0 0.9 %finish.1 = (f32[1,1024]{1,0:T(1,128)}, f32[1,16]{1,0:T(1,128)}) custom-call(f32[1,1024]{1,0:T(1,128)S(1)} %get-tuple-element.16.src_live_ref, f32[1,16]{1,0:T(1,128)S(1)} %get-tuple-element.17.own_live_ref, f32[4,128]{1,0:T(4,128)S(1)} %add_select_fusion.stats_ref, f32[128,1024]{1,0:T(8,128)S(1)} %get-tuple-element.21.near_scores_ref.near_ref, ...), custom_call_target="tpu_custom_call" | custom-call | tf_op jit(solution)/shard_map/finish/pallas_call | solution.py:278
  (10 shorter events, 0.1 us)
Async XLA Ops:
  2.1 5.4 %collective-permute-start = (bf16[16,1152]{1,0:T(8,128)(2,1)S(1)}, bf16[16,1152]{1,0:T(8,128)(2,1)S(1)}, u32[]{:S(2)}, u32[]{:S(2)}) collective-permute-start(bf16[16,1152]{1,0:T(8,128)(2,1)S(1)} %get-tuple-element.18), channel_id=1, source_target_pairs={{0,9},{1,8},{2,11},{3,10},{4,13},{5,12},{6,15},{7,14},{8,1},{9,0},... | collective-permute-start | bytes 110600 | tf_op jit(solution)/shard_map/ppermute | solution.py:29
  7.5 5.5 %collective-permute-start.1 = (bf16[32,1152]{1,0:T(8,128)(2,1)S(1)}, bf16[32,1152]{1,0:T(8,128)(2,1)S(1)}, u32[]{:S(2)}, u32[]{:S(2)}) collective-permute-start(bf16[32,1152]{1,0:T(8,128)(2,1)S(1)} %get-tuple-element.30), channel_id=1, source_target_pairs={{0,7},{1,6},{2,5},{3,4},{4,3},{5,2},{6,1},{7,0},{8,15},{9,14},{10,... | collective-permute-start | bytes 221192 | tf_op jit(solution)/shard_map/ppermute | solution.py:29
  10.4 4.6 %collective-permute-start.2 = (bf16[32,1152]{1,0:T(8,128)(2,1)S(1)}, bf16[32,1152]{1,0:T(8,128)(2,1)S(1)}, u32[]{:S(2)}, u32[]{:S(2)}) collective-permute-start(bf16[32,1152]{1,0:T(8,128)(2,1)S(1)} %get-tuple-element.30), channel_id=1, source_target_pairs={{0,5},{1,4},{2,7},{3,6},{4,1},{5,0},{6,3},{7,2},{8,13},{9,12},{10,... | collective-permute-start | bytes 221192 | tf_op jit(solution)/shard_map/ppermute | solution.py:29
  10.8 4.3 %collective-permute-start.3 = (bf16[32,1152]{1,0:T(8,128)(2,1)S(1)}, bf16[32,1152]{1,0:T(8,128)(2,1)S(1)}, u32[]{:S(2)}, u32[]{:S(2)}) collective-permute-start(bf16[32,1152]{1,0:T(8,128)(2,1)S(1)} %get-tuple-element.30), channel_id=1, source_target_pairs={{0,3},{1,2},{2,1},{3,0},{4,7},{5,6},{6,5},{7,4},{8,11},{9,10},{10,... | collective-permute-start | bytes 221192 | tf_op jit(solution)/shard_map/ppermute | solution.py:29
  15.1 3.6 %collective-permute-start.4 = (bf16[128,1152]{1,0:T(8,128)(2,1)S(1)}, bf16[128,1152]{1,0:T(8,128)(2,1)S(1)}, u32[]{:S(2)}, u32[]{:S(2)}) collective-permute-start(bf16[128,1152]{1,0:T(8,128)(2,1)S(1)} %constant_dynamic-update-slice_fusion.2.near_ref), channel_id=1, source_target_pairs={{0,1},{1,0},{2,3},{3,2},{4,5},{5,4},{6,7},{7,6},{8,9},{9,8},{10,11... | collective-permute-start | bytes 884744 | tf_op jit(solution)/shard_map/ppermute | solution.py:29
  19.9 1.3 %collective-permute-start.5 = (f32[4,128]{1,0:T(4,128)S(1)}, f32[4,128]{1,0:T(4,128)S(1)}, u32[]{:S(2)}, u32[]{:S(2)}) collective-permute-start(f32[4,128]{1,0:T(4,128)S(1)} %get-tuple-element.25), channel_id=1, source_target_pairs={{0,1},{1,0},{2,3},{3,2},{4,5},{5,4},{6,7},{7,6},{8,9},{9,8},{10,11... | collective-permute-start | bytes 6152 | tf_op jit(solution)/shard_map/ppermute | solution.py:29
  21.3 4.1 %collective-permute-start.6 = (f32[4,128]{1,0:T(4,128)S(1)}, f32[4,128]{1,0:T(4,128)S(1)}, u32[]{:S(2)}, u32[]{:S(2)}) collective-permute-start(f32[4,128]{1,0:T(4,128)S(1)} %add_select_fusion.2), channel_id=1, source_target_pairs={{0,9},{1,8},{2,11},{3,10},{4,13},{5,12},{6,15},{7,14},{8,1},{9,0},... | collective-permute-start | bytes 6152 | tf_op jit(solution)/shard_map/ppermute | solution.py:29
  25.5 3.5 %collective-permute-start.9 = (f32[4,128]{1,0:T(4,128)S(1)}, f32[4,128]{1,0:T(4,128)S(1)}, u32[]{:S(2)}, u32[]{:S(2)}) collective-permute-start(f32[4,128]{1,0:T(4,128)S(1)} %add_select_fusion.1), channel_id=1, source_target_pairs={{0,3},{1,2},{2,1},{3,0},{4,7},{5,6},{6,5},{7,4},{8,11},{9,10},{10,... | collective-permute-start | bytes 6152 | tf_op jit(solution)/shard_map/ppermute | solution.py:29
  26.7 3.5 %collective-permute-start.8 = (f32[4,128]{1,0:T(4,128)S(1)}, f32[4,128]{1,0:T(4,128)S(1)}, u32[]{:S(2)}, u32[]{:S(2)}) collective-permute-start(f32[4,128]{1,0:T(4,128)S(1)} %add_select_fusion.1), channel_id=1, source_target_pairs={{0,5},{1,4},{2,7},{3,6},{4,1},{5,0},{6,3},{7,2},{8,13},{9,12},{10,... | collective-permute-start | bytes 6152 | tf_op jit(solution)/shard_map/ppermute | solution.py:29
  29.0 3.9 %collective-permute-start.7 = (f32[4,128]{1,0:T(4,128)S(1)}, f32[4,128]{1,0:T(4,128)S(1)}, u32[]{:S(2)}, u32[]{:S(2)}) collective-permute-start(f32[4,128]{1,0:T(4,128)S(1)} %add_select_fusion.1), channel_id=1, source_target_pairs={{0,7},{1,6},{2,5},{3,4},{4,3},{5,2},{6,1},{7,0},{8,15},{9,14},{10,... | collective-permute-start | bytes 6152 | tf_op jit(solution)/shard_map/ppermute | solution.py:29

commit v4 on v3

v4 whole, which is shorter than its diff:
```python
import functools

import jax
import jax.numpy as jnp
from jax import lax
from jax.experimental import pallas as pl
from jax.experimental.pallas import tpu as pltpu
from jax.sharding import PartitionSpec as P


NEG_BIG = -1e30
LOG2_E = 1.4426950408889634
LN_2 = 0.6931471805599453
LANES = 128
SMEM = pl.BlockSpec(memory_space=pltpu.SMEM)
VMEM = pl.BlockSpec(memory_space=pltpu.VMEM)
HBM = pl.BlockSpec(memory_space=pltpu.HBM)


def exchange_phases(ranks):
    bits = list(range(ranks.bit_length() - 2, 0, -1))
    phases = [[bits.pop(0)]] if len(bits) % 2 else []
    return phases + [[low, high] for high, low in zip(bits[::2], bits[1::2])]


def phase_masks(bits):
    masks = [0]
    for bit in bits:
        masks = masks + [mask | (1 << bit) for mask in masks]
    return [mask | 1 for mask in masks[1:]]


def own_slot(phases, rank):
    place = 0
    for index, bit in enumerate(sum(phases, [])):
        place = place | (((rank >> bit) & 1) << index)
    return place


def crossed(phases, slot):
    crossing, index = 0, 0
    for bits in phases:
        part = (slot >> index) & ((1 << len(bits)) - 1)
        crossing = crossing ^ jnp.where(part != 0, 1, 0)
        index += len(bits)
    return crossing


def exchange(block, ranks, mask):
    return lax.ppermute(block, "blk", [(i, i ^ mask) for i in range(ranks)])


def on_chip(array):
    return pltpu.with_memory_space_constraint(array, pltpu.VMEM)


def in_hbm(array):
    return pltpu.with_memory_space_constraint(array, pltpu.HBM)


def diagonal(size):
    shape = (size, size)
    return lax.broadcasted_iota(jnp.int32, shape, 0) == lax.broadcasted_iota(jnp.int32, shape, 1)


def column_to_row(column, eye):
    return jnp.sum(jnp.where(eye, column, 0.0), axis=0, keepdims=True)


def row_to_column(row, eye):
    return jnp.sum(jnp.where(eye, row, 0.0), axis=1, keepdims=True)


def pack_kernel(count_ref, tgt_hbm, scale_hbm, packed_ref, live_ref, scale_ref, sems):
    rows, depth = tgt_hbm.shape
    copies = [
        pltpu.make_async_copy(scale_hbm, scale_ref, sems.at[0]),
        pltpu.make_async_copy(tgt_hbm, packed_ref.at[:, pl.ds(0, depth)], sems.at[1]),
    ]
    for copy in copies:
        copy.start()
    copies[0].wait()
    live = lax.broadcasted_iota(jnp.int32, (1, rows), 1) < count_ref[0]
    live_ref[...] = jnp.where(live, 1.0, 0.0)
    scale = row_to_column(jnp.where(live, scale_ref[...], 0.0), diagonal(rows))
    high = scale.astype(jnp.bfloat16).astype(jnp.float32)
    rest = scale - high
    middle = rest.astype(jnp.bfloat16).astype(jnp.float32)
    low = rest - middle
    lane = lax.broadcasted_iota(jnp.int32, (rows, LANES), 1)
    terms = jnp.where(lane == 0, high, jnp.where(lane == 1, middle, jnp.where(lane == 2, low, 0.0)))
    packed_ref[:, depth:] = terms.astype(jnp.bfloat16)
    copies[1].wait()


def load_kernel(src_hbm, scale_hbm, src_ref, scale_ref, sems):
    copies = [
        pltpu.make_async_copy(src_hbm, src_ref, sems.at[0]),
        pltpu.make_async_copy(scale_hbm, scale_ref, sems.at[1]),
    ]
    for copy in copies:
        copy.start()
    copies[1].wait()
    scale_ref[...] = scale_ref[...] * LOG2_E
    copies[0].wait()


def column_block(sources):
    return 2 * LANES if sources % (2 * LANES) == 0 else LANES


def fold(values, op):
    return functools.reduce(op, [values[:, at : at + LANES] for at in range(0, values.shape[1], LANES)])


class Half:
    def __init__(self, blocks_ref, src_ref, scale_ref, live_ref, scores_ref, peak_sc, sum_sc):
        self.blocks, self.src, self.scale, self.live = blocks_ref, src_ref, scale_ref, live_ref
        self.scores, self.peak, self.sums = scores_ref, peak_sc, sum_sc
        self.starts = range(0, blocks_ref.shape[0], LANES)

    def columns(self, at, size):
        depth = self.src.shape[1]
        columns = pl.ds(at, size)
        live = self.live[:, columns] > 0.5
        largest = []
        for start in self.starts:
            rows = pl.ds(start, LANES)
            product = lax.dot_general(
                self.blocks[rows, :depth], self.src[columns, :], (((1,), (1,)), ((), ())),
                preferred_element_type=jnp.float32,
            )
            scale = jnp.sum(self.blocks[rows, depth:].astype(jnp.float32), axis=1, keepdims=True)
            scores = jnp.where(scale > 0.0, product * scale * self.scale[:, columns], NEG_BIG)
            self.scores[rows, columns] = scores
            largest.append(jnp.max(scores, axis=0, keepdims=True))
            masked = jnp.where(live, scores, NEG_BIG)
            peak = fold(masked, jnp.maximum)
            if at:
                before = self.peak[rows, :]
                peak = jnp.maximum(before, peak)
            sums = functools.reduce(
                jnp.add, [jnp.exp2(masked[:, tile : tile + LANES] - peak) for tile in range(0, size, LANES)]
            )
            if at:
                sums = sums + self.sums[rows, :] * jnp.exp2(before - peak)
            self.peak[rows, :] = peak
            self.sums[rows, :] = sums
        return functools.reduce(jnp.maximum, largest)

    def exp_sums(self, at, size, row_max):
        columns = pl.ds(at, size)
        parts = [
            jnp.sum(jnp.exp2(self.scores[pl.ds(start, LANES), columns] - row_max), axis=0, keepdims=True)
            for start in self.starts
        ]
        return functools.reduce(jnp.add, parts)

    def logs(self, eye):
        rows = []
        for start in self.starts:
            peak = self.peak[pl.ds(start, LANES), :]
            highest = jnp.max(peak, axis=1, keepdims=True)
            total = jnp.sum(self.sums[pl.ds(start, LANES), :] * jnp.exp2(peak - highest), axis=1, keepdims=True)
            rows.append(column_to_row(highest + jnp.log(total) * LOG2_E, eye))
        return rows


def near_kernel(
    near_ref, src_ref, src_scale_ref, src_live_ref, scores_ref, row_max_ref, row_sum_ref, logs_ref, peak_sc, sum_sc
):
    half = Half(near_ref, src_ref, src_scale_ref, src_live_ref, scores_ref, peak_sc, sum_sc)
    sources = src_ref.shape[0]
    size = column_block(sources)
    for at in range(0, sources, size):
        row_max = half.columns(at, size)
        row_max_ref[:, pl.ds(at, size)] = row_max
        row_sum_ref[:, pl.ds(at, size)] = half.exp_sums(at, size, row_max)
    for row, values in enumerate(half.logs(diagonal(LANES))):
        logs_ref[pl.ds(row, 1), :] = values


def slot_lanes(phases, tgt_dev, row):
    me = lax.axis_index("blk")
    lane = lax.broadcasted_iota(jnp.int32, (1, LANES), 1)
    slot = (lane + row * LANES) // tgt_dev
    core_0 = (crossed(phases, slot) ^ (me & 1)) == 0
    return core_0, lane ^ ((own_slot(phases, me) * tgt_dev) & (LANES - 1))


def shared_row(phases, tgt_dev, row):
    return row ^ ((own_slot(phases, lax.axis_index("blk")) * tgt_dev) // LANES)


def permuted(row, lanes):
    shape = (8, LANES)
    lanes = jnp.broadcast_to(lanes, shape)
    return jnp.take_along_axis(jnp.broadcast_to(row, shape), lanes, axis=1)[:1, :]


def far_kernel(
    phases, tgt_dev,
    far_ref, src_ref, src_scale_ref, src_live_ref, near_scores_ref, near_max_ref, near_sum_ref, near_logs_ref,
    scores_ref, row_den_ref, stats_ref, peak_sc, sum_sc, near_best_sc, far_best_sc,
):
    half = Half(far_ref, src_ref, src_scale_ref, src_live_ref, scores_ref, peak_sc, sum_sc)
    sources = src_ref.shape[0]
    size = column_block(sources)
    for at in range(0, sources, size):
        columns = pl.ds(at, size)
        far_max = half.columns(at, size)
        near_max = near_max_ref[:, columns]
        row_max = jnp.maximum(near_max, far_max)
        row_sum = near_sum_ref[:, columns] * jnp.exp2(near_max - row_max) + half.exp_sums(at, size, row_max)
        row_den = row_max + jnp.log(row_sum) * LOG2_E
        row_den_ref[:, columns] = row_den
        taken = jnp.where(src_live_ref[:, columns] > 0.5, 0.5 * row_den, -NEG_BIG)
        for ref, best_sc in ((near_scores_ref, near_best_sc), (scores_ref, far_best_sc)):
            for start in half.starts:
                rows = pl.ds(start, LANES)
                best = fold(ref[rows, columns] - taken, jnp.maximum)
                best_sc[rows, :] = jnp.maximum(best_sc[rows, :], best) if at else best
    eye = diagonal(LANES)
    count = len(half.starts)
    logs = half.logs(eye)
    for row, start in enumerate(half.starts):
        rows = pl.ds(start, LANES)
        near_best, far_best = (
            column_to_row(jnp.max(best_sc[rows, :], axis=1, keepdims=True), eye)
            for best_sc in (near_best_sc, far_best_sc)
        )
        core_0, lanes = slot_lanes(phases, tgt_dev, row)
        place = shared_row(phases, tgt_dev, row)
        pairs = ((near_logs_ref[pl.ds(row, 1), :], logs[row]), (near_best, far_best))
        for kind, (near, far) in enumerate(pairs):
            for core, values in enumerate((jnp.where(core_0, near, far), jnp.where(core_0, far, near))):
                stats_ref[pl.ds((2 * kind + core) * count + place, 1), :] = permuted(values, lanes)


def merged(parts):
    highest = functools.reduce(jnp.maximum, parts)
    logs = highest + jnp.log(sum(jnp.exp2(part - highest) for part in parts)) * LOG2_E
    row = lax.broadcasted_iota(jnp.int32, highest.shape, 0)
    return jnp.where(row < highest.shape[0] // 2, logs, highest)


def finish_kernel(
    phases, tgt_dev, src_live_ref, own_live_ref, stats_ref, near_ref, far_ref, row_den_ref,
    best_source_ref, best_target_ref,
):
    me = lax.axis_index("blk")
    sources = near_ref.shape[1]
    count = near_ref.shape[0] // LANES
    eye = diagonal(LANES)
    row_best = jnp.full((1, sources), NEG_BIG, jnp.float32)
    for row in range(count):
        core_0, lanes = slot_lanes(phases, tgt_dev, row)
        place = shared_row(phases, tgt_dev, row)
        first = permuted(0.5 * stats_ref[pl.ds(place, 1), :], lanes)
        second = permuted(0.5 * stats_ref[pl.ds(count + place, 1), :], lanes)
        for ref, values in (
            (near_ref, jnp.where(core_0, first, second)),
            (far_ref, jnp.where(core_0, second, first)),
        ):
            margin = ref[pl.ds(row * LANES, LANES), :] - row_to_column(values, eye)
            row_best = jnp.maximum(row_best, jnp.max(margin, axis=0, keepdims=True))
    best_source_ref[...] = jnp.where(src_live_ref[...] > 0.5, (row_best - 0.5 * row_den_ref[...]) * LN_2, 0.0)
    core, first = me & 1, own_slot(phases, me) * tgt_dev
    row = core * count + first // LANES
    best = stats_ref[pl.ds(2 * count + row, 1), :] - 0.5 * stats_ref[pl.ds(row, 1), :]
    lane = lax.broadcasted_iota(jnp.int32, (tgt_dev, LANES), 1)
    wanted = lax.broadcasted_iota(jnp.int32, (tgt_dev, LANES), 0) + (first & (LANES - 1))
    own = jnp.sum(jnp.where(lane == wanted, best * LN_2, 0.0), axis=1, keepdims=True)
    best_target_ref[...] = jnp.where(own_live_ref[...] > 0.5, column_to_row(own, diagonal(tgt_dev)), 0.0)


def mine(src_emb, src_scale, src_count, tgt_emb, tgt_scale, tgt_count):
    ranks = lax.axis_size("blk")
    params = pltpu.CompilerParams(vmem_limit_bytes=24 << 20)
    src_dev, depth = src_emb.shape
    tgt_dev = tgt_emb.shape[0]
    half = ranks // 2 * tgt_dev
    width = depth + LANES
    phases = exchange_phases(ranks)
    source_line = pltpu.VMEM((1, src_dev), jnp.float32)
    half_shape = pltpu.VMEM((half, src_dev), jnp.float32)
    near, own_live = pl.pallas_call(
        pack_kernel,
        out_shape=(pltpu.VMEM((tgt_dev, width), jnp.bfloat16), pltpu.VMEM((1, tgt_dev), jnp.float32)),
        in_specs=[SMEM, HBM, HBM],
        out_specs=(VMEM, VMEM),
        scratch_shapes=[
            pltpu.VMEM((1, tgt_dev), jnp.float32),
            pltpu.SemaphoreType.DMA((2,)),
        ],
        compiler_params=params,
        name="pack",
    )(tgt_count, in_hbm(tgt_emb), in_hbm(tgt_scale.reshape(1, tgt_dev)))
    load = pl.pallas_call(
        load_kernel,
        out_shape=(pltpu.VMEM((src_dev, depth), src_emb.dtype), source_line),
        in_specs=[HBM, HBM],
        out_specs=(VMEM, VMEM),
        scratch_shapes=[pltpu.SemaphoreType.DMA((2,))],
        compiler_params=params,
        cost_estimate=pl.CostEstimate(flops=0, bytes_accessed=2 * src_emb.size * 2, transcendentals=0),
        name="load",
    )
    sources, source_scales = load(in_hbm(src_emb), in_hbm(src_scale.reshape(1, src_dev)))
    sources_live = jnp.where(lax.broadcasted_iota(jnp.int32, (1, src_dev), 1) < src_count, 1.0, 0.0)
    for bits in phases:
        came = [exchange(near, ranks, mask) for mask in phase_masks(bits)]
        near = jnp.concatenate([near] + came, axis=0)
    far = exchange(near, ranks, 1)
    half_lanes = pltpu.VMEM((half, LANES), jnp.float32)
    near_scores, near_max, near_sum, near_logs = pl.pallas_call(
        near_kernel,
        out_shape=(half_shape, source_line, source_line, pltpu.VMEM((half // LANES, LANES), jnp.float32)),
        in_specs=[VMEM] * 4,
        out_specs=(VMEM,) * 4,
        scratch_shapes=[half_lanes] * 2,
        compiler_params=params,
        cost_estimate=pl.CostEstimate(
            flops=2 * half * src_dev * depth, bytes_accessed=4 * half * src_dev, transcendentals=2 * half * src_dev
        ),
        name="near",
    )(on_chip(near), on_chip(sources), on_chip(source_scales), on_chip(sources_live))
    far_scores, row_den, stats = pl.pallas_call(
        functools.partial(far_kernel, phases, tgt_dev),
        out_shape=(half_shape, source_line, pltpu.VMEM((4 * half // LANES, LANES), jnp.float32)),
        in_specs=[VMEM] * 8,
        out_specs=(VMEM,) * 3,
        scratch_shapes=[half_lanes] * 4,
        compiler_params=params,
        name="far",
    )(
        on_chip(far), on_chip(sources), on_chip(source_scales), on_chip(sources_live),
        on_chip(near_scores), on_chip(near_max), on_chip(near_sum), on_chip(near_logs),
    )
    stats = merged([stats, exchange(stats, ranks, 1)])
    for bits in phases:
        came = [exchange(stats, ranks, mask) for mask in phase_masks(bits)]
        stats = merged([stats] + came)
    best_source, best_target = pl.pallas_call(
        functools.partial(finish_kernel, phases, tgt_dev),
        out_shape=(
            jax.ShapeDtypeStruct((1, src_dev), jnp.float32),
            jax.ShapeDtypeStruct((1, tgt_dev), jnp.float32),
        ),
        in_specs=[VMEM] * 6,
        out_specs=(VMEM, VMEM),
        compiler_params=params,
        name="finish",
    )(
        on_chip(sources_live), on_chip(own_live), on_chip(stats), on_chip(near_scores), on_chip(far_scores),
        on_chip(row_den),
    )
    return best_source.reshape(src_dev), best_target.reshape(tgt_dev)


def solution(mesh):
    return jax.shard_map(
        mine,
        mesh=mesh,
        in_specs=(
            P(("pairs", "blk"), None),
            P(("pairs", "blk")),
            P(("pairs", "blk")),
            P(("pairs", "blk"), None),
            P(("pairs", "blk")),
            P(("pairs", "blk")),
        ),
        out_specs=(P(("pairs", "blk")), P(("pairs", "blk"))),
        check_vma=False,
    )
```

time: 34 us -> 33 us (0.971)
  waiting for transfers between devices: 11.9 us -> 10.9 us
    ppermute x10, waiting for transfers between devices: 11.9 us -> 10.9 us  [exchange(): return lax.ppermute(block, 'blk', [(i, i ^ mask) for i in range(ranks)])]
  transfers between devices with their start and end apart: 10 -> 10, of which waited for: 8 -> 9; matrix products, arithmetic and copies ran while one was open for 0% -> 0% of each run, Pallas kernels for 8% -> 8%
where the time goes in v4:
time: 33 us; the launch traced here: 32.7 us
  starting transfers between devices  14 us (42%)
  waiting for transfers between devices  10.9 us (33%)
  Pallas kernels  5.62 us (17%)
  between operations  1.98 us (6%)
    ppermute x10, starting transfers between devices, exchange(): return lax.ppermute(block, 'blk', [(i, i ^ mask) for i in range(ranks)])  14 us
    ppermute x10, waiting for transfers between devices, exchange(): return lax.ppermute(block, 'blk', [(i, i ^ mask) for i in range(ranks)])  10.9 us
    pallas_call x1, Pallas kernels, mine(): load(in_hbm(src_emb), in_hbm(src_scale.reshape(1, src_dev)))  1.61 us
    pallas_call x1, Pallas kernels, mine(): pl.pallas_call(functools.partial(far_kernel, phases, tgt_dev), out_shape=...  1.26 us
    pallas_call x1, Pallas kernels, mine(): pl.pallas_call(near_kernel, out_shape=(half_shape, source_line, source_li...  1.09 us
    pallas_call x1, Pallas kernels, mine(): pl.pallas_call(functools.partial(finish_kernel, phases, tgt_dev), out_sha...  0.87 us
    pallas_call x1, Pallas kernels, mine(): pl.pallas_call(pack_kernel, out_shape=(pltpu.VMEM((tgt_dev, width), jnp.b...  0.79 us
  transfers between devices with their start and end apart: 10, of which 9 were waited for; matrix products, arithmetic and copies ran while one was open for 0% of the time, Pallas kernels for 8%

profile of v4, /device:TPU:0, one launch (start us, length us, event | category | flops | bytes accessed | tf_op | source)
XLA Modules:
  0.0 32.7 jit_solution(7947239367647343480)
XLA Ops:
  1.3 0.8 %pack.1 = (bf16[16,1152]{1,0:T(8,128)(2,1)S(1)}, f32[1,16]{1,0:T(1,128)S(1)}) custom-call(s32[1]{0:T(128)S(6)} %copy.14.count_ref, bf16[16,1024]{1,0:T(8,128)(2,1)} %tgt_hbm.1, f32[1,16]{1,0:T(1,128)} %bitcast.7), custom_call_target="tpu_custom_call" | custom-call | tf_op jit(solution)/shard_map/pack/pallas_call | solution.py:287
  2.1 3.6 %collective-permute-start = (bf16[16,1152]{1,0:T(8,128)(2,1)S(1)}, bf16[16,1152]{1,0:T(8,128)(2,1)S(1)}, u32[]{:S(2)}, u32[]{:S(2)}) collective-permute-start(bf16[16,1152]{1,0:T(8,128)(2,1)S(1)} %get-tuple-element.16), channel_id=1, source_target_pairs={{0,9},{1,8},{2,11},{3,10},{4,13},{5,12},{6,15},{7,14},{8,1},{9,0},... | collective-permute-start | bytes 110600 | tf_op jit(solution)/shard_map/ppermute | solution.py:50
  5.7 1.9 %collective-permute-done = bf16[16,1152]{1,0:T(8,128)(2,1)S(1)} collective-permute-done((bf16[16,1152]{1,0:T(8,128)(2,1)S(1)}, bf16[16,1152]{1,0:T(8,128)(2,1)S(1)}, u32[]{:S(2)}, u32[]{:S(2)}) %collective-permute-start) | collective-permute-done | bytes 36896 | tf_op jit(solution)/shard_map/ppermute | solution.py:50
  7.5 1.8 %collective-permute-start.1 = (bf16[32,1152]{1,0:T(8,128)(2,1)S(1)}, bf16[32,1152]{1,0:T(8,128)(2,1)S(1)}, u32[]{:S(2)}, u32[]{:S(2)}) collective-permute-start(bf16[32,1152]{1,0:T(8,128)(2,1)S(1)} %get-tuple-element.28), channel_id=1, source_target_pairs={{0,3},{1,2},{2,1},{3,0},{4,7},{5,6},{6,5},{7,4},{8,11},{9,10},{10,... | collective-permute-start | bytes 221192 | tf_op jit(solution)/shard_map/ppermute | solution.py:50
  9.4 1.6 %collective-permute-start.2 = (bf16[32,1152]{1,0:T(8,128)(2,1)S(1)}, bf16[32,1152]{1,0:T(8,128)(2,1)S(1)}, u32[]{:S(2)}, u32[]{:S(2)}) collective-permute-start(bf16[32,1152]{1,0:T(8,128)(2,1)S(1)} %get-tuple-element.28), channel_id=1, source_target_pairs={{0,5},{1,4},{2,7},{3,6},{4,1},{5,0},{6,3},{7,2},{8,13},{9,12},{10,... | collective-permute-start | bytes 221192 | tf_op jit(solution)/shard_map/ppermute | solution.py:50
  10.9 0.8 %collective-permute-done.1 = bf16[32,1152]{1,0:T(8,128)(2,1)S(1)} collective-permute-done((bf16[32,1152]{1,0:T(8,128)(2,1)S(1)}, bf16[32,1152]{1,0:T(8,128)(2,1)S(1)}, u32[]{:S(2)}, u32[]{:S(2)}) %collective-permute-start.1) | collective-permute-done | bytes 73760 | tf_op jit(solution)/shard_map/ppermute | solution.py:50
  11.7 1.9 %collective-permute-done.2 = bf16[32,1152]{1,0:T(8,128)(2,1)S(1)} collective-permute-done((bf16[32,1152]{1,0:T(8,128)(2,1)S(1)}, bf16[32,1152]{1,0:T(8,128)(2,1)S(1)}, u32[]{:S(2)}, u32[]{:S(2)}) %collective-permute-start.2) | collective-permute-done | bytes 73760 | tf_op jit(solution)/shard_map/ppermute | solution.py:50
  13.6 2.5 %collective-permute-done.3 = bf16[32,1152]{1,0:T(8,128)(2,1)S(1)} collective-permute-done((bf16[32,1152]{1,0:T(8,128)(2,1)S(1)}, bf16[32,1152]{1,0:T(8,128)(2,1)S(1)}, u32[]{:S(2)}, u32[]{:S(2)}) %collective-permute-start.3) | collective-permute-done | bytes 73760 | tf_op jit(solution)/shard_map/ppermute | solution.py:50
  16.1 0.2 collective-permute-start.4
  17.0 1.6 %load.1 = (bf16[1024,1024]{1,0:T(8,128)(2,1)S(1)}, f32[1,1024]{1,0:T(1,128)S(1)}) custom-call(bf16[1024,1024]{1,0:T(8,128)(2,1)} %src_hbm.1, f32[1,1024]{1,0:T(1,128)} %bitcast.6), custom_call_target="tpu_custom_call" | custom-call | bytes 4194304 | tf_op jit(solution)/shard_map/load/pallas_call | solution.py:309
  18.6 1.1 %near.1 = (f32[128,1024]{1,0:T(8,128)S(1)}, f32[1,1024]{1,0:T(1,128)S(1)}, f32[1,1024]{1,0:T(1,128)S(1)}, f32[1,128]{1,0:T(1,128)S(1)}) custom-call(bf16[128,1152]{1,0:T(8,128)(2,1)S(1)} %constant_dynamic-update-slice_fusion.2.near_ref, bf16[1024,1024]{1,0:T(8,128)(2,1)S(1)} %get-tuple-element.17.src_ref, f32[1,1024]{1,0:T(1,128)S(1)} %get-tuple-element.18.src_scale_ref, ...), custom_call_target="tpu_custom_call" | custom-call | flops 268435456 | bytes 524288 | tf_op jit(solution)/shard_map/near/pallas_call | solution.py:316
  19.7 1.3 %far.1 = (f32[128,1024]{1,0:T(8,128)S(1)}, f32[1,1024]{1,0:T(1,128)S(1)}, f32[4,128]{1,0:T(4,128)S(1)}) custom-call(bf16[128,1152]{1,0:T(8,128)(2,1)S(1)} %collective-permute-done.4.far_ref, bf16[1024,1024]{1,0:T(8,128)(2,1)S(1)} %get-tuple-element.17.src_ref, f32[1,1024]{1,0:T(1,128)S(1)} %get-tuple-element.18.src_scale_ref, ...), custom_call_target="tpu_custom_call" | custom-call | tf_op jit(solution)/shard_map/far/pallas_call | solution.py:328
  21.0 0.4 %collective-permute-start.5 = (f32[4,128]{1,0:T(4,128)S(1)}, f32[4,128]{1,0:T(4,128)S(1)}, u32[]{:S(2)}, u32[]{:S(2)}) collective-permute-start(f32[4,128]{1,0:T(4,128)S(1)} %get-tuple-element.23), channel_id=1, source_target_pairs={{0,1},{1,0},{2,3},{3,2},{4,5},{5,4},{6,7},{7,6},{8,9},{9,8},{10,11... | collective-permute-start | bytes 6152 | tf_op jit(solution)/shard_map/ppermute | solution.py:50
  21.4 0.8 %collective-permute-done.5 = f32[4,128]{1,0:T(4,128)S(1)} collective-permute-done((f32[4,128]{1,0:T(4,128)S(1)}, f32[4,128]{1,0:T(4,128)S(1)}, u32[]{:S(2)}, u32[]{:S(2)}) %collective-permute-start.5) | collective-permute-done | bytes 2080 | tf_op jit(solution)/shard_map/ppermute | solution.py:50
  22.3 3.5 %collective-permute-start.6 = (f32[4,128]{1,0:T(4,128)S(1)}, f32[4,128]{1,0:T(4,128)S(1)}, u32[]{:S(2)}, u32[]{:S(2)}) collective-permute-start(f32[4,128]{1,0:T(4,128)S(1)} %add_select_fusion.2), channel_id=1, source_target_pairs={{0,9},{1,8},{2,11},{3,10},{4,13},{5,12},{6,15},{7,14},{8,1},{9,0},... | collective-permute-start | bytes 6152 | tf_op jit(solution)/shard_map/ppermute | solution.py:50
  25.7 1.3 %collective-permute-done.6 = f32[4,128]{1,0:T(4,128)S(1)} collective-permute-done((f32[4,128]{1,0:T(4,128)S(1)}, f32[4,128]{1,0:T(4,128)S(1)}, u32[]{:S(2)}, u32[]{:S(2)}) %collective-permute-start.6) | collective-permute-done | bytes 2080 | tf_op jit(solution)/shard_map/ppermute | solution.py:50
  27.1 1.3 %collective-permute-start.9 = (f32[4,128]{1,0:T(4,128)S(1)}, f32[4,128]{1,0:T(4,128)S(1)}, u32[]{:S(2)}, u32[]{:S(2)}) collective-permute-start(f32[4,128]{1,0:T(4,128)S(1)} %add_select_fusion.1), channel_id=1, source_target_pairs={{0,7},{1,6},{2,5},{3,4},{4,3},{5,2},{6,1},{7,0},{8,15},{9,14},{10,... | collective-permute-start | bytes 6152 | tf_op jit(solution)/shard_map/ppermute | solution.py:50
  28.4 0.4 %collective-permute-start.8 = (f32[4,128]{1,0:T(4,128)S(1)}, f32[4,128]{1,0:T(4,128)S(1)}, u32[]{:S(2)}, u32[]{:S(2)}) collective-permute-start(f32[4,128]{1,0:T(4,128)S(1)} %add_select_fusion.1), channel_id=1, source_target_pairs={{0,5},{1,4},{2,7},{3,6},{4,1},{5,0},{6,3},{7,2},{8,13},{9,12},{10,... | collective-permute-start | bytes 6152 | tf_op jit(solution)/shard_map/ppermute | solution.py:50
  28.8 1.3 %collective-permute-start.7 = (f32[4,128]{1,0:T(4,128)S(1)}, f32[4,128]{1,0:T(4,128)S(1)}, u32[]{:S(2)}, u32[]{:S(2)}) collective-permute-start(f32[4,128]{1,0:T(4,128)S(1)} %add_select_fusion.1), channel_id=1, source_target_pairs={{0,3},{1,2},{2,1},{3,0},{4,7},{5,6},{6,5},{7,4},{8,11},{9,10},{10,... | collective-permute-start | bytes 6152 | tf_op jit(solution)/shard_map/ppermute | solution.py:50
  30.1 0.9 %collective-permute-done.9 = f32[4,128]{1,0:T(4,128)S(1)} collective-permute-done((f32[4,128]{1,0:T(4,128)S(1)}, f32[4,128]{1,0:T(4,128)S(1)}, u32[]{:S(2)}, u32[]{:S(2)}) %collective-permute-start.9) | collective-permute-done | bytes 2080 | tf_op jit(solution)/shard_map/ppermute | solution.py:50
  31.0 0.4 %collective-permute-done.8 = f32[4,128]{1,0:T(4,128)S(1)} collective-permute-done((f32[4,128]{1,0:T(4,128)S(1)}, f32[4,128]{1,0:T(4,128)S(1)}, u32[]{:S(2)}, u32[]{:S(2)}) %collective-permute-start.8) | collective-permute-done | bytes 2080 | tf_op jit(solution)/shard_map/ppermute | solution.py:50
  31.4 0.4 %collective-permute-done.7 = f32[4,128]{1,0:T(4,128)S(1)} collective-permute-done((f32[4,128]{1,0:T(4,128)S(1)}, f32[4,128]{1,0:T(4,128)S(1)}, u32[]{:S(2)}, u32[]{:S(2)}) %collective-permute-start.7) | collective-permute-done | bytes 2080 | tf_op jit(solution)/shard_map/ppermute | solution.py:50
  31.8 0.1 add_select_fusion.stats_ref
  31.9 0.9 %finish.1 = (f32[1,1024]{1,0:T(1,128)}, f32[1,16]{1,0:T(1,128)}) custom-call(f32[1,1024]{1,0:T(1,128)S(1)} %compare_select_fusion.src_live_ref, f32[1,16]{1,0:T(1,128)S(1)} %get-tuple-element.15.own_live_ref, f32[4,128]{1,0:T(4,128)S(1)} %add_select_fusion.stats_ref, f32[128,1024]{1,0:T(8,128)S(1)} %get-tuple-element.19.near_scores_ref.near_ref, ...), custom_call_target="tpu_custom_call" | custom-call | tf_op jit(solution)/shard_map/finish/pallas_call | solution.py:344
  (11 shorter events, 0.2 us)
Async XLA Ops:
  2.1 5.4 %collective-permute-start = (bf16[16,1152]{1,0:T(8,128)(2,1)S(1)}, bf16[16,1152]{1,0:T(8,128)(2,1)S(1)}, u32[]{:S(2)}, u32[]{:S(2)}) collective-permute-start(bf16[16,1152]{1,0:T(8,128)(2,1)S(1)} %get-tuple-element.16), channel_id=1, source_target_pairs={{0,9},{1,8},{2,11},{3,10},{4,13},{5,12},{6,15},{7,14},{8,1},{9,0},... | collective-permute-start | bytes 110600 | tf_op jit(solution)/shard_map/ppermute | solution.py:50
  7.5 4.2 %collective-permute-start.1 = (bf16[32,1152]{1,0:T(8,128)(2,1)S(1)}, bf16[32,1152]{1,0:T(8,128)(2,1)S(1)}, u32[]{:S(2)}, u32[]{:S(2)}) collective-permute-start(bf16[32,1152]{1,0:T(8,128)(2,1)S(1)} %get-tuple-element.28), channel_id=1, source_target_pairs={{0,3},{1,2},{2,1},{3,0},{4,7},{5,6},{6,5},{7,4},{8,11},{9,10},{10,... | collective-permute-start | bytes 221192 | tf_op jit(solution)/shard_map/ppermute | solution.py:50
  9.4 4.2 %collective-permute-start.2 = (bf16[32,1152]{1,0:T(8,128)(2,1)S(1)}, bf16[32,1152]{1,0:T(8,128)(2,1)S(1)}, u32[]{:S(2)}, u32[]{:S(2)}) collective-permute-start(bf16[32,1152]{1,0:T(8,128)(2,1)S(1)} %get-tuple-element.28), channel_id=1, source_target_pairs={{0,5},{1,4},{2,7},{3,6},{4,1},{5,0},{6,3},{7,2},{8,13},{9,12},{10,... | collective-permute-start | bytes 221192 | tf_op jit(solution)/shard_map/ppermute | solution.py:50
  10.9 5.2 %collective-permute-start.3 = (bf16[32,1152]{1,0:T(8,128)(2,1)S(1)}, bf16[32,1152]{1,0:T(8,128)(2,1)S(1)}, u32[]{:S(2)}, u32[]{:S(2)}) collective-permute-start(bf16[32,1152]{1,0:T(8,128)(2,1)S(1)} %get-tuple-element.28), channel_id=1, source_target_pairs={{0,7},{1,6},{2,5},{3,4},{4,3},{5,2},{6,1},{7,0},{8,15},{9,14},{10,... | collective-permute-start | bytes 221192 | tf_op jit(solution)/shard_map/ppermute | solution.py:50
  16.1 3.6 %collective-permute-start.4 = (bf16[128,1152]{1,0:T(8,128)(2,1)S(1)}, bf16[128,1152]{1,0:T(8,128)(2,1)S(1)}, u32[]{:S(2)}, u32[]{:S(2)}) collective-permute-start(bf16[128,1152]{1,0:T(8,128)(2,1)S(1)} %constant_dynamic-update-slice_fusion.2.near_ref), channel_id=1, source_target_pairs={{0,1},{1,0},{2,3},{3,2},{4,5},{5,4},{6,7},{7,6},{8,9},{9,8},{10,11... | collective-permute-start | bytes 884744 | tf_op jit(solution)/shard_map/ppermute | solution.py:50
  21.0 1.2 %collective-permute-start.5 = (f32[4,128]{1,0:T(4,128)S(1)}, f32[4,128]{1,0:T(4,128)S(1)}, u32[]{:S(2)}, u32[]{:S(2)}) collective-permute-start(f32[4,128]{1,0:T(4,128)S(1)} %get-tuple-element.23), channel_id=1, source_target_pairs={{0,1},{1,0},{2,3},{3,2},{4,5},{5,4},{6,7},{7,6},{8,9},{9,8},{10,11... | collective-permute-start | bytes 6152 | tf_op jit(solution)/shard_map/ppermute | solution.py:50
  22.3 4.8 %collective-permute-start.6 = (f32[4,128]{1,0:T(4,128)S(1)}, f32[4,128]{1,0:T(4,128)S(1)}, u32[]{:S(2)}, u32[]{:S(2)}) collective-permute-start(f32[4,128]{1,0:T(4,128)S(1)} %add_select_fusion.2), channel_id=1, source_target_pairs={{0,9},{1,8},{2,11},{3,10},{4,13},{5,12},{6,15},{7,14},{8,1},{9,0},... | collective-permute-start | bytes 6152 | tf_op jit(solution)/shard_map/ppermute | solution.py:50
  27.1 3.9 %collective-permute-start.9 = (f32[4,128]{1,0:T(4,128)S(1)}, f32[4,128]{1,0:T(4,128)S(1)}, u32[]{:S(2)}, u32[]{:S(2)}) collective-permute-start(f32[4,128]{1,0:T(4,128)S(1)} %add_select_fusion.1), channel_id=1, source_target_pairs={{0,7},{1,6},{2,5},{3,4},{4,3},{5,2},{6,1},{7,0},{8,15},{9,14},{10,... | collective-permute-start | bytes 6152 | tf_op jit(solution)/shard_map/ppermute | solution.py:50
  28.4 3.0 %collective-permute-start.8 = (f32[4,128]{1,0:T(4,128)S(1)}, f32[4,128]{1,0:T(4,128)S(1)}, u32[]{:S(2)}, u32[]{:S(2)}) collective-permute-start(f32[4,128]{1,0:T(4,128)S(1)} %add_select_fusion.1), channel_id=1, source_target_pairs={{0,5},{1,4},{2,7},{3,6},{4,1},{5,0},{6,3},{7,2},{8,13},{9,12},{10,... | collective-permute-start | bytes 6152 | tf_op jit(solution)/shard_map/ppermute | solution.py:50
  28.8 3.0 %collective-permute-start.7 = (f32[4,128]{1,0:T(4,128)S(1)}, f32[4,128]{1,0:T(4,128)S(1)}, u32[]{:S(2)}, u32[]{:S(2)}) collective-permute-start(f32[4,128]{1,0:T(4,128)S(1)} %add_select_fusion.1), channel_id=1, source_target_pairs={{0,3},{1,2},{2,1},{3,0},{4,7},{5,6},{6,5},{7,4},{8,11},{9,10},{10,... | collective-permute-start | bytes 6152 | tf_op jit(solution)/shard_map/ppermute | solution.py:50

commit v5 on v4

--- a/solution.py
+++ b/solution.py
@@ -106,7 +106,7 @@
 
 
 def column_block(sources):
-    return 2 * LANES if sources % (2 * LANES) == 0 else LANES
+    return 4 * LANES if sources % (4 * LANES) == 0 else LANES
 
 
 def fold(values, op):
@@ -246,11 +246,20 @@
 
 def finish_kernel(
     phases, tgt_dev, src_live_ref, own_live_ref, stats_ref, near_ref, far_ref, row_den_ref,
-    best_source_ref, best_target_ref,
+    best_source_hbm, best_target_hbm, source_sc, target_sc, sems,
 ):
     me = lax.axis_index("blk")
     sources = near_ref.shape[1]
     count = near_ref.shape[0] // LANES
+    core, first = me & 1, own_slot(phases, me) * tgt_dev
+    row = core * count + first // LANES
+    best = stats_ref[pl.ds(2 * count + row, 1), :] - 0.5 * stats_ref[pl.ds(row, 1), :]
+    lane = lax.broadcasted_iota(jnp.int32, (tgt_dev, LANES), 1)
+    wanted = lax.broadcasted_iota(jnp.int32, (tgt_dev, LANES), 0) + (first & (LANES - 1))
+    own = jnp.sum(jnp.where(lane == wanted, best * LN_2, 0.0), axis=1, keepdims=True)
+    target_sc[...] = jnp.where(own_live_ref[...] > 0.5, column_to_row(own, diagonal(tgt_dev)), 0.0)
+    target_copy = pltpu.make_async_copy(target_sc, best_target_hbm, sems.at[0])
+    target_copy.start()
     eye = diagonal(LANES)
     row_best = jnp.full((1, sources), NEG_BIG, jnp.float32)
     for row in range(count):
@@ -264,14 +273,11 @@
         ):
             margin = ref[pl.ds(row * LANES, LANES), :] - row_to_column(values, eye)
             row_best = jnp.maximum(row_best, jnp.max(margin, axis=0, keepdims=True))
-    best_source_ref[...] = jnp.where(src_live_ref[...] > 0.5, (row_best - 0.5 * row_den_ref[...]) * LN_2, 0.0)
-    core, first = me & 1, own_slot(phases, me) * tgt_dev
-    row = core * count + first // LANES
-    best = stats_ref[pl.ds(2 * count + row, 1), :] - 0.5 * stats_ref[pl.ds(row, 1), :]
-    lane = lax.broadcasted_iota(jnp.int32, (tgt_dev, LANES), 1)
-    wanted = lax.broadcasted_iota(jnp.int32, (tgt_dev, LANES), 0) + (first & (LANES - 1))
-    own = jnp.sum(jnp.where(lane == wanted, best * LN_2, 0.0), axis=1, keepdims=True)
-    best_target_ref[...] = jnp.where(own_live_ref[...] > 0.5, column_to_row(own, diagonal(tgt_dev)), 0.0)
+    source_sc[...] = jnp.where(src_live_ref[...] > 0.5, (row_best - 0.5 * row_den_ref[...]) * LN_2, 0.0)
+    source_copy = pltpu.make_async_copy(source_sc, best_source_hbm, sems.at[1])
+    source_copy.start()
+    target_copy.wait()
+    source_copy.wait()
 
 
 def mine(src_emb, src_scale, src_count, tgt_emb, tgt_scale, tgt_count):
@@ -310,8 +316,13 @@
     sources_live = jnp.where(lax.broadcasted_iota(jnp.int32, (1, src_dev), 1) < src_count, 1.0, 0.0)
     for bits in phases:
         came = [exchange(near, ranks, mask) for mask in phase_masks(bits)]
-        near = jnp.concatenate([near] + came, axis=0)
-    far = exchange(near, ranks, 1)
+        held, near = near, jnp.concatenate([near] + came, axis=0)
+    early = exchange(jnp.concatenate([held, came[-1]], axis=0), ranks, 1)
+    if len(came) > 1:
+        late = exchange(jnp.concatenate(came[:-1], axis=0), ranks, 1)
+        far = jnp.concatenate([early[: held.shape[0]], late, early[held.shape[0] :]], axis=0)
+    else:
+        far = early
     half_lanes = pltpu.VMEM((half, LANES), jnp.float32)
     near_scores, near_max, near_sum, near_logs = pl.pallas_call(
         near_kernel,
@@ -344,11 +355,16 @@
     best_source, best_target = pl.pallas_call(
         functools.partial(finish_kernel, phases, tgt_dev),
         out_shape=(
-            jax.ShapeDtypeStruct((1, src_dev), jnp.float32),
-            jax.ShapeDtypeStruct((1, tgt_dev), jnp.float32),
+            pltpu.HBM((1, src_dev), jnp.float32),
+            pltpu.HBM((1, tgt_dev), jnp.float32),
         ),
         in_specs=[VMEM] * 6,
-        out_specs=(VMEM, VMEM),
+        out_specs=(HBM, HBM),
+        scratch_shapes=[
+            pltpu.VMEM((1, src_dev), jnp.float32),
+            pltpu.VMEM((1, tgt_dev), jnp.float32),
+            pltpu.SemaphoreType.DMA((2,)),
+        ],
         compiler_params=params,
         name="finish",
     )(

time: 33 us -> 30.4 us (0.921)
  waiting for transfers between devices: 10.9 us -> 8.42 us
    ppermute x10 -> x11, waiting for transfers between devices: 10.9 us -> 8.42 us  [exchange(): return lax.ppermute(block, 'blk', [(i, i ^ mask) for i in range(ranks)])]
    ppermute x10 -> x11, starting transfers between devices: 14 us -> 13.9 us  [exchange(): return lax.ppermute(block, 'blk', [(i, i ^ mask) for i in range(ranks)])]
  transfers between devices with their start and end apart: 10 -> 11, of which waited for: 9 -> 7; matrix products, arithmetic and copies ran while one was open for 0% -> 0% of each run, Pallas kernels for 8% -> 9%
where the time goes in v5:
time: 30.4 us; the launch traced here: 30.1 us
  starting transfers between devices  13.9 us (46%)
  waiting for transfers between devices  8.42 us (28%)
  Pallas kernels  5.51 us (18%)
  between operations  2.02 us (7%)
    ppermute x11, starting transfers between devices, exchange(): return lax.ppermute(block, 'blk', [(i, i ^ mask) for i in range(ranks)])  13.9 us
    ppermute x11, waiting for transfers between devices, exchange(): return lax.ppermute(block, 'blk', [(i, i ^ mask) for i in range(ranks)])  8.42 us
    pallas_call x1, Pallas kernels, mine(): load(in_hbm(src_emb), in_hbm(src_scale.reshape(1, src_dev)))  1.61 us
    pallas_call x1, Pallas kernels, mine(): pl.pallas_call(functools.partial(far_kernel, phases, tgt_dev), out_shape=...  1.18 us
    pallas_call x1, Pallas kernels, mine(): pl.pallas_call(near_kernel, out_shape=(half_shape, source_line, source_li...  1.05 us
    pallas_call x1, Pallas kernels, mine(): pl.pallas_call(functools.partial(finish_kernel, phases, tgt_dev), out_sha...  0.88 us
    pallas_call x1, Pallas kernels, mine(): pl.pallas_call(pack_kernel, out_shape=(pltpu.VMEM((tgt_dev, width), jnp.b...  0.79 us
  transfers between devices with their start and end apart: 11, of which 7 were waited for; matrix products, arithmetic and copies ran while one was open for 0% of the time, Pallas kernels for 9%

profile of v5, /device:TPU:0, one launch (start us, length us, event | category | flops | bytes accessed | tf_op | source)
XLA Modules:
  0.0 30.1 jit_solution(8636035197551695146)
XLA Ops:
  1.3 0.8 %pack.1 = (bf16[16,1152]{1,0:T(8,128)(2,1)S(1)}, f32[1,16]{1,0:T(1,128)S(1)}) custom-call(s32[1]{0:T(128)S(6)} %copy.14.count_ref, bf16[16,1024]{1,0:T(8,128)(2,1)} %tgt_hbm.1, f32[1,16]{1,0:T(1,128)} %bitcast.7), custom_call_target="tpu_custom_call" | custom-call | tf_op jit(solution)/shard_map/pack/pallas_call | solution.py:293
  2.1 3.6 %collective-permute-start = (bf16[16,1152]{1,0:T(8,128)(2,1)S(1)}, bf16[16,1152]{1,0:T(8,128)(2,1)S(1)}, u32[]{:S(2)}, u32[]{:S(2)}) collective-permute-start(bf16[16,1152]{1,0:T(8,128)(2,1)S(1)} %get-tuple-element.16), channel_id=1, source_target_pairs={{0,9},{1,8},{2,11},{3,10},{4,13},{5,12},{6,15},{7,14},{8,1},{9,0},... | collective-permute-start | bytes 110600 | tf_op jit(solution)/shard_map/ppermute | solution.py:50
  6.3 1.6 %load.1 = (bf16[1024,1024]{1,0:T(8,128)(2,1)S(1)}, f32[1,1024]{1,0:T(1,128)S(1)}) custom-call(bf16[1024,1024]{1,0:T(8,128)(2,1)} %src_hbm.1, f32[1,1024]{1,0:T(1,128)} %bitcast.6), custom_call_target="tpu_custom_call" | custom-call | bytes 4194304 | tf_op jit(solution)/shard_map/load/pallas_call | solution.py:315
  8.0 2.9 %collective-permute-start.1 = (bf16[32,1152]{1,0:T(8,128)(2,1)S(1)}, bf16[32,1152]{1,0:T(8,128)(2,1)S(1)}, u32[]{:S(2)}, u32[]{:S(2)}) collective-permute-start(bf16[32,1152]{1,0:T(8,128)(2,1)S(1)} %get-tuple-element.31), channel_id=1, source_target_pairs={{0,7},{1,6},{2,5},{3,4},{4,3},{5,2},{6,1},{7,0},{8,15},{9,14},{10,... | collective-permute-start | bytes 221192 | tf_op jit(solution)/shard_map/ppermute | solution.py:50
  10.8 0.7 %collective-permute-start.3 = (bf16[32,1152]{1,0:T(8,128)(2,1)S(1)}, bf16[32,1152]{1,0:T(8,128)(2,1)S(1)}, u32[]{:S(2)}, u32[]{:S(2)}) collective-permute-start(bf16[32,1152]{1,0:T(8,128)(2,1)S(1)} %get-tuple-element.31), channel_id=1, source_target_pairs={{0,3},{1,2},{2,1},{3,0},{4,7},{5,6},{6,5},{7,4},{8,11},{9,10},{10,... | collective-permute-start | bytes 221192 | tf_op jit(solution)/shard_map/ppermute | solution.py:50
  11.5 2.0 %collective-permute-done.1 = bf16[32,1152]{1,0:T(8,128)(2,1)S(1)} collective-permute-done((bf16[32,1152]{1,0:T(8,128)(2,1)S(1)}, bf16[32,1152]{1,0:T(8,128)(2,1)S(1)}, u32[]{:S(2)}, u32[]{:S(2)}) %collective-permute-start.1) | collective-permute-done | bytes 73760 | tf_op jit(solution)/shard_map/ppermute | solution.py:50
  13.5 0.1 collective-permute-start.2
  13.6 1.7 %collective-permute-done.4 = bf16[32,1152]{1,0:T(8,128)(2,1)S(1)} collective-permute-done((bf16[32,1152]{1,0:T(8,128)(2,1)S(1)}, bf16[32,1152]{1,0:T(8,128)(2,1)S(1)}, u32[]{:S(2)}, u32[]{:S(2)}) %collective-permute-start.4) | collective-permute-done | bytes 73760 | tf_op jit(solution)/shard_map/ppermute | solution.py:50
  15.3 0.2 collective-permute-start.5
  15.5 1.0 %near.1 = (f32[128,1024]{1,0:T(8,128)S(1)}, f32[1,1024]{1,0:T(1,128)S(1)}, f32[1,1024]{1,0:T(1,128)S(1)}, f32[1,128]{1,0:T(1,128)S(1)}) custom-call(bf16[128,1152]{1,0:T(8,128)(2,1)S(1)} %constant_dynamic-update-slice_fusion.2.near_ref, bf16[1024,1024]{1,0:T(8,128)(2,1)S(1)} %get-tuple-element.17.src_ref, f32[1,1024]{1,0:T(1,128)S(1)} %get-tuple-element.18.src_scale_ref, ...), custom_call_target="tpu_custom_call" | custom-call | flops 268435456 | bytes 524288 | tf_op jit(solution)/shard_map/near/pallas_call | solution.py:327
  16.6 0.1 collective-permute-done.5
  16.8 1.2 %far.1 = (f32[128,1024]{1,0:T(8,128)S(1)}, f32[1,1024]{1,0:T(1,128)S(1)}, f32[4,128]{1,0:T(4,128)S(1)}) custom-call(bf16[128,1152]{1,0:T(8,128)(2,1)S(1)} %pad_maximum_fusion.far_ref, bf16[1024,1024]{1,0:T(8,128)(2,1)S(1)} %get-tuple-element.17.src_ref, f32[1,1024]{1,0:T(1,128)S(1)} %get-tuple-element.18.src_scale_ref, ...), custom_call_target="tpu_custom_call" | custom-call | tf_op jit(solution)/shard_map/far/pallas_call | solution.py:339
  17.9 0.3 collective-permute-start.6
  18.2 0.9 %collective-permute-done.6 = f32[4,128]{1,0:T(4,128)S(1)} collective-permute-done((f32[4,128]{1,0:T(4,128)S(1)}, f32[4,128]{1,0:T(4,128)S(1)}, u32[]{:S(2)}, u32[]{:S(2)}) %collective-permute-start.6) | collective-permute-done | bytes 2080 | tf_op jit(solution)/shard_map/ppermute | solution.py:50
  19.1 0.1 add_select_fusion.2
  19.2 2.7 %collective-permute-start.7 = (f32[4,128]{1,0:T(4,128)S(1)}, f32[4,128]{1,0:T(4,128)S(1)}, u32[]{:S(2)}, u32[]{:S(2)}) collective-permute-start(f32[4,128]{1,0:T(4,128)S(1)} %add_select_fusion.2), channel_id=1, source_target_pairs={{0,9},{1,8},{2,11},{3,10},{4,13},{5,12},{6,15},{7,14},{8,1},{9,0},... | collective-permute-start | bytes 6152 | tf_op jit(solution)/shard_map/ppermute | solution.py:50
  21.9 1.3 %collective-permute-done.7 = f32[4,128]{1,0:T(4,128)S(1)} collective-permute-done((f32[4,128]{1,0:T(4,128)S(1)}, f32[4,128]{1,0:T(4,128)S(1)}, u32[]{:S(2)}, u32[]{:S(2)}) %collective-permute-start.7) | collective-permute-done | bytes 2080 | tf_op jit(solution)/shard_map/ppermute | solution.py:50
  23.2 0.1 add_select_fusion.1
  23.2 2.9 %collective-permute-start.10 = (f32[4,128]{1,0:T(4,128)S(1)}, f32[4,128]{1,0:T(4,128)S(1)}, u32[]{:S(2)}, u32[]{:S(2)}) collective-permute-start(f32[4,128]{1,0:T(4,128)S(1)} %add_select_fusion.1), channel_id=1, source_target_pairs={{0,7},{1,6},{2,5},{3,4},{4,3},{5,2},{6,1},{7,0},{8,15},{9,14},{10,... | collective-permute-start | bytes 6152 | tf_op jit(solution)/shard_map/ppermute | solution.py:50
  26.2 0.6 %collective-permute-start.8 = (f32[4,128]{1,0:T(4,128)S(1)}, f32[4,128]{1,0:T(4,128)S(1)}, u32[]{:S(2)}, u32[]{:S(2)}) collective-permute-start(f32[4,128]{1,0:T(4,128)S(1)} %add_select_fusion.1), channel_id=1, source_target_pairs={{0,3},{1,2},{2,1},{3,0},{4,7},{5,6},{6,5},{7,4},{8,11},{9,10},{10,... | collective-permute-start | bytes 6152 | tf_op jit(solution)/shard_map/ppermute | solution.py:50
  26.7 0.7 %collective-permute-done.10 = f32[4,128]{1,0:T(4,128)S(1)} collective-permute-done((f32[4,128]{1,0:T(4,128)S(1)}, f32[4,128]{1,0:T(4,128)S(1)}, u32[]{:S(2)}, u32[]{:S(2)}) %collective-permute-start.10) | collective-permute-done | bytes 2080 | tf_op jit(solution)/shard_map/ppermute | solution.py:50
  27.5 1.7 %collective-permute-done.9 = f32[4,128]{1,0:T(4,128)S(1)} collective-permute-done((f32[4,128]{1,0:T(4,128)S(1)}, f32[4,128]{1,0:T(4,128)S(1)}, u32[]{:S(2)}, u32[]{:S(2)}) %collective-permute-start.9) | collective-permute-done | bytes 2080 | tf_op jit(solution)/shard_map/ppermute | solution.py:50
  29.2 0.1 add_select_fusion.stats_ref
  29.3 0.9 %finish.1 = (f32[1,1024]{1,0:T(1,128)}, f32[1,16]{1,0:T(1,128)}) custom-call(f32[1,1024]{1,0:T(1,128)S(1)} %compare_select_fusion.src_live_ref, f32[1,16]{1,0:T(1,128)S(1)} %get-tuple-element.15.own_live_ref, f32[4,128]{1,0:T(4,128)S(1)} %add_select_fusion.stats_ref, f32[128,1024]{1,0:T(8,128)S(1)} %get-tuple-element.19.near_scores_ref.near_ref, ...), custom_call_target="tpu_custom_call" | custom-call | tf_op jit(solution)/shard_map/finish/pallas_call | solution.py:355
  (17 shorter events, 0.2 us)
Async XLA Ops:
  2.1 5.9 %collective-permute-start = (bf16[16,1152]{1,0:T(8,128)(2,1)S(1)}, bf16[16,1152]{1,0:T(8,128)(2,1)S(1)}, u32[]{:S(2)}, u32[]{:S(2)}) collective-permute-start(bf16[16,1152]{1,0:T(8,128)(2,1)S(1)} %get-tuple-element.16), channel_id=1, source_target_pairs={{0,9},{1,8},{2,11},{3,10},{4,13},{5,12},{6,15},{7,14},{8,1},{9,0},... | collective-permute-start | bytes 110600 | tf_op jit(solution)/shard_map/ppermute | solution.py:50
  8.0 5.5 %collective-permute-start.1 = (bf16[32,1152]{1,0:T(8,128)(2,1)S(1)}, bf16[32,1152]{1,0:T(8,128)(2,1)S(1)}, u32[]{:S(2)}, u32[]{:S(2)}) collective-permute-start(bf16[32,1152]{1,0:T(8,128)(2,1)S(1)} %get-tuple-element.31), channel_id=1, source_target_pairs={{0,7},{1,6},{2,5},{3,4},{4,3},{5,2},{6,1},{7,0},{8,15},{9,14},{10,... | collective-permute-start | bytes 221192 | tf_op jit(solution)/shard_map/ppermute | solution.py:50
  10.8 4.4 %collective-permute-start.4 = (bf16[32,1152]{1,0:T(8,128)(2,1)S(1)}, bf16[32,1152]{1,0:T(8,128)(2,1)S(1)}, u32[]{:S(2)}, u32[]{:S(2)}) collective-permute-start(bf16[32,1152]{1,0:T(8,128)(2,1)S(1)} %get-tuple-element.31), channel_id=1, source_target_pairs={{0,5},{1,4},{2,7},{3,6},{4,1},{5,0},{6,3},{7,2},{8,13},{9,12},{10,... | collective-permute-start | bytes 221192 | tf_op jit(solution)/shard_map/ppermute | solution.py:50
  10.8 4.4 %collective-permute-start.3 = (bf16[32,1152]{1,0:T(8,128)(2,1)S(1)}, bf16[32,1152]{1,0:T(8,128)(2,1)S(1)}, u32[]{:S(2)}, u32[]{:S(2)}) collective-permute-start(bf16[32,1152]{1,0:T(8,128)(2,1)S(1)} %get-tuple-element.31), channel_id=1, source_target_pairs={{0,3},{1,2},{2,1},{3,0},{4,7},{5,6},{6,5},{7,4},{8,11},{9,10},{10,... | collective-permute-start | bytes 221192 | tf_op jit(solution)/shard_map/ppermute | solution.py:50
  13.5 3.1 %collective-permute-start.2 = (bf16[64,1152]{1,0:T(8,128)(2,1)S(1)}, bf16[64,1152]{1,0:T(8,128)(2,1)S(1)}, u32[]{:S(2)}, u32[]{:S(2)}) collective-permute-start(bf16[64,1152]{1,0:T(8,128)(2,1)S(1)} %pad_maximum_fusion.1), channel_id=1, source_target_pairs={{0,1},{1,0},{2,3},{3,2},{4,5},{5,4},{6,7},{7,6},{8,9},{9,8},{10,11... | collective-permute-start | bytes 442376 | tf_op jit(solution)/shard_map/ppermute | solution.py:50
  15.3 1.4 %collective-permute-start.5 = (bf16[64,1152]{1,0:T(8,128)(2,1)S(1)}, bf16[64,1152]{1,0:T(8,128)(2,1)S(1)}, u32[]{:S(2)}, u32[]{:S(2)}) collective-permute-start(bf16[64,1152]{1,0:T(8,128)(2,1)S(1)} %pad_maximum_fusion.2), channel_id=1, source_target_pairs={{0,1},{1,0},{2,3},{3,2},{4,5},{5,4},{6,7},{7,6},{8,9},{9,8},{10,11... | collective-permute-start | bytes 442376 | tf_op jit(solution)/shard_map/ppermute | solution.py:50
  17.9 1.2 %collective-permute-start.6 = (f32[4,128]{1,0:T(4,128)S(1)}, f32[4,128]{1,0:T(4,128)S(1)}, u32[]{:S(2)}, u32[]{:S(2)}) collective-permute-start(f32[4,128]{1,0:T(4,128)S(1)} %get-tuple-element.23), channel_id=1, source_target_pairs={{0,1},{1,0},{2,3},{3,2},{4,5},{5,4},{6,7},{7,6},{8,9},{9,8},{10,11... | collective-permute-start | bytes 6152 | tf_op jit(solution)/shard_map/ppermute | solution.py:50
  19.2 4.0 %collective-permute-start.7 = (f32[4,128]{1,0:T(4,128)S(1)}, f32[4,128]{1,0:T(4,128)S(1)}, u32[]{:S(2)}, u32[]{:S(2)}) collective-permute-start(f32[4,128]{1,0:T(4,128)S(1)} %add_select_fusion.2), channel_id=1, source_target_pairs={{0,9},{1,8},{2,11},{3,10},{4,13},{5,12},{6,15},{7,14},{8,1},{9,0},... | collective-permute-start | bytes 6152 | tf_op jit(solution)/shard_map/ppermute | solution.py:50
  23.2 4.2 %collective-permute-start.10 = (f32[4,128]{1,0:T(4,128)S(1)}, f32[4,128]{1,0:T(4,128)S(1)}, u32[]{:S(2)}, u32[]{:S(2)}) collective-permute-start(f32[4,128]{1,0:T(4,128)S(1)} %add_select_fusion.1), channel_id=1, source_target_pairs={{0,7},{1,6},{2,5},{3,4},{4,3},{5,2},{6,1},{7,0},{8,15},{9,14},{10,... | collective-permute-start | bytes 6152 | tf_op jit(solution)/shard_map/ppermute | solution.py:50
  26.2 3.0 %collective-permute-start.9 = (f32[4,128]{1,0:T(4,128)S(1)}, f32[4,128]{1,0:T(4,128)S(1)}, u32[]{:S(2)}, u32[]{:S(2)}) collective-permute-start(f32[4,128]{1,0:T(4,128)S(1)} %add_select_fusion.1), channel_id=1, source_target_pairs={{0,5},{1,4},{2,7},{3,6},{4,1},{5,0},{6,3},{7,2},{8,13},{9,12},{10,... | collective-permute-start | bytes 6152 | tf_op jit(solution)/shard_map/ppermute | solution.py:50
  26.2 3.0 %collective-permute-start.8 = (f32[4,128]{1,0:T(4,128)S(1)}, f32[4,128]{1,0:T(4,128)S(1)}, u32[]{:S(2)}, u32[]{:S(2)}) collective-permute-start(f32[4,128]{1,0:T(4,128)S(1)} %add_select_fusion.1), channel_id=1, source_target_pairs={{0,3},{1,2},{2,1},{3,0},{4,7},{5,6},{6,5},{7,4},{8,11},{9,10},{10,... | collective-permute-start | bytes 6152 | tf_op jit(solution)/shard_map/ppermute | solution.py:50

commit v6 on v5

--- a/solution.py
+++ b/solution.py
@@ -28,6 +28,10 @@
     for bit in bits:
         masks = masks + [mask | (1 << bit) for mask in masks]
     return [mask | 1 for mask in masks[1:]]
+
+
+def sends_ahead(phases, phase):
+    return phase == 0 and len(phases) > 1 and len(phases[0]) == 1
 
 
 def own_slot(phases, rank):
@@ -314,8 +318,17 @@
     )
     sources, source_scales = load(in_hbm(src_emb), in_hbm(src_scale.reshape(1, src_dev)))
     sources_live = jnp.where(lax.broadcasted_iota(jnp.int32, (1, src_dev), 1) < src_count, 1.0, 0.0)
-    for bits in phases:
-        came = [exchange(near, ranks, mask) for mask in phase_masks(bits)]
+    ahead = None
+    for phase, bits in enumerate(phases):
+        masks = phase_masks(bits)
+        if ahead is None:
+            came = [exchange(near, ranks, mask) for mask in masks]
+            if sends_ahead(phases, phase):
+                ahead = exchange(near, ranks, phase_masks(phases[1])[0])
+        else:
+            rest = exchange(came[0], ranks, masks[0])
+            came = [jnp.concatenate([ahead, rest], axis=0)] + [exchange(near, ranks, mask) for mask in masks[1:]]
+            ahead = None
         held, near = near, jnp.concatenate([near] + came, axis=0)
     early = exchange(jnp.concatenate([held, came[-1]], axis=0), ranks, 1)
     if len(came) > 1:

time: 30.4 us -> 30.4 us (level)
    ppermute x11 -> x12, waiting for transfers between devices: 8.42 us -> 8.64 us  [exchange(): return lax.ppermute(block, 'blk', [(i, i ^ mask) for i in range(ranks)])]
    ppermute x11 -> x12, starting transfers between devices: 13.9 us -> 13.7 us  [exchange(): return lax.ppermute(block, 'blk', [(i, i ^ mask) for i in range(ranks)])]
  transfers between devices with their start and end apart: 11 -> 12, of which waited for: 7 -> 5; matrix products, arithmetic and copies ran while one was open for 0% -> 0% of each run, Pallas kernels for 9% -> 9%
where the time goes in v6:
time: 30.4 us; the launch traced here: 30.2 us
  starting transfers between devices  13.7 us (45%)
  waiting for transfers between devices  8.64 us (28%)
  Pallas kernels  5.51 us (18%)
  between operations  2.03 us (7%)
    ppermute x12, starting transfers between devices, exchange(): return lax.ppermute(block, 'blk', [(i, i ^ mask) for i in range(ranks)])  13.7 us
    ppermute x12, waiting for transfers between devices, exchange(): return lax.ppermute(block, 'blk', [(i, i ^ mask) for i in range(ranks)])  8.64 us
    pallas_call x1, Pallas kernels, mine(): load(in_hbm(src_emb), in_hbm(src_scale.reshape(1, src_dev)))  1.61 us
    pallas_call x1, Pallas kernels, mine(): pl.pallas_call(functools.partial(far_kernel, phases, tgt_dev), out_shape=...  1.18 us
    pallas_call x1, Pallas kernels, mine(): pl.pallas_call(near_kernel, out_shape=(half_shape, source_line, source_li...  1.05 us
    pallas_call x1, Pallas kernels, mine(): pl.pallas_call(functools.partial(finish_kernel, phases, tgt_dev), out_sha...  0.88 us
    pallas_call x1, Pallas kernels, mine(): pl.pallas_call(pack_kernel, out_shape=(pltpu.VMEM((tgt_dev, width), jnp.b...  0.79 us
  transfers between devices with their start and end apart: 12, of which 5 were waited for; matrix products, arithmetic and copies ran while one was open for 0% of the time, Pallas kernels for 9%

profile of v6, /device:TPU:0, one launch (start us, length us, event | category | flops | bytes accessed | tf_op | source)
XLA Modules:
  0.0 30.2 jit_solution(755008997261434410)
XLA Ops:
  1.3 0.8 %pack.1 = (bf16[16,1152]{1,0:T(8,128)(2,1)S(1)}, f32[1,16]{1,0:T(1,128)S(1)}) custom-call(s32[1]{0:T(128)S(6)} %copy.15.count_ref, bf16[16,1024]{1,0:T(8,128)(2,1)} %tgt_hbm.1, f32[1,16]{1,0:T(1,128)} %bitcast.7), custom_call_target="tpu_custom_call" | custom-call | tf_op jit(solution)/shard_map/pack/pallas_call | solution.py:297
  2.1 3.6 %collective-permute-start = (bf16[16,1152]{1,0:T(8,128)(2,1)S(1)}, bf16[16,1152]{1,0:T(8,128)(2,1)S(1)}, u32[]{:S(2)}, u32[]{:S(2)}) collective-permute-start(bf16[16,1152]{1,0:T(8,128)(2,1)S(1)} %get-tuple-element.16), channel_id=1, source_target_pairs={{0,9},{1,8},{2,11},{3,10},{4,13},{5,12},{6,15},{7,14},{8,1},{9,0},... | collective-permute-start | bytes 110600 | tf_op jit(solution)/shard_map/ppermute | solution.py:54
  5.6 1.8 %collective-permute-start.3 = (bf16[16,1152]{1,0:T(8,128)(2,1)S(1)}, bf16[16,1152]{1,0:T(8,128)(2,1)S(1)}, u32[]{:S(2)}, u32[]{:S(2)}) collective-permute-start(bf16[16,1152]{1,0:T(8,128)(2,1)S(1)} %get-tuple-element.16), channel_id=1, source_target_pairs={{0,3},{1,2},{2,1},{3,0},{4,7},{5,6},{6,5},{7,4},{8,11},{9,10},{10,... | collective-permute-start | bytes 110600 | tf_op jit(solution)/shard_map/ppermute | solution.py:54
  8.1 1.6 %load.1 = (bf16[1024,1024]{1,0:T(8,128)(2,1)S(1)}, f32[1,1024]{1,0:T(1,128)S(1)}) custom-call(bf16[1024,1024]{1,0:T(8,128)(2,1)} %src_hbm.1, f32[1,1024]{1,0:T(1,128)} %bitcast.6), custom_call_target="tpu_custom_call" | custom-call | bytes 4194304 | tf_op jit(solution)/shard_map/load/pallas_call | solution.py:319
  9.8 1.1 %collective-permute-start.1 = (bf16[32,1152]{1,0:T(8,128)(2,1)S(1)}, bf16[32,1152]{1,0:T(8,128)(2,1)S(1)}, u32[]{:S(2)}, u32[]{:S(2)}) collective-permute-start(bf16[32,1152]{1,0:T(8,128)(2,1)S(1)} %get-tuple-element.31), channel_id=1, source_target_pairs={{0,7},{1,6},{2,5},{3,4},{4,3},{5,2},{6,1},{7,0},{8,15},{9,14},{10,... | collective-permute-start | bytes 221192 | tf_op jit(solution)/shard_map/ppermute | solution.py:54
  10.8 0.7 %collective-permute-start.5 = (bf16[32,1152]{1,0:T(8,128)(2,1)S(1)}, bf16[32,1152]{1,0:T(8,128)(2,1)S(1)}, u32[]{:S(2)}, u32[]{:S(2)}) collective-permute-start(bf16[32,1152]{1,0:T(8,128)(2,1)S(1)} %get-tuple-element.31), channel_id=1, source_target_pairs={{0,5},{1,4},{2,7},{3,6},{4,1},{5,0},{6,3},{7,2},{8,13},{9,12},{10,... | collective-permute-start | bytes 221192 | tf_op jit(solution)/shard_map/ppermute | solution.py:54
  11.5 1.1 %collective-permute-start.4 = (bf16[16,1152]{1,0:T(8,128)(2,1)S(1)}, bf16[16,1152]{1,0:T(8,128)(2,1)S(1)}, u32[]{:S(2)}, u32[]{:S(2)}) collective-permute-start(bf16[16,1152]{1,0:T(8,128)(2,1)S(1)} %collective-permute-done), channel_id=1, source_target_pairs={{0,3},{1,2},{2,1},{3,0},{4,7},{5,6},{6,5},{7,4},{8,11},{9,10},{10,... | collective-permute-start | bytes 110600 | tf_op jit(solution)/shard_map/ppermute | solution.py:54
  12.6 3.5 %collective-permute-done.4 = bf16[16,1152]{1,0:T(8,128)(2,1)S(1)} collective-permute-done((bf16[16,1152]{1,0:T(8,128)(2,1)S(1)}, bf16[16,1152]{1,0:T(8,128)(2,1)S(1)}, u32[]{:S(2)}, u32[]{:S(2)}) %collective-permute-start.4) | collective-permute-done | bytes 36896 | tf_op jit(solution)/shard_map/ppermute | solution.py:54
  16.1 0.2 collective-permute-start.2
  16.3 0.5 %collective-permute-start.6 = (bf16[64,1152]{1,0:T(8,128)(2,1)S(1)}, bf16[64,1152]{1,0:T(8,128)(2,1)S(1)}, u32[]{:S(2)}, u32[]{:S(2)}) collective-permute-start(bf16[64,1152]{1,0:T(8,128)(2,1)S(1)} %pad_maximum_fusion.2), channel_id=1, source_target_pairs={{0,1},{1,0},{2,3},{3,2},{4,5},{5,4},{6,7},{7,6},{8,9},{9,8},{10,11... | collective-permute-start | bytes 442376 | tf_op jit(solution)/shard_map/ppermute | solution.py:54
  16.8 1.0 %near.1 = (f32[128,1024]{1,0:T(8,128)S(1)}, f32[1,1024]{1,0:T(1,128)S(1)}, f32[1,1024]{1,0:T(1,128)S(1)}, f32[1,128]{1,0:T(1,128)S(1)}) custom-call(bf16[128,1152]{1,0:T(8,128)(2,1)S(1)} %constant_dynamic-update-slice_fusion.2.near_ref, bf16[1024,1024]{1,0:T(8,128)(2,1)S(1)} %get-tuple-element.17.src_ref, f32[1,1024]{1,0:T(1,128)S(1)} %get-tuple-element.18.src_scale_ref, ...), custom_call_target="tpu_custom_call" | custom-call | flops 268435456 | bytes 524288 | tf_op jit(solution)/shard_map/near/pallas_call | solution.py:340
  17.9 1.2 %far.1 = (f32[128,1024]{1,0:T(8,128)S(1)}, f32[1,1024]{1,0:T(1,128)S(1)}, f32[4,128]{1,0:T(4,128)S(1)}) custom-call(bf16[128,1152]{1,0:T(8,128)(2,1)S(1)} %pad_maximum_fusion.far_ref, bf16[1024,1024]{1,0:T(8,128)(2,1)S(1)} %get-tuple-element.17.src_ref, f32[1,1024]{1,0:T(1,128)S(1)} %get-tuple-element.18.src_scale_ref, ...), custom_call_target="tpu_custom_call" | custom-call | tf_op jit(solution)/shard_map/far/pallas_call | solution.py:352
  19.1 0.3 collective-permute-start.7
  19.4 0.9 %collective-permute-done.7 = f32[4,128]{1,0:T(4,128)S(1)} collective-permute-done((f32[4,128]{1,0:T(4,128)S(1)}, f32[4,128]{1,0:T(4,128)S(1)}, u32[]{:S(2)}, u32[]{:S(2)}) %collective-permute-start.7) | collective-permute-done | bytes 2080 | tf_op jit(solution)/shard_map/ppermute | solution.py:54
  20.3 0.1 add_select_fusion.2
  20.3 1.5 %collective-permute-start.8 = (f32[4,128]{1,0:T(4,128)S(1)}, f32[4,128]{1,0:T(4,128)S(1)}, u32[]{:S(2)}, u32[]{:S(2)}) collective-permute-start(f32[4,128]{1,0:T(4,128)S(1)} %add_select_fusion.2), channel_id=1, source_target_pairs={{0,9},{1,8},{2,11},{3,10},{4,13},{5,12},{6,15},{7,14},{8,1},{9,0},... | collective-permute-start | bytes 6152 | tf_op jit(solution)/shard_map/ppermute | solution.py:54
  21.9 2.4 %collective-permute-done.8 = f32[4,128]{1,0:T(4,128)S(1)} collective-permute-done((f32[4,128]{1,0:T(4,128)S(1)}, f32[4,128]{1,0:T(4,128)S(1)}, u32[]{:S(2)}, u32[]{:S(2)}) %collective-permute-start.8) | collective-permute-done | bytes 2080 | tf_op jit(solution)/shard_map/ppermute | solution.py:54
  24.3 0.1 add_select_fusion.1
  24.3 1.9 %collective-permute-start.11 = (f32[4,128]{1,0:T(4,128)S(1)}, f32[4,128]{1,0:T(4,128)S(1)}, u32[]{:S(2)}, u32[]{:S(2)}) collective-permute-start(f32[4,128]{1,0:T(4,128)S(1)} %add_select_fusion.1), channel_id=1, source_target_pairs={{0,7},{1,6},{2,5},{3,4},{4,3},{5,2},{6,1},{7,0},{8,15},{9,14},{10,... | collective-permute-start | bytes 6152 | tf_op jit(solution)/shard_map/ppermute | solution.py:54
  26.2 1.2 %collective-permute-start.9 = (f32[4,128]{1,0:T(4,128)S(1)}, f32[4,128]{1,0:T(4,128)S(1)}, u32[]{:S(2)}, u32[]{:S(2)}) collective-permute-start(f32[4,128]{1,0:T(4,128)S(1)} %add_select_fusion.1), channel_id=1, source_target_pairs={{0,3},{1,2},{2,1},{3,0},{4,7},{5,6},{6,5},{7,4},{8,11},{9,10},{10,... | collective-permute-start | bytes 6152 | tf_op jit(solution)/shard_map/ppermute | solution.py:54
  27.4 0.9 %collective-permute-done.11 = f32[4,128]{1,0:T(4,128)S(1)} collective-permute-done((f32[4,128]{1,0:T(4,128)S(1)}, f32[4,128]{1,0:T(4,128)S(1)}, u32[]{:S(2)}, u32[]{:S(2)}) %collective-permute-start.11) | collective-permute-done | bytes 2080 | tf_op jit(solution)/shard_map/ppermute | solution.py:54
  28.3 1.0 %collective-permute-done.10 = f32[4,128]{1,0:T(4,128)S(1)} collective-permute-done((f32[4,128]{1,0:T(4,128)S(1)}, f32[4,128]{1,0:T(4,128)S(1)}, u32[]{:S(2)}, u32[]{:S(2)}) %collective-permute-start.10) | collective-permute-done | bytes 2080 | tf_op jit(solution)/shard_map/ppermute | solution.py:54
  29.2 0.1 add_select_fusion.stats_ref
  29.3 0.9 %finish.1 = (f32[1,1024]{1,0:T(1,128)}, f32[1,16]{1,0:T(1,128)}) custom-call(f32[1,1024]{1,0:T(1,128)S(1)} %compare_select_fusion.src_live_ref, f32[1,16]{1,0:T(1,128)S(1)} %get-tuple-element.15.own_live_ref, f32[4,128]{1,0:T(4,128)S(1)} %add_select_fusion.stats_ref, f32[128,1024]{1,0:T(8,128)S(1)} %get-tuple-element.19.near_scores_ref.near_ref, ...), custom_call_target="tpu_custom_call" | custom-call | tf_op jit(solution)/shard_map/finish/pallas_call | solution.py:368
  (20 shorter events, 0.2 us)
Async XLA Ops:
  2.1 7.7 %collective-permute-start = (bf16[16,1152]{1,0:T(8,128)(2,1)S(1)}, bf16[16,1152]{1,0:T(8,128)(2,1)S(1)}, u32[]{:S(2)}, u32[]{:S(2)}) collective-permute-start(bf16[16,1152]{1,0:T(8,128)(2,1)S(1)} %get-tuple-element.16), channel_id=1, source_target_pairs={{0,9},{1,8},{2,11},{3,10},{4,13},{5,12},{6,15},{7,14},{8,1},{9,0},... | collective-permute-start | bytes 110600 | tf_op jit(solution)/shard_map/ppermute | solution.py:54
  5.6 7.0 %collective-permute-start.3 = (bf16[16,1152]{1,0:T(8,128)(2,1)S(1)}, bf16[16,1152]{1,0:T(8,128)(2,1)S(1)}, u32[]{:S(2)}, u32[]{:S(2)}) collective-permute-start(bf16[16,1152]{1,0:T(8,128)(2,1)S(1)} %get-tuple-element.16), channel_id=1, source_target_pairs={{0,3},{1,2},{2,1},{3,0},{4,7},{5,6},{6,5},{7,4},{8,11},{9,10},{10,... | collective-permute-start | bytes 110600 | tf_op jit(solution)/shard_map/ppermute | solution.py:54
  9.8 6.3 %collective-permute-start.1 = (bf16[32,1152]{1,0:T(8,128)(2,1)S(1)}, bf16[32,1152]{1,0:T(8,128)(2,1)S(1)}, u32[]{:S(2)}, u32[]{:S(2)}) collective-permute-start(bf16[32,1152]{1,0:T(8,128)(2,1)S(1)} %get-tuple-element.31), channel_id=1, source_target_pairs={{0,7},{1,6},{2,5},{3,4},{4,3},{5,2},{6,1},{7,0},{8,15},{9,14},{10,... | collective-permute-start | bytes 221192 | tf_op jit(solution)/shard_map/ppermute | solution.py:54
  10.8 5.4 %collective-permute-start.5 = (bf16[32,1152]{1,0:T(8,128)(2,1)S(1)}, bf16[32,1152]{1,0:T(8,128)(2,1)S(1)}, u32[]{:S(2)}, u32[]{:S(2)}) collective-permute-start(bf16[32,1152]{1,0:T(8,128)(2,1)S(1)} %get-tuple-element.31), channel_id=1, source_target_pairs={{0,5},{1,4},{2,7},{3,6},{4,1},{5,0},{6,3},{7,2},{8,13},{9,12},{10,... | collective-permute-start | bytes 221192 | tf_op jit(solution)/shard_map/ppermute | solution.py:54
  11.5 4.5 %collective-permute-start.4 = (bf16[16,1152]{1,0:T(8,128)(2,1)S(1)}, bf16[16,1152]{1,0:T(8,128)(2,1)S(1)}, u32[]{:S(2)}, u32[]{:S(2)}) collective-permute-start(bf16[16,1152]{1,0:T(8,128)(2,1)S(1)} %collective-permute-done), channel_id=1, source_target_pairs={{0,3},{1,2},{2,1},{3,0},{4,7},{5,6},{6,5},{7,4},{8,11},{9,10},{10,... | collective-permute-start | bytes 110600 | tf_op jit(solution)/shard_map/ppermute | solution.py:54
  16.1 1.7 %collective-permute-start.2 = (bf16[64,1152]{1,0:T(8,128)(2,1)S(1)}, bf16[64,1152]{1,0:T(8,128)(2,1)S(1)}, u32[]{:S(2)}, u32[]{:S(2)}) collective-permute-start(bf16[64,1152]{1,0:T(8,128)(2,1)S(1)} %pad_maximum_fusion.1), channel_id=1, source_target_pairs={{0,1},{1,0},{2,3},{3,2},{4,5},{5,4},{6,7},{7,6},{8,9},{9,8},{10,11... | collective-permute-start | bytes 442376 | tf_op jit(solution)/shard_map/ppermute | solution.py:54
  16.3 1.6 %collective-permute-start.6 = (bf16[64,1152]{1,0:T(8,128)(2,1)S(1)}, bf16[64,1152]{1,0:T(8,128)(2,1)S(1)}, u32[]{:S(2)}, u32[]{:S(2)}) collective-permute-start(bf16[64,1152]{1,0:T(8,128)(2,1)S(1)} %pad_maximum_fusion.2), channel_id=1, source_target_pairs={{0,1},{1,0},{2,3},{3,2},{4,5},{5,4},{6,7},{7,6},{8,9},{9,8},{10,11... | collective-permute-start | bytes 442376 | tf_op jit(solution)/shard_map/ppermute | solution.py:54
  19.1 1.2 %collective-permute-start.7 = (f32[4,128]{1,0:T(4,128)S(1)}, f32[4,128]{1,0:T(4,128)S(1)}, u32[]{:S(2)}, u32[]{:S(2)}) collective-permute-start(f32[4,128]{1,0:T(4,128)S(1)} %get-tuple-element.23), channel_id=1, source_target_pairs={{0,1},{1,0},{2,3},{3,2},{4,5},{5,4},{6,7},{7,6},{8,9},{9,8},{10,11... | collective-permute-start | bytes 6152 | tf_op jit(solution)/shard_map/ppermute | solution.py:54
  20.3 3.9 %collective-permute-start.8 = (f32[4,128]{1,0:T(4,128)S(1)}, f32[4,128]{1,0:T(4,128)S(1)}, u32[]{:S(2)}, u32[]{:S(2)}) collective-permute-start(f32[4,128]{1,0:T(4,128)S(1)} %add_select_fusion.2), channel_id=1, source_target_pairs={{0,9},{1,8},{2,11},{3,10},{4,13},{5,12},{6,15},{7,14},{8,1},{9,0},... | collective-permute-start | bytes 6152 | tf_op jit(solution)/shard_map/ppermute | solution.py:54
  24.3 3.9 %collective-permute-start.11 = (f32[4,128]{1,0:T(4,128)S(1)}, f32[4,128]{1,0:T(4,128)S(1)}, u32[]{:S(2)}, u32[]{:S(2)}) collective-permute-start(f32[4,128]{1,0:T(4,128)S(1)} %add_select_fusion.1), channel_id=1, source_target_pairs={{0,7},{1,6},{2,5},{3,4},{4,3},{5,2},{6,1},{7,0},{8,15},{9,14},{10,... | collective-permute-start | bytes 6152 | tf_op jit(solution)/shard_map/ppermute | solution.py:54
  26.2 3.0 %collective-permute-start.10 = (f32[4,128]{1,0:T(4,128)S(1)}, f32[4,128]{1,0:T(4,128)S(1)}, u32[]{:S(2)}, u32[]{:S(2)}) collective-permute-start(f32[4,128]{1,0:T(4,128)S(1)} %add_select_fusion.1), channel_id=1, source_target_pairs={{0,5},{1,4},{2,7},{3,6},{4,1},{5,0},{6,3},{7,2},{8,13},{9,12},{10,... | collective-permute-start | bytes 6152 | tf_op jit(solution)/shard_map/ppermute | solution.py:54
  26.2 3.0 %collective-permute-start.9 = (f32[4,128]{1,0:T(4,128)S(1)}, f32[4,128]{1,0:T(4,128)S(1)}, u32[]{:S(2)}, u32[]{:S(2)}) collective-permute-start(f32[4,128]{1,0:T(4,128)S(1)} %add_select_fusion.1), channel_id=1, source_target_pairs={{0,3},{1,2},{2,1},{3,0},{4,7},{5,6},{6,5},{7,4},{8,11},{9,10},{10,... | collective-permute-start | bytes 6152 | tf_op jit(solution)/shard_map/ppermute | solution.py:54

commit v7 on v5

--- a/solution.py
+++ b/solution.py
@@ -28,6 +28,13 @@
     for bit in bits:
         masks = masks + [mask | (1 << bit) for mask in masks]
     return [mask | 1 for mask in masks[1:]]
+
+
+def masks_ahead(phases):
+    if len(phases) < 2 or len(phases[0]) > 1:
+        return []
+    masks = phase_masks(phases[1])
+    return [masks[-1], masks[0]]
 
 
 def own_slot(phases, rank):
@@ -314,8 +321,20 @@
     )
     sources, source_scales = load(in_hbm(src_emb), in_hbm(src_scale.reshape(1, src_dev)))
     sources_live = jnp.where(lax.broadcasted_iota(jnp.int32, (1, src_dev), 1) < src_count, 1.0, 0.0)
-    for bits in phases:
-        came = [exchange(near, ranks, mask) for mask in phase_masks(bits)]
+    ahead = {}
+    for phase, bits in enumerate(phases):
+        masks = phase_masks(bits)
+        sent_ahead, ahead = ahead, {}
+        if sent_ahead:
+            blocks = came[0]
+        came = [
+            jnp.concatenate([sent_ahead[mask], exchange(blocks, ranks, mask)], axis=0)
+            if mask in sent_ahead
+            else exchange(near, ranks, mask)
+            for mask in masks
+        ]
+        if phase == 0:
+            ahead = {mask: exchange(near, ranks, mask) for mask in masks_ahead(phases)}
         held, near = near, jnp.concatenate([near] + came, axis=0)
     early = exchange(jnp.concatenate([held, came[-1]], axis=0), ranks, 1)
     if len(came) > 1:

time: 30.4 us -> 31.7 us (1.043)
  starting transfers between devices: 13.9 us -> 15.4 us
    ppermute x11 -> x13, starting transfers between devices: 13.9 us -> 15.4 us  [exchange(): return lax.ppermute(block, 'blk', [(i, i ^ mask) for i in range(ranks)])]
    ppermute x11 -> x13, waiting for transfers between devices: 8.42 us -> 8.18 us  [exchange(): return lax.ppermute(block, 'blk', [(i, i ^ mask) for i in range(ranks)])]
  transfers between devices with their start and end apart: 11 -> 13, of which waited for: 7 -> 7; matrix products, arithmetic and copies ran while one was open for 0% -> 0% of each run, Pallas kernels for 9% -> 8%
where the time goes in v7:
time: 31.7 us; the launch traced here: 31.4 us
  starting transfers between devices  15.4 us (49%)
  waiting for transfers between devices  8.18 us (26%)
  Pallas kernels  5.51 us (17%)
  between operations  2.04 us (6%)
    ppermute x13, starting transfers between devices, exchange(): return lax.ppermute(block, 'blk', [(i, i ^ mask) for i in range(ranks)])  15.4 us
    ppermute x13, waiting for transfers between devices, exchange(): return lax.ppermute(block, 'blk', [(i, i ^ mask) for i in range(ranks)])  8.18 us
    pallas_call x1, Pallas kernels, mine(): load(in_hbm(src_emb), in_hbm(src_scale.reshape(1, src_dev)))  1.61 us
    pallas_call x1, Pallas kernels, mine(): pl.pallas_call(functools.partial(far_kernel, phases, tgt_dev), out_shape=...  1.18 us
    pallas_call x1, Pallas kernels, mine(): pl.pallas_call(near_kernel, out_shape=(half_shape, source_line, source_li...  1.04 us
    pallas_call x1, Pallas kernels, mine(): pl.pallas_call(functools.partial(finish_kernel, phases, tgt_dev), out_sha...  0.88 us
    pallas_call x1, Pallas kernels, mine(): pl.pallas_call(pack_kernel, out_shape=(pltpu.VMEM((tgt_dev, width), jnp.b...  0.79 us
  transfers between devices with their start and end apart: 13, of which 7 were waited for; matrix products, arithmetic and copies ran while one was open for 0% of the time, Pallas kernels for 8%

profile of v7, /device:TPU:0, one launch (start us, length us, event | category | flops | bytes accessed | tf_op | source)
XLA Modules:
  0.0 31.4 jit_solution(8685380154905874278)
XLA Ops:
  1.3 0.8 %pack.1 = (bf16[16,1152]{1,0:T(8,128)(2,1)S(1)}, f32[1,16]{1,0:T(1,128)S(1)}) custom-call(s32[1]{0:T(128)S(6)} %copy.15.count_ref, bf16[16,1024]{1,0:T(8,128)(2,1)} %tgt_hbm.1, f32[1,16]{1,0:T(1,128)} %bitcast.7), custom_call_target="tpu_custom_call" | custom-call | tf_op jit(solution)/shard_map/pack/pallas_call | solution.py:300
  2.1 3.6 %collective-permute-start = (bf16[16,1152]{1,0:T(8,128)(2,1)S(1)}, bf16[16,1152]{1,0:T(8,128)(2,1)S(1)}, u32[]{:S(2)}, u32[]{:S(2)}) collective-permute-start(bf16[16,1152]{1,0:T(8,128)(2,1)S(1)} %get-tuple-element.16), channel_id=1, source_target_pairs={{0,9},{1,8},{2,11},{3,10},{4,13},{5,12},{6,15},{7,14},{8,1},{9,0},... | collective-permute-start | bytes 110600 | tf_op jit(solution)/shard_map/ppermute | solution.py:57
  5.6 2.8 %collective-permute-start.1 = (bf16[16,1152]{1,0:T(8,128)(2,1)S(1)}, bf16[16,1152]{1,0:T(8,128)(2,1)S(1)}, u32[]{:S(2)}, u32[]{:S(2)}) collective-permute-start(bf16[16,1152]{1,0:T(8,128)(2,1)S(1)} %get-tuple-element.16), channel_id=1, source_target_pairs={{0,7},{1,6},{2,5},{3,4},{4,3},{5,2},{6,1},{7,0},{8,15},{9,14},{10,... | collective-permute-start | bytes 110600 | tf_op jit(solution)/shard_map/ppermute | solution.py:57
  9.1 1.6 %load.1 = (bf16[1024,1024]{1,0:T(8,128)(2,1)S(1)}, f32[1,1024]{1,0:T(1,128)S(1)}) custom-call(bf16[1024,1024]{1,0:T(8,128)(2,1)} %src_hbm.1, f32[1,1024]{1,0:T(1,128)} %bitcast.6), custom_call_target="tpu_custom_call" | custom-call | bytes 4194304 | tf_op jit(solution)/shard_map/load/pallas_call | solution.py:322
  10.8 0.7 %collective-permute-start.6 = (bf16[32,1152]{1,0:T(8,128)(2,1)S(1)}, bf16[32,1152]{1,0:T(8,128)(2,1)S(1)}, u32[]{:S(2)}, u32[]{:S(2)}) collective-permute-start(bf16[32,1152]{1,0:T(8,128)(2,1)S(1)} %pad_maximum_fusion.3), channel_id=1, source_target_pairs={{0,5},{1,4},{2,7},{3,6},{4,1},{5,0},{6,3},{7,2},{8,13},{9,12},{10,... | collective-permute-start | bytes 221192 | tf_op jit(solution)/shard_map/ppermute | solution.py:57
  11.5 2.0 %collective-permute-start.2 = (bf16[16,1152]{1,0:T(8,128)(2,1)S(1)}, bf16[16,1152]{1,0:T(8,128)(2,1)S(1)}, u32[]{:S(2)}, u32[]{:S(2)}) collective-permute-start(bf16[16,1152]{1,0:T(8,128)(2,1)S(1)} %collective-permute-done), channel_id=1, source_target_pairs={{0,7},{1,6},{2,5},{3,4},{4,3},{5,2},{6,1},{7,0},{8,15},{9,14},{10,... | collective-permute-start | bytes 110600 | tf_op jit(solution)/shard_map/ppermute | solution.py:57
  13.5 0.8 %collective-permute-start.5 = (bf16[16,1152]{1,0:T(8,128)(2,1)S(1)}, bf16[16,1152]{1,0:T(8,128)(2,1)S(1)}, u32[]{:S(2)}, u32[]{:S(2)}) collective-permute-start(bf16[16,1152]{1,0:T(8,128)(2,1)S(1)} %collective-permute-done), channel_id=1, source_target_pairs={{0,3},{1,2},{2,1},{3,0},{4,7},{5,6},{6,5},{7,4},{8,11},{9,10},{10,... | collective-permute-start | bytes 110600 | tf_op jit(solution)/shard_map/ppermute | solution.py:57
  14.3 1.9 %collective-permute-done.2 = bf16[16,1152]{1,0:T(8,128)(2,1)S(1)} collective-permute-done((bf16[16,1152]{1,0:T(8,128)(2,1)S(1)}, bf16[16,1152]{1,0:T(8,128)(2,1)S(1)}, u32[]{:S(2)}, u32[]{:S(2)}) %collective-permute-start.2) | collective-permute-done | bytes 36896 | tf_op jit(solution)/shard_map/ppermute | solution.py:57
  16.3 0.8 %collective-permute-start.3 = (bf16[64,1152]{1,0:T(8,128)(2,1)S(1)}, bf16[64,1152]{1,0:T(8,128)(2,1)S(1)}, u32[]{:S(2)}, u32[]{:S(2)}) collective-permute-start(bf16[64,1152]{1,0:T(8,128)(2,1)S(1)} %pad_maximum_fusion.1), channel_id=1, source_target_pairs={{0,1},{1,0},{2,3},{3,2},{4,5},{5,4},{6,7},{7,6},{8,9},{9,8},{10,11... | collective-permute-start | bytes 442376 | tf_op jit(solution)/shard_map/ppermute | solution.py:57
  17.1 0.2 collective-permute-done.5
  17.3 0.3 %collective-permute-start.7 = (bf16[64,1152]{1,0:T(8,128)(2,1)S(1)}, bf16[64,1152]{1,0:T(8,128)(2,1)S(1)}, u32[]{:S(2)}, u32[]{:S(2)}) collective-permute-start(bf16[64,1152]{1,0:T(8,128)(2,1)S(1)} %pad_maximum_fusion.2), channel_id=1, source_target_pairs={{0,1},{1,0},{2,3},{3,2},{4,5},{5,4},{6,7},{7,6},{8,9},{9,8},{10,11... | collective-permute-start | bytes 442376 | tf_op jit(solution)/shard_map/ppermute | solution.py:57
  17.7 1.0 %near.1 = (f32[128,1024]{1,0:T(8,128)S(1)}, f32[1,1024]{1,0:T(1,128)S(1)}, f32[1,1024]{1,0:T(1,128)S(1)}, f32[1,128]{1,0:T(1,128)S(1)}) custom-call(bf16[128,1152]{1,0:T(8,128)(2,1)S(1)} %constant_dynamic-update-slice_fusion.near_ref, bf16[1024,1024]{1,0:T(8,128)(2,1)S(1)} %get-tuple-element.17.src_ref, f32[1,1024]{1,0:T(1,128)S(1)} %get-tuple-element.18.src_scale_ref, ...), custom_call_target="tpu_custom_call" | custom-call | flops 268435456 | bytes 524288 | tf_op jit(solution)/shard_map/near/pallas_call | solution.py:346
  18.8 1.2 %far.1 = (f32[128,1024]{1,0:T(8,128)S(1)}, f32[1,1024]{1,0:T(1,128)S(1)}, f32[4,128]{1,0:T(4,128)S(1)}) custom-call(bf16[128,1152]{1,0:T(8,128)(2,1)S(1)} %pad_maximum_fusion.far_ref, bf16[1024,1024]{1,0:T(8,128)(2,1)S(1)} %get-tuple-element.17.src_ref, f32[1,1024]{1,0:T(1,128)S(1)} %get-tuple-element.18.src_scale_ref, ...), custom_call_target="tpu_custom_call" | custom-call | tf_op jit(solution)/shard_map/far/pallas_call | solution.py:358
  20.0 0.2 collective-permute-start.8
  20.2 0.9 %collective-permute-done.8 = f32[4,128]{1,0:T(4,128)S(1)} collective-permute-done((f32[4,128]{1,0:T(4,128)S(1)}, f32[4,128]{1,0:T(4,128)S(1)}, u32[]{:S(2)}, u32[]{:S(2)}) %collective-permute-start.8) | collective-permute-done | bytes 2080 | tf_op jit(solution)/shard_map/ppermute | solution.py:57
  21.2 1.0 %collective-permute-start.9 = (f32[4,128]{1,0:T(4,128)S(1)}, f32[4,128]{1,0:T(4,128)S(1)}, u32[]{:S(2)}, u32[]{:S(2)}) collective-permute-start(f32[4,128]{1,0:T(4,128)S(1)} %add_select_fusion.2), channel_id=1, source_target_pairs={{0,9},{1,8},{2,11},{3,10},{4,13},{5,12},{6,15},{7,14},{8,1},{9,0},... | collective-permute-start | bytes 6152 | tf_op jit(solution)/shard_map/ppermute | solution.py:57
  22.2 3.0 %collective-permute-done.9 = f32[4,128]{1,0:T(4,128)S(1)} collective-permute-done((f32[4,128]{1,0:T(4,128)S(1)}, f32[4,128]{1,0:T(4,128)S(1)}, u32[]{:S(2)}, u32[]{:S(2)}) %collective-permute-start.9) | collective-permute-done | bytes 2080 | tf_op jit(solution)/shard_map/ppermute | solution.py:57
  25.2 1.7 %collective-permute-start.12 = (f32[4,128]{1,0:T(4,128)S(1)}, f32[4,128]{1,0:T(4,128)S(1)}, u32[]{:S(2)}, u32[]{:S(2)}) collective-permute-start(f32[4,128]{1,0:T(4,128)S(1)} %add_select_fusion.1), channel_id=1, source_target_pairs={{0,7},{1,6},{2,5},{3,4},{4,3},{5,2},{6,1},{7,0},{8,15},{9,14},{10,... | collective-permute-start | bytes 6152 | tf_op jit(solution)/shard_map/ppermute | solution.py:57
  26.9 0.5 %collective-permute-start.11 = (f32[4,128]{1,0:T(4,128)S(1)}, f32[4,128]{1,0:T(4,128)S(1)}, u32[]{:S(2)}, u32[]{:S(2)}) collective-permute-start(f32[4,128]{1,0:T(4,128)S(1)} %add_select_fusion.1), channel_id=1, source_target_pairs={{0,5},{1,4},{2,7},{3,6},{4,1},{5,0},{6,3},{7,2},{8,13},{9,12},{10,... | collective-permute-start | bytes 6152 | tf_op jit(solution)/shard_map/ppermute | solution.py:57
  27.5 0.8 %collective-permute-start.10 = (f32[4,128]{1,0:T(4,128)S(1)}, f32[4,128]{1,0:T(4,128)S(1)}, u32[]{:S(2)}, u32[]{:S(2)}) collective-permute-start(f32[4,128]{1,0:T(4,128)S(1)} %add_select_fusion.1), channel_id=1, source_target_pairs={{0,3},{1,2},{2,1},{3,0},{4,7},{5,6},{6,5},{7,4},{8,11},{9,10},{10,... | collective-permute-start | bytes 6152 | tf_op jit(solution)/shard_map/ppermute | solution.py:57
  28.3 0.9 %collective-permute-done.12 = f32[4,128]{1,0:T(4,128)S(1)} collective-permute-done((f32[4,128]{1,0:T(4,128)S(1)}, f32[4,128]{1,0:T(4,128)S(1)}, u32[]{:S(2)}, u32[]{:S(2)}) %collective-permute-start.12) | collective-permute-done | bytes 2080 | tf_op jit(solution)/shard_map/ppermute | solution.py:57
  29.1 0.8 %collective-permute-done.11 = f32[4,128]{1,0:T(4,128)S(1)} collective-permute-done((f32[4,128]{1,0:T(4,128)S(1)}, f32[4,128]{1,0:T(4,128)S(1)}, u32[]{:S(2)}, u32[]{:S(2)}) %collective-permute-start.11) | collective-permute-done | bytes 2080 | tf_op jit(solution)/shard_map/ppermute | solution.py:57
  30.0 0.5 %collective-permute-done.10 = f32[4,128]{1,0:T(4,128)S(1)} collective-permute-done((f32[4,128]{1,0:T(4,128)S(1)}, f32[4,128]{1,0:T(4,128)S(1)}, u32[]{:S(2)}, u32[]{:S(2)}) %collective-permute-start.10) | collective-permute-done | bytes 2080 | tf_op jit(solution)/shard_map/ppermute | solution.py:57
  30.6 0.9 %finish.1 = (f32[1,1024]{1,0:T(1,128)}, f32[1,16]{1,0:T(1,128)}) custom-call(f32[1,1024]{1,0:T(1,128)S(1)} %compare_select_fusion.src_live_ref, f32[1,16]{1,0:T(1,128)S(1)} %get-tuple-element.15.own_live_ref, f32[4,128]{1,0:T(4,128)S(1)} %add_select_fusion.stats_ref, f32[128,1024]{1,0:T(8,128)S(1)} %get-tuple-element.19.near_scores_ref.near_ref, ...), custom_call_target="tpu_custom_call" | custom-call | tf_op jit(solution)/shard_map/finish/pallas_call | solution.py:374
  (24 shorter events, 0.4 us)
Async XLA Ops:
  2.1 8.7 %collective-permute-start = (bf16[16,1152]{1,0:T(8,128)(2,1)S(1)}, bf16[16,1152]{1,0:T(8,128)(2,1)S(1)}, u32[]{:S(2)}, u32[]{:S(2)}) collective-permute-start(bf16[16,1152]{1,0:T(8,128)(2,1)S(1)} %get-tuple-element.16), channel_id=1, source_target_pairs={{0,9},{1,8},{2,11},{3,10},{4,13},{5,12},{6,15},{7,14},{8,1},{9,0},... | collective-permute-start | bytes 110600 | tf_op jit(solution)/shard_map/ppermute | solution.py:57
  5.6 8.7 %collective-permute-start.1 = (bf16[16,1152]{1,0:T(8,128)(2,1)S(1)}, bf16[16,1152]{1,0:T(8,128)(2,1)S(1)}, u32[]{:S(2)}, u32[]{:S(2)}) collective-permute-start(bf16[16,1152]{1,0:T(8,128)(2,1)S(1)} %get-tuple-element.16), channel_id=1, source_target_pairs={{0,7},{1,6},{2,5},{3,4},{4,3},{5,2},{6,1},{7,0},{8,15},{9,14},{10,... | collective-permute-start | bytes 110600 | tf_op jit(solution)/shard_map/ppermute | solution.py:57
  8.5 5.8 %collective-permute-start.4 = (bf16[16,1152]{1,0:T(8,128)(2,1)S(1)}, bf16[16,1152]{1,0:T(8,128)(2,1)S(1)}, u32[]{:S(2)}, u32[]{:S(2)}) collective-permute-start(bf16[16,1152]{1,0:T(8,128)(2,1)S(1)} %get-tuple-element.16), channel_id=1, source_target_pairs={{0,3},{1,2},{2,1},{3,0},{4,7},{5,6},{6,5},{7,4},{8,11},{9,10},{10,... | collective-permute-start | bytes 110600 | tf_op jit(solution)/shard_map/ppermute | solution.py:57
  10.8 6.5 %collective-permute-start.6 = (bf16[32,1152]{1,0:T(8,128)(2,1)S(1)}, bf16[32,1152]{1,0:T(8,128)(2,1)S(1)}, u32[]{:S(2)}, u32[]{:S(2)}) collective-permute-start(bf16[32,1152]{1,0:T(8,128)(2,1)S(1)} %pad_maximum_fusion.3), channel_id=1, source_target_pairs={{0,5},{1,4},{2,7},{3,6},{4,1},{5,0},{6,3},{7,2},{8,13},{9,12},{10,... | collective-permute-start | bytes 221192 | tf_op jit(solution)/shard_map/ppermute | solution.py:57
  11.5 4.7 %collective-permute-start.2 = (bf16[16,1152]{1,0:T(8,128)(2,1)S(1)}, bf16[16,1152]{1,0:T(8,128)(2,1)S(1)}, u32[]{:S(2)}, u32[]{:S(2)}) collective-permute-start(bf16[16,1152]{1,0:T(8,128)(2,1)S(1)} %collective-permute-done), channel_id=1, source_target_pairs={{0,7},{1,6},{2,5},{3,4},{4,3},{5,2},{6,1},{7,0},{8,15},{9,14},{10,... | collective-permute-start | bytes 110600 | tf_op jit(solution)/shard_map/ppermute | solution.py:57
  13.5 3.8 %collective-permute-start.5 = (bf16[16,1152]{1,0:T(8,128)(2,1)S(1)}, bf16[16,1152]{1,0:T(8,128)(2,1)S(1)}, u32[]{:S(2)}, u32[]{:S(2)}) collective-permute-start(bf16[16,1152]{1,0:T(8,128)(2,1)S(1)} %collective-permute-done), channel_id=1, source_target_pairs={{0,3},{1,2},{2,1},{3,0},{4,7},{5,6},{6,5},{7,4},{8,11},{9,10},{10,... | collective-permute-start | bytes 110600 | tf_op jit(solution)/shard_map/ppermute | solution.py:57
  16.3 2.5 %collective-permute-start.3 = (bf16[64,1152]{1,0:T(8,128)(2,1)S(1)}, bf16[64,1152]{1,0:T(8,128)(2,1)S(1)}, u32[]{:S(2)}, u32[]{:S(2)}) collective-permute-start(bf16[64,1152]{1,0:T(8,128)(2,1)S(1)} %pad_maximum_fusion.1), channel_id=1, source_target_pairs={{0,1},{1,0},{2,3},{3,2},{4,5},{5,4},{6,7},{7,6},{8,9},{9,8},{10,11... | collective-permute-start | bytes 442376 | tf_op jit(solution)/shard_map/ppermute | solution.py:57
  17.3 1.5 %collective-permute-start.7 = (bf16[64,1152]{1,0:T(8,128)(2,1)S(1)}, bf16[64,1152]{1,0:T(8,128)(2,1)S(1)}, u32[]{:S(2)}, u32[]{:S(2)}) collective-permute-start(bf16[64,1152]{1,0:T(8,128)(2,1)S(1)} %pad_maximum_fusion.2), channel_id=1, source_target_pairs={{0,1},{1,0},{2,3},{3,2},{4,5},{5,4},{6,7},{7,6},{8,9},{9,8},{10,11... | collective-permute-start | bytes 442376 | tf_op jit(solution)/shard_map/ppermute | solution.py:57
  20.0 1.2 %collective-permute-start.8 = (f32[4,128]{1,0:T(4,128)S(1)}, f32[4,128]{1,0:T(4,128)S(1)}, u32[]{:S(2)}, u32[]{:S(2)}) collective-permute-start(f32[4,128]{1,0:T(4,128)S(1)} %get-tuple-element.23), channel_id=1, source_target_pairs={{0,1},{1,0},{2,3},{3,2},{4,5},{5,4},{6,7},{7,6},{8,9},{9,8},{10,11... | collective-permute-start | bytes 6152 | tf_op jit(solution)/shard_map/ppermute | solution.py:57
  21.2 3.9 %collective-permute-start.9 = (f32[4,128]{1,0:T(4,128)S(1)}, f32[4,128]{1,0:T(4,128)S(1)}, u32[]{:S(2)}, u32[]{:S(2)}) collective-permute-start(f32[4,128]{1,0:T(4,128)S(1)} %add_select_fusion.2), channel_id=1, source_target_pairs={{0,9},{1,8},{2,11},{3,10},{4,13},{5,12},{6,15},{7,14},{8,1},{9,0},... | collective-permute-start | bytes 6152 | tf_op jit(solution)/shard_map/ppermute | solution.py:57
  25.2 3.9 %collective-permute-start.12 = (f32[4,128]{1,0:T(4,128)S(1)}, f32[4,128]{1,0:T(4,128)S(1)}, u32[]{:S(2)}, u32[]{:S(2)}) collective-permute-start(f32[4,128]{1,0:T(4,128)S(1)} %add_select_fusion.1), channel_id=1, source_target_pairs={{0,7},{1,6},{2,5},{3,4},{4,3},{5,2},{6,1},{7,0},{8,15},{9,14},{10,... | collective-permute-start | bytes 6152 | tf_op jit(solution)/shard_map/ppermute | solution.py:57
  26.9 3.0 %collective-permute-start.11 = (f32[4,128]{1,0:T(4,128)S(1)}, f32[4,128]{1,0:T(4,128)S(1)}, u32[]{:S(2)}, u32[]{:S(2)}) collective-permute-start(f32[4,128]{1,0:T(4,128)S(1)} %add_select_fusion.1), channel_id=1, source_target_pairs={{0,5},{1,4},{2,7},{3,6},{4,1},{5,0},{6,3},{7,2},{8,13},{9,12},{10,... | collective-permute-start | bytes 6152 | tf_op jit(solution)/shard_map/ppermute | solution.py:57
  27.5 3.0 %collective-permute-start.10 = (f32[4,128]{1,0:T(4,128)S(1)}, f32[4,128]{1,0:T(4,128)S(1)}, u32[]{:S(2)}, u32[]{:S(2)}) collective-permute-start(f32[4,128]{1,0:T(4,128)S(1)} %add_select_fusion.1), channel_id=1, source_target_pairs={{0,3},{1,2},{2,1},{3,0},{4,7},{5,6},{6,5},{7,4},{8,11},{9,10},{10,... | collective-permute-start | bytes 6152 | tf_op jit(solution)/shard_map/ppermute | solution.py:57
